TPU v7x, 32 devices: a whole 2x2x4 slice. The times are simulated.
32 devices in a mesh: groups: 2 (over y), blk: 4 (over z), layer: 2 (over x), rep: 2 (over core).
Axes of the slice: x: 2, y: 2, z: 4, core: 2. Of those that a mesh axis runs over, the one named last changes fastest.
Arguments:
- train_grads: bfloat16 [2, 8192, 4096], P('layer', ('groups', 'blk')), parts along dimension 1, may hold values from -0.29882812 to 0.29882812
- queries: bfloat16 [2, 2, 512, 4096], P('layer', 'rep', ('groups', 'blk')), parts along dimension 2, may hold values from -0.59765625 to 0.59765625
- bases: bfloat16 [2, 64, 128], P('layer', ('blk', 'rep')), may hold values from -0.75 to 0.75
- eigenvalues: float32 [2, 4096], P('layer', ('blk', 'rep')), may hold values from 0.01 to 10
Outputs:
- scores: float32 [2, 256, 8192], P('rep', 'layer', ('groups', 'blk')), parts along dimension 2
There are 2 independent parts, one for each index of `groups`. A program takes and returns all parts, laid end to end along the dimension named above; an argument that names none is the same for every part. Nothing has to cross between parts.
All inputs are finite; a program needn't handle non-finite values.
Results may differ from a plain program's by a relative error of at most 0.0042.
Values may be sent and summed in bfloat16 or wider, within the bound.
No kernel may reach another device: no remote copies, remote signals or barrier semaphores. Data moves between devices by JAX's collectives and lax.ppermute only.
A program may use at most 128 MiB of HBM per device.

v0:
```python
import functools

import jax
import jax.numpy as jnp
from jax import lax
from jax.experimental import pallas as pl
from jax.experimental.pallas import tpu as pltpu
from jax.sharding import PartitionSpec as P

TILE = 16
HALF = 8
BF16, F32 = jnp.bfloat16, jnp.float32
IN_VMEM = pl.BlockSpec(memory_space=pltpu.VMEM)
IN_SMEM = pl.BlockSpec(memory_space=pltpu.SMEM)


def dot(a, b):
    return jnp.dot(a, b, preferred_element_type=F32)


def call(kernel, out_shape, in_specs, scratch, args, flops, grant):
    outs = out_shape if isinstance(out_shape, (list, tuple)) else [out_shape]
    moved = sum(a.size * a.dtype.itemsize for a in list(args) + list(outs))
    return pl.pallas_call(
        kernel,
        out_shape=out_shape,
        in_specs=in_specs,
        out_specs=jax.tree.map(lambda _: IN_VMEM, out_shape),
        scratch_shapes=scratch,
        compiler_params=pltpu.CompilerParams(vmem_limit_bytes=grant),
        cost_estimate=pl.CostEstimate(flops=flops, bytes_accessed=moved, transcendentals=0),
    )(*args)


def line_plan(count):
    plan, arrivals = {}, [[] for _ in range(count)]
    for step in range(1, count):
        for parity in range(2):
            pairs = []
            for low in range(parity, count - 1, 2):
                high = low + 1
                if low - (step - 1) >= 0:
                    pairs.append((low, high))
                    arrivals[high].append((step, parity, low - (step - 1)))
                if high + (step - 1) < count:
                    pairs.append((high, low))
                    arrivals[low].append((step, parity, high + (step - 1)))
            if pairs:
                plan[step, parity] = pairs
    return plan, arrivals


def lookup(values, index):
    value = jnp.int32(values[0])
    for i, v in enumerate(values[1:], 1):
        if v != values[0]:
            value = jnp.where(index == i, jnp.int32(v), value)
    return value


def spread(matrix, rows, cols, keep):
    size = matrix.shape[0]
    r = lax.broadcasted_iota(jnp.int32, (rows, size), 0)
    i = lax.broadcasted_iota(jnp.int32, (rows, size), 1)
    j = lax.broadcasted_iota(jnp.int32, (size, cols), 0)
    c = lax.broadcasted_iota(jnp.int32, (size, cols), 1)
    down = jnp.where(lax.rem(r, size) == i, 1.0, 0.0).astype(BF16)
    along = jnp.where(lax.rem(c, size) == j, 1.0, 0.0).astype(BF16)
    full = dot(dot(down, matrix.astype(BF16)).astype(BF16), along)
    block_row = lax.broadcasted_iota(jnp.int32, (rows, cols), 0) // size
    block_col = lax.broadcasted_iota(jnp.int32, (rows, cols), 1) // size
    return jnp.where(keep(block_row, block_col), full, 0.0).astype(BF16)


def comb(matrix, out_ref):
    size = matrix.shape[0]
    wide = size * HALF
    j = lax.broadcasted_iota(jnp.int32, (size, wide), 0)
    c = lax.broadcasted_iota(jnp.int32, (size, wide), 1)
    rows = dot(matrix.astype(BF16), jnp.where(c // HALF == j, 1.0, 0.0).astype(BF16))
    r = lax.broadcasted_iota(jnp.int32, (HALF, wide), 0)
    c = lax.broadcasted_iota(jnp.int32, (HALF, wide), 1)
    keep = r == lax.rem(c, HALF)
    for i in range(0, size, 2):
        pair = [
            jnp.where(keep, jnp.broadcast_to(rows[k : k + 1], (HALF, wide)), 0.0) for k in (i, i + 1)
        ]
        out_ref[i * HALF : (i + 2) * HALF, :] = jnp.concatenate(pair, axis=0).astype(BF16)


def prep_kernel(shape, here_ref, *refs):
    count, reps, base_rows, eigen_rows, fold = shape
    parts = refs[:count]
    w1_ref, but_ref, bu_ref, w5_ref, inv_ref, base3, eigen3, base, eigen, pad = refs[count:]
    z, rep = here_ref[0], here_ref[2]
    each = base_rows + eigen_rows
    for d in range(count):
        for e in range(reps):
            source = lax.rem(z + count - d, count) * reps + lax.rem(rep + reps - e, reps)
            base3[source] = parts[d][e * each : e * each + base_rows, :]
            eigen3[source] = parts[d][e * each + base_rows : (e + 1) * each, :]
    for s in range(count * reps):
        base[s * base_rows : (s + 1) * base_rows, :] = base3[s]
        eigen[s * eigen_rows : (s + 1) * eigen_rows, :] = eigen3[s]
    size = base.shape[0]
    basis = base[...]
    left, right = basis[:, :size], basis[:, size:]
    turned = basis.T
    left_t, right_t = turned[:size], turned[size:]
    wide = 2 * size * fold
    w1_ref[...] = spread(
        right, wide, wide, lambda r, c: (r // 2 == lax.rem(c, fold)) & (lax.rem(r, 2) == c // fold)
    )
    w5_ref[...] = spread(
        right_t, wide, wide, lambda r, c: (c // 2 == lax.rem(r, fold)) & (lax.rem(c, 2) == r // fold)
    )
    comb(left_t, but_ref)
    comb(left, bu_ref)
    values = eigen[...]
    inverse = 1.0 / (values + 0.1 * (jnp.sum(values) / (size * size)))
    shifted = pltpu.roll(inverse, size, 1)
    lane = lax.broadcasted_iota(jnp.int32, inverse.shape, 1)
    pad[pl.ds(0, size // 2, stride=2), :] = jnp.where(lane < size, inverse, shifted)
    pad[pl.ds(1, size // 2, stride=2), :] = jnp.where(lane < size, shifted, inverse)
    for i in range(size):
        row = jnp.broadcast_to(pad[i : i + 1, :], (HALF, 2 * size))
        for h in range(fold // 2):
            inv_ref[i * HALF : (i + 1) * HALF, h * 2 * size : (h + 1) * 2 * size] = row


def rotation_constants(parts, here, reps, base_rows, eigen_rows, size, fold):
    count = len(parts)
    wide, tall = 2 * size * fold, HALF * size
    shard = count * reps
    return call(
        functools.partial(prep_kernel, (count, reps, base_rows, eigen_rows, fold)),
        [
            jax.ShapeDtypeStruct((wide, wide), BF16),
            jax.ShapeDtypeStruct((tall, tall), BF16),
            jax.ShapeDtypeStruct((tall, tall), BF16),
            jax.ShapeDtypeStruct((wide, wide), BF16),
            jax.ShapeDtypeStruct((tall, size * fold), F32),
        ],
        [IN_SMEM] + [IN_VMEM] * count,
        [
            pltpu.VMEM((shard, base_rows, 2 * size), F32),
            pltpu.VMEM((shard, eigen_rows, 2 * size), F32),
            pltpu.VMEM((size, 2 * size), F32),
            pltpu.VMEM((size // 2, 2 * size), F32),
            pltpu.VMEM((size, 2 * size), F32),
        ],
        (here, *parts),
        flops=2 * wide * wide * 2 * size,
        grant=12 << 20,
    )


def rotate_kernel(sources, choice, splits, here_ref, *refs):
    inputs, refs = refs[:sources], refs[sources:]
    w1_ref, but_ref, bu_ref, w5_ref, inv_ref = refs[:5]
    outs = refs[5 : 6 + splits]
    tall, first, second = refs[6 + splits :]
    fold = inputs[0].shape[0] // TILE
    lanes = w1_ref.shape[0] // fold
    size = lanes // 2
    pairs = size // 2
    half = size * fold

    def gather_rows(q_ref):
        for a in range(pairs):
            for h in range(fold):
                tall[a * TILE : (a + 1) * TILE, h * lanes : (h + 1) * lanes] = q_ref[
                    h * TILE : (h + 1) * TILE, a * lanes : (a + 1) * lanes
                ]

    if sources == 1:
        gather_rows(inputs[0])
    else:
        which = lookup(choice, here_ref[0])
        for i in range(sources):
            pl.when(which == i)(functools.partial(gather_rows, inputs[i]))
    chunk = 8
    parts = TILE // HALF
    for a0 in range(0, pairs, chunk):
        rows = dot(tall[a0 * TILE : (a0 + chunk) * TILE, :], w1_ref[...])
        for a in range(a0, a0 + chunk):
            for part in range(parts):
                low = (a - a0) * TILE + part * HALF
                for odd in range(2):
                    at = (2 * a + odd) * HALF
                    first[part, at : at + HALF, :] = rows[low : low + HALF, odd * half : (odd + 1) * half]
    but, bu, inverse = but_ref[...], bu_ref[...], inv_ref[...]
    for part in range(parts):
        scaled = (dot(but, first[part].astype(BF16)) * inverse).astype(BF16)
        second[part] = dot(bu, scaled)
    for a in range(pairs):
        for odd in range(2):
            at = (2 * a + odd) * HALF
            value = jnp.concatenate([second[part, at : at + HALF, :] for part in range(parts)], axis=0)
            tall[a * TILE : (a + 1) * TILE, odd * half : (odd + 1) * half] = value.astype(BF16)
    for a0 in range(0, pairs, chunk):
        rows = dot(tall[a0 * TILE : (a0 + chunk) * TILE, :], w5_ref[...]).astype(BF16)
        for a in range(a0, a0 + chunk):
            for h in range(fold):
                value = rows[(a - a0) * TILE : (a - a0 + 1) * TILE, h * lanes : (h + 1) * lanes]
                outs[0][h * TILE : (h + 1) * TILE, a * lanes : (a + 1) * lanes] = value
                if splits:
                    per = fold // splits
                    low = (h % per) * TILE
                    outs[1 + h // per][low : low + TILE, a * lanes : (a + 1) * lanes] = value


def rotate(here, choice, inputs, constants, splits=0):
    rows, width = inputs[0].shape
    fold = rows // TILE
    wide = constants[0].shape[0]
    size = wide // (2 * fold)
    shapes = [jax.ShapeDtypeStruct((rows, width), BF16)]
    shapes += [jax.ShapeDtypeStruct((rows // splits, width), BF16)] * splits if splits else []
    return call(
        functools.partial(rotate_kernel, len(inputs), choice, splits),
        shapes,
        [IN_SMEM] + [IN_VMEM] * (len(inputs) + 5),
        [
            pltpu.VMEM((size // 2 * TILE, wide), BF16),
            pltpu.VMEM((TILE // HALF, size * HALF, size * fold), F32),
            pltpu.VMEM((TILE // HALF, size * HALF, size * fold), F32),
        ],
        (here, *inputs, *constants),
        flops=8 * rows * width * size * fold,
        grant=12 << 20,
    )


def fill(held, units, choices, here_ref):
    at = 0
    for candidates, choice in zip(units, choices):
        rows = candidates[0].shape[0]

        def take(ref, at=at, rows=rows):
            held[at : at + rows, :] = ref[...]

        if len(candidates) == 1:
            take(candidates[0])
        else:
            which = lookup(choice, here_ref[0])
            for i, ref in enumerate(candidates):
                pl.when(which == i)(functools.partial(take, ref))
        at += rows


def products(held, x_ref, kept_ref):
    total = x_ref.shape[0]
    step = min(256, total)
    for t in range(0, total, step):
        kept_ref[:, t : t + step] = lax.dot_general(
            x_ref[t : t + step, :], held[...], (((1,), (1,)), ((), ())), preferred_element_type=F32
        ).T


def grid_lookup(table, z, owner):
    value = lookup([row[0] for row in table], z)
    for o in range(1, len(table[0])):
        value = jnp.where(owner == o, lookup([row[o] for row in table], z), value)
    return value


def aligned(start, rows):
    return pl.ds(pl.multiple_of(start, rows), rows)


def early_kernel(shape, choices, table, piece, here_ref, *refs):
    refs = list(refs)
    units = [[refs.pop(0) for _ in range(n)] for n in shape]
    x_ref, kept_ref, *sent = refs[:-1]
    held = refs[-1]
    fill(held, units, choices, here_ref)
    products(held, x_ref, kept_ref)
    z, x = here_ref[0], here_ref[1]
    layers = len(sent) + 1
    for d, sent_ref in enumerate(sent, 1):
        target = lax.rem(x + d, layers)
        for p in range(len(table) - 1):
            start = grid_lookup(table[p], z, target)
            sent_ref[p * piece : (p + 1) * piece, :] = kept_ref[aligned(start, piece), :].astype(BF16)


def late_kernel(shape, choices, table, piece, here_ref, *refs):
    refs = list(refs)
    units = [[refs.pop(0) for _ in range(n)] for n in shape]
    x_ref, early_ref, kept_ref, *sent = refs[:-1]
    held = refs[-1]
    fill(held, units, choices, here_ref)
    products(held, x_ref, kept_ref)
    z, x = here_ref[0], here_ref[1]
    layers = len(sent) + 1
    for d, sent_ref in enumerate(sent, 1):
        start = grid_lookup(table[-1], z, lax.rem(x + d, layers))
        last = early_ref.shape[0]

        @pl.when(start == last)
        def _(sent_ref=sent_ref):
            sent_ref[...] = kept_ref[...].astype(BF16)

        @pl.when(start != last)
        def _(sent_ref=sent_ref, start=start):
            sent_ref[...] = early_ref[aligned(start, piece), :].astype(BF16)


def finish_kernel(table, places, piece, layers, here_ref, early_ref, late_ref, *refs):
    *received, out_ref = refs
    z, x = here_ref[0], here_ref[1]
    shifts = layers - 1
    first, second = received[:shifts], received[shifts:]
    last = early_ref.shape[0]
    count = len(table)
    for p in range(count):
        start = grid_lookup(table[p], z, x)
        place = aligned(grid_lookup(places[p], z, x), piece)
        if p < count - 1:
            value = early_ref[aligned(start, piece), :]
            for ref in first:
                value = value + ref[p * piece : (p + 1) * piece, :].astype(F32)
            out_ref[place, :] = value
            continue
        other = second[0][...].astype(F32)
        for ref in second[1:]:
            other = other + ref[...].astype(F32)

        @pl.when(start == last)
        def _():
            out_ref[place, :] = late_ref[...] + other

        @pl.when(start != last)
        def _():
            out_ref[place, :] = early_ref[aligned(start, piece), :] + other


def load_kernel(x_ref, out_ref, sem):
    pieces = sem.shape[0]
    step = x_ref.shape[0] // pieces
    copies = []
    for i in range(pieces):
        rows = pl.ds(i * step, step)
        copies.append(pltpu.make_async_copy(x_ref.at[rows], out_ref.at[rows], sem.at[i]))
    for copy in copies:
        copy.start()
    for copy in copies:
        copy.wait()


def resident(x):
    return pl.pallas_call(
        load_kernel,
        out_shape=pltpu.VMEM(x.shape, x.dtype),
        in_specs=[pl.BlockSpec(memory_space=pltpu.HBM)],
        out_specs=IN_VMEM,
        scratch_shapes=[pltpu.SemaphoreType.DMA((8,))],
        compiler_params=pltpu.CompilerParams(vmem_limit_bytes=12 << 20),
        cost_estimate=pl.CostEstimate(
            flops=0, bytes_accessed=2 * x.size * x.dtype.itemsize, transcendentals=0
        ),
    )(x)


def steps(train_grads, queries, bases, eigenvalues):
    blocks, layers, reps = lax.axis_size("blk"), lax.axis_size("layer"), lax.axis_size("rep")
    z, x, rep = lax.axis_index("blk"), lax.axis_index("layer"), lax.axis_index("rep")
    train = train_grads[0]
    own = queries[0, 0]
    base_rows, lanes = bases.shape[1:]
    size = lanes // 2
    rows = own.shape[0]
    fold = rows // TILE
    per_owner = blocks // layers

    plan, arrivals = line_plan(blocks)
    here = jnp.stack([z, x, rep]).astype(jnp.int32)
    splits = 2

    raw, turned = {}, {}
    raw[1, 1] = lax.ppermute(own, "blk", plan[1, 1])
    raw[1, 0] = lax.ppermute(own, "blk", plan[1, 0])

    eigen = eigenvalues.reshape(-1, lanes)
    eigen_rows = eigen.shape[0]
    packed = jnp.concatenate([bases[0].astype(F32), eigen], axis=0)
    pair = [packed]
    for e in range(1, reps):
        pair.append(lax.ppermute(packed, "rep", [(r, (r + e) % reps) for r in range(reps)]))
    pair = jnp.concatenate(pair, axis=0)
    parts = [pair]
    for d in range(1, blocks):
        parts.append(lax.ppermute(pair, "blk", [(a, (a + d) % blocks) for a in range(blocks)]))
    train, _ = lax.optimization_barrier((train, pair))
    train = resident(train)
    raw[1, 1], train = lax.optimization_barrier((raw[1, 1], train))
    raw[2, 0] = lax.ppermute(raw[1, 1], "blk", plan[2, 0])

    constants = rotation_constants(parts, here, reps, base_rows, eigen_rows, size, fold)
    alone = [0] * blocks
    whole_first, *turned[1, 0] = rotate(here, alone, [raw[1, 0]], constants, splits)
    whole_own, = rotate(here, alone, [own], constants)

    block_of = [list(range(blocks))] + [[a[j][2] for a in arrivals] for j in range(blocks - 1)]
    source_of = [None] + [[a[j][:2] for a in arrivals] for j in range(blocks - 1)]
    units, choices = [[whole_own], [whole_first]], [alone, alone]
    gate = whole_own
    for step, parity in plan:
        if step == 1 or (step, parity) in raw:
            continue
        before = (step - 1, 1 - parity)
        if before not in turned:
            turned[before] = rotate(here, alone, [raw[before]], constants, splits)[1:]
        pieces = turned[before]
        if step > 2:
            pieces = [lax.optimization_barrier((w, gate))[0] for w in pieces]
        turned[step, parity] = [lax.ppermute(w, "blk", plan[step, parity]) for w in pieces]

    for j in range(2, blocks):
        names = sorted(set(source_of[j]))
        fresh = [n for n in names if n in raw and n not in turned]
        ready = [n for n in names if n not in fresh]
        if fresh:
            choice = [fresh.index(s) if s in fresh else 0 for s in source_of[j]]
            wide = rotate(here, choice, [raw[n] for n in fresh], constants, splits if ready else 0)
        if not ready:
            units.append([wide[0]])
            choices.append(alone)
            continue
        for part in range(splits):
            candidates = [wide[1 + part]] if fresh else []
            offset = len(candidates)
            candidates += [turned[n][part] for n in ready]
            units.append(candidates)
            choices.append([0 if s in fresh else offset + ready.index(s) for s in source_of[j]])

    piece = rows // splits
    count = per_owner * splits
    table = [[[0] * layers for _ in range(blocks)] for _ in range(count)]
    places = [[[0] * layers for _ in range(blocks)] for _ in range(count)]
    for a in range(blocks):
        for o in range(layers):
            mine = [j for j in range(blocks) if block_of[j][a] // per_owner == o]
            for p in range(count):
                j, part = mine[p // splits], p % splits
                table[p][a][o] = j * rows + part * piece
                places[p][a][o] = block_of[j][a] % per_owner * rows + part * piece

    def shifted(sent):
        return [
            lax.ppermute(s, "layer", [(o, (o + d) % layers) for o in range(layers)])
            for d, s in enumerate(sent, 1)
        ]

    def scores(kernel, units, choices, inputs, sent_rows, grant):
        held = sum(u[0].shape[0] for u in units)
        total, width = train.shape
        flat = [w for u in units for w in u] + [train] + inputs
        sent_shape = jax.ShapeDtypeStruct((sent_rows, total), BF16)
        return call(
            functools.partial(kernel, [len(u) for u in units], choices, table, piece),
            [jax.ShapeDtypeStruct((held, total), F32)] + [sent_shape] * (layers - 1),
            [IN_SMEM] + [IN_VMEM] * len(flat),
            [pltpu.VMEM((held, width), BF16)],
            (here, *flat),
            flops=2 * held * total * width,
            grant=grant,
        )

    early, *sent = scores(early_kernel, units[:-1], choices[:-1], [], (count - 1) * piece, 16 << 20)
    first = shifted(sent)
    late, *sent = scores(late_kernel, units[-1:], choices[-1:], [early], piece, 12 << 20)
    second = shifted(sent)
    out = call(
        functools.partial(finish_kernel, table, places, piece, layers),
        jax.ShapeDtypeStruct((per_owner * rows, train.shape[0]), F32),
        [IN_SMEM] + [IN_VMEM] * (2 + 2 * (layers - 1)),
        [],
        (here, early, late, *first, *second),
        flops=per_owner * rows * train.shape[0],
        grant=12 << 20,
    )
    return out[None]


def solution(mesh):
    return jax.shard_map(
        steps,
        mesh=mesh,
        in_specs=(
            P("layer", ("groups", "blk"), None),
            P("layer", "rep", ("groups", "blk"), None),
            P("layer", ("blk", "rep"), None),
            P("layer", ("blk", "rep")),
        ),
        out_specs=P("rep", "layer", ("groups", "blk")),
        check_vma=False,
    )
```

profile of v0, /device:TPU:0, one launch (start us, length us, event | category | flops | bytes accessed | tf_op | source)
XLA Modules:
  0.0 59.6 jit_solution(13838064839373493661)
XLA Ops:
  0.0 0.7 %collective-permute-start.5 = (bf16[64,4096]{1,0:T(8,128)(2,1)}, bf16[64,4096]{1,0:T(8,128)(2,1)S(1)}, u32[]{:S(2)}, u32[]{:S(2)}) collective-permute-start(bf16[64,4096]{1,0:T(8,128)(2,1)} %bitcast.11), channel_id=1, source_target_pairs={{4,8},{8,4},{5,9},{9,5},{6,10},{10,6},{7,11},{11,7},{20,24},{24,20... | collective-permute-start | bytes 1572872 | tf_op jit(solution)/shard_map/ppermute | solution.py:382
  0.7 5.9 %collective-permute-start.4 = (bf16[64,4096]{1,0:T(8,128)(2,1)}, bf16[64,4096]{1,0:T(8,128)(2,1)S(1)}, u32[]{:S(2)}, u32[]{:S(2)}) collective-permute-start(bf16[64,4096]{1,0:T(8,128)(2,1)} %bitcast.12), channel_id=1, source_target_pairs={{0,4},{4,0},{8,12},{12,8},{1,5},{5,1},{9,13},{13,9},{2,6},{6,2},{1... | collective-permute-start | bytes 1572872 | tf_op jit(solution)/shard_map/ppermute | solution.py:383
  6.6 0.7 %bitcast_convert_fusion = f32[8,128]{1,0:T(8,128)S(1)} fusion(bf16[1,8,128]{2,1,0:T(8,128)(2,1)} %param.6), kind=kLoop, calls=%fused_computation.2 | loop fusion | flops 1024 | bytes 6144 | tf_op jit(solution)/shard_map/convert_element_type | solution.py:387
  7.3 0.7 %pad_maximum_fusion.1 = f32[12,128]{1,0:T(8,128)S(1)} fusion(f32[4,128]{1,0:T(4,128)} %bitcast.14, f32[8,128]{1,0:T(8,128)S(1)} %bitcast_convert_fusion), kind=kLoop, calls=%fused_computation.1 | loop fusion | flops 1536 | bytes 12288 | tf_op jit(solution)/shard_map/concatenate | solution.py:387
  8.0 0.0 collective-permute-start
  8.0 1.2 %collective-permute-done = f32[12,128]{1,0:T(8,128)S(1)} collective-permute-done((f32[12,128]{1,0:T(8,128)S(1)}, f32[12,128]{1,0:T(8,128)S(1)}, u32[]{:S(2)}, u32[]{:S(2)}) %collective-permute-start) | collective-permute-done | bytes 6176 | tf_op jit(solution)/shard_map/ppermute | solution.py:390
  9.1 0.7 %pad_maximum_fusion.refs_0_ = f32[24,128]{1,0:T(8,128)S(1)} fusion(f32[12,128]{1,0:T(8,128)S(1)} %collective-permute-done, f32[4,128]{1,0:T(4,128)} %bitcast.15, f32[8,128]{1,0:T(8,128)S(1)} %bitcast_convert_fusion), kind=kLoop, calls=%fused_computation | loop fusion | flops 6144 | bytes 24576 | tf_op jit(solution)/shard_map/concatenate | solution.py:391
  9.8 0.0 collective-permute-start.1
  9.9 1.9 %collective-permute-start.2 = (f32[24,128]{1,0:T(8,128)S(1)}, f32[24,128]{1,0:T(8,128)S(1)}, u32[]{:S(2)}, u32[]{:S(2)}) collective-permute-start(f32[24,128]{1,0:T(8,128)S(1)} %pad_maximum_fusion.refs_0_), channel_id=1, source_target_pairs={{0,8},{4,12},{8,0},{12,4},{1,9},{5,13},{9,1},{13,5},{2,10},{6,14},... | collective-permute-start | bytes 36872 | tf_op jit(solution)/shard_map/ppermute | solution.py:394
  11.7 1.9 %collective-permute-start.3 = (f32[24,128]{1,0:T(8,128)S(1)}, f32[24,128]{1,0:T(8,128)S(1)}, u32[]{:S(2)}, u32[]{:S(2)}) collective-permute-start(f32[24,128]{1,0:T(8,128)S(1)} %pad_maximum_fusion.refs_0_), channel_id=1, source_target_pairs={{0,12},{4,0},{8,4},{12,8},{1,13},{5,1},{9,5},{13,9},{2,14},{6,2},{... | collective-permute-start | bytes 36872 | tf_op jit(solution)/shard_map/ppermute | solution.py:394
  13.7 0.1 pad_add_fusion.here_ref
  13.7 0.0 copy-start
  13.7 3.4 %copy-done = bf16[1,1024,4096]{2,1,0:T(8,128)(2,1)S(1)} copy-done((bf16[1,1024,4096]{2,1,0:T(8,128)(2,1)S(1)}, bf16[1,1024,4096]{2,1,0:T(8,128)(2,1)}, u32[]{:S(2)}) %copy-start) | copy-done | bytes 8388632
  17.1 0.0 copy-start.1
  17.1 0.6 %shard_map.49.refs_5_.refs_2_ = bf16[1024,4096]{1,0:T(8,128)(2,1)S(1)} custom-call(bf16[1024,4096]{1,0:T(8,128)(2,1)S(1)} %bitcast.10), custom_call_target="tpu_custom_call" | custom-call | bytes 16777216 | tf_op jit(solution)/shard_map/pallas_call | solution.py:353
  17.8 2.3 %collective-permute-done.1.refs_1_ = f32[24,128]{1,0:T(8,128)S(1)} collective-permute-done((f32[24,128]{1,0:T(8,128)S(1)}, f32[24,128]{1,0:T(8,128)S(1)}, u32[]{:S(2)}, u32[]{:S(2)}) %collective-permute-start.1) | collective-permute-done | bytes 12320 | tf_op jit(solution)/shard_map/ppermute | solution.py:394
  20.0 0.0 collective-permute-done.2.refs_2_
  20.0 0.0 collective-permute-done.3.refs_3_
  20.1 1.5 %shard_map.46 = (bf16[512,512]{1,0:T(8,128)(2,1)S(1)}, bf16[512,512]{1,0:T(8,128)(2,1)S(1)}, bf16[512,512]{1,0:T(8,128)(2,1)S(1)}, bf16[512,512]{1,0:T(8,128)(2,1)S(1)}, f32[512,256]{1,0:T(8,128)S(1)}) custom-call(s32[3]{0:T(128)S(1)} %pad_add_fusion.here_ref, f32[24,128]{1,0:T(8,128)S(1)} %pad_maximum_fusion.refs_0_, ...), custom_call_target="tpu_custom_call" | custom-call | flops 67108864 | bytes 2670604 | tf_op jit(solution)/shard_map/pallas_call | solution.py:24
  21.6 0.0 collective-permute-done.5.refs_0_
  21.6 1.3 %collective-permute-start.6 = (bf16[64,4096]{1,0:T(8,128)(2,1)S(1)}, bf16[64,4096]{1,0:T(8,128)(2,1)S(1)}, u32[]{:S(2)}, u32[]{:S(2)}) collective-permute-start(bf16[64,4096]{1,0:T(8,128)(2,1)S(1)} %collective-permute-done.5.refs_0_), channel_id=1, source_target_pairs={{4,0},{8,12},{5,1},{9,13},{6,2},{10,14},{7,3},{11,15},{20,16},{24,... | collective-permute-start | bytes 1572872 | tf_op jit(solution)/shard_map/ppermute | solution.py:398
  22.9 0.0 collective-permute-done.4.refs_0_
  22.9 2.2 %shard_map.48 = (bf16[64,4096]{1,0:T(8,128)(2,1)S(1)}, bf16[32,4096]{1,0:T(8,128)(2,1)S(1)}, bf16[32,4096]{1,0:T(8,128)(2,1)S(1)}) custom-call(s32[3]{0:T(128)S(1)} %pad_add_fusion.here_ref, bf16[64,4096]{1,0:T(8,128)(2,1)S(1)} %collective-permute-done.4.refs_0_, bf16[512,512]{1,0:T(8,128)(2,1)S(1)} %get-tuple-element.22.refs_1_.refs_2_, ...), custom_call_target="tpu_custom_call" | custom-call | flops 536870912 | bytes 4194316 | tf_op jit(solution)/shard_map/pallas_call | solution.py:24
  25.1 0.7 %collective-permute-start.7 = (bf16[32,4096]{1,0:T(8,128)(2,1)S(1)}, bf16[32,4096]{1,0:T(8,128)(2,1)S(1)}, u32[]{:S(2)}, u32[]{:S(2)}) collective-permute-start(bf16[32,4096]{1,0:T(8,128)(2,1)S(1)} %get-tuple-element.30), channel_id=1, source_target_pairs={{4,8},{8,4},{5,9},{9,5},{6,10},{10,6},{7,11},{11,7},{20,24},{24,20... | collective-permute-start | bytes 786440 | tf_op jit(solution)/shard_map/ppermute | solution.py:418
  25.8 0.7 %collective-permute-start.9 = (bf16[32,4096]{1,0:T(8,128)(2,1)S(1)}, bf16[32,4096]{1,0:T(8,128)(2,1)S(1)}, u32[]{:S(2)}, u32[]{:S(2)}) collective-permute-start(bf16[32,4096]{1,0:T(8,128)(2,1)S(1)} %get-tuple-element.34), channel_id=1, source_target_pairs={{4,8},{8,4},{5,9},{9,5},{6,10},{10,6},{7,11},{11,7},{20,24},{24,20... | collective-permute-start | bytes 786440 | tf_op jit(solution)/shard_map/ppermute | solution.py:418
  26.5 0.0 copy-done.1
  26.5 2.2 %shard_map.47.refs_0_ = bf16[64,4096]{1,0:T(8,128)(2,1)S(1)} custom-call(s32[3]{0:T(128)S(1)} %pad_add_fusion.here_ref, bf16[64,4096]{1,0:T(8,128)(2,1)S(1)} %bitcast.13, bf16[512,512]{1,0:T(8,128)(2,1)S(1)} %get-tuple-element.22.refs_1_.refs_2_, bf16[512,512]{1,0:T(8,128)(2,1)S(1)} %get-tuple-element.23.refs_2_.refs_3_, ...), custom_call_target="tpu_custom_call" | custom-call | flops 536870912 | bytes 3670028 | tf_op jit(solution)/shard_map/pallas_call | solution.py:24
  28.7 0.0 collective-permute-done.7.refs_3_
  28.7 1.3 %collective-permute-start.8 = (bf16[32,4096]{1,0:T(8,128)(2,1)S(1)}, bf16[32,4096]{1,0:T(8,128)(2,1)S(1)}, u32[]{:S(2)}, u32[]{:S(2)}) collective-permute-start(bf16[32,4096]{1,0:T(8,128)(2,1)S(1)} %collective-permute-done.7.refs_3_), channel_id=1, source_target_pairs={{4,0},{8,12},{5,1},{9,13},{6,2},{10,14},{7,3},{11,15},{20,16},{24,... | collective-permute-start | bytes 786440 | tf_op jit(solution)/shard_map/ppermute | solution.py:418
  30.0 0.0 collective-permute-done.9.refs_0_
  30.0 1.3 %collective-permute-start.10 = (bf16[32,4096]{1,0:T(8,128)(2,1)S(1)}, bf16[32,4096]{1,0:T(8,128)(2,1)S(1)}, u32[]{:S(2)}, u32[]{:S(2)}) collective-permute-start(bf16[32,4096]{1,0:T(8,128)(2,1)S(1)} %collective-permute-done.9.refs_0_), channel_id=1, source_target_pairs={{4,0},{8,12},{5,1},{9,13},{6,2},{10,14},{7,3},{11,15},{20,16},{24,... | collective-permute-start | bytes 786440 | tf_op jit(solution)/shard_map/ppermute | solution.py:418
  31.3 4.2 %collective-permute-done.6.refs_1_ = bf16[64,4096]{1,0:T(8,128)(2,1)S(1)} collective-permute-done((bf16[64,4096]{1,0:T(8,128)(2,1)S(1)}, bf16[64,4096]{1,0:T(8,128)(2,1)S(1)}, u32[]{:S(2)}, u32[]{:S(2)}) %collective-permute-start.6) | collective-permute-done | bytes 524320 | tf_op jit(solution)/shard_map/ppermute | solution.py:398
  35.4 2.3 %shard_map.50.refs_2_ = bf16[64,4096]{1,0:T(8,128)(2,1)S(1)} custom-call(s32[3]{0:T(128)S(1)} %pad_add_fusion.here_ref, bf16[64,4096]{1,0:T(8,128)(2,1)S(1)} %collective-permute-done.5.refs_0_, bf16[64,4096]{1,0:T(8,128)(2,1)S(1)} %collective-permute-done.6.refs_1_, bf16[512,512]{1,0:T(8,128)(2,1)S(1)} %get-tuple-element.22.refs_1_.refs_2_, ...), custom_call_target="tpu_custom_call" | custom-call | flops 536870912 | bytes 4194316 | tf_op jit(solution)/shard_map/pallas_call | solution.py:24
  37.7 8.5 %collective-permute-done.8.refs_4_ = bf16[32,4096]{1,0:T(8,128)(2,1)S(1)} collective-permute-done((bf16[32,4096]{1,0:T(8,128)(2,1)S(1)}, bf16[32,4096]{1,0:T(8,128)(2,1)S(1)}, u32[]{:S(2)}, u32[]{:S(2)}) %collective-permute-start.8) | collective-permute-done | bytes 262176 | tf_op jit(solution)/shard_map/ppermute | solution.py:418
  46.2 3.2 %shard_map.51 = (f32[224,1024]{1,0:T(8,128)S(1)}, bf16[96,1024]{1,0:T(8,128)(2,1)S(1)}) custom-call(s32[3]{0:T(128)S(1)} %pad_add_fusion.here_ref, bf16[64,4096]{1,0:T(8,128)(2,1)S(1)} %shard_map.47.refs_0_, bf16[64,4096]{1,0:T(8,128)(2,1)S(1)} %get-tuple-element.27.refs_1_, bf16[64,4096]{1,0:T(8,128)(2,1)S(1)} %shard_map.50.refs_2_, ...), custom_call_target="tpu_custom_call" | custom-call | flops 1879048192 | bytes 11599884 | tf_op jit(solution)/shard_map/pallas_call | solution.py:24
  49.4 1.6 %collective-permute-start.11 = (bf16[96,1024]{1,0:T(8,128)(2,1)S(1)}, bf16[96,1024]{1,0:T(8,128)(2,1)S(1)}, u32[]{:S(2)}, u32[]{:S(2)}) collective-permute-start(bf16[96,1024]{1,0:T(8,128)(2,1)S(1)} %get-tuple-element.37), channel_id=1, source_target_pairs={{0,2},{2,0},{1,3},{3,1},{4,6},{6,4},{5,7},{7,5},{8,10},{10,8},{9,1... | collective-permute-start | bytes 589832 | tf_op jit(solution)/shard_map/ppermute | solution.py:452
  51.0 0.0 collective-permute-done.10.refs_1_
  51.0 2.9 %shard_map.52 = (f32[32,1024]{1,0:T(8,128)S(1)}, bf16[32,1024]{1,0:T(8,128)(2,1)S(1)}) custom-call(s32[3]{0:T(128)S(1)} %pad_add_fusion.here_ref, bf16[32,4096]{1,0:T(8,128)(2,1)S(1)} %collective-permute-done.9.refs_0_, bf16[32,4096]{1,0:T(8,128)(2,1)S(1)} %collective-permute-done.10.refs_1_, bf16[1024,4096]{1,0:T(8,128)(2,1)S(1)} %shard_map.49.refs_5_.refs_2_, ...), custom_call_target="tpu_custom_call" | custom-call | flops 268435456 | bytes 10027020 | tf_op jit(solution)/shard_map/pallas_call | solution.py:24
  53.9 0.6 %collective-permute-start.12 = (bf16[32,1024]{1,0:T(8,128)(2,1)S(1)}, bf16[32,1024]{1,0:T(8,128)(2,1)S(1)}, u32[]{:S(2)}, u32[]{:S(2)}) collective-permute-start(bf16[32,1024]{1,0:T(8,128)(2,1)S(1)} %get-tuple-element.38), channel_id=1, source_target_pairs={{0,2},{2,0},{1,3},{3,1},{4,6},{6,4},{5,7},{7,5},{8,10},{10,8},{9,1... | collective-permute-start | bytes 196616 | tf_op jit(solution)/shard_map/ppermute | solution.py:452
  54.5 3.7 %collective-permute-done.12.refs_1_ = bf16[32,1024]{1,0:T(8,128)(2,1)S(1)} collective-permute-done((bf16[32,1024]{1,0:T(8,128)(2,1)S(1)}, bf16[32,1024]{1,0:T(8,128)(2,1)S(1)}, u32[]{:S(2)}, u32[]{:S(2)}) %collective-permute-start.12) | collective-permute-done | bytes 65568 | tf_op jit(solution)/shard_map/ppermute | solution.py:452
  58.2 0.0 collective-permute-done.11.refs_0_
  58.3 1.4 %shard_map.53 = f32[128,1024]{1,0:T(8,128)} custom-call(s32[3]{0:T(128)S(1)} %pad_add_fusion.here_ref, f32[224,1024]{1,0:T(8,128)S(1)} %get-tuple-element.33.refs_3_.early_ref, f32[32,1024]{1,0:T(8,128)S(1)} %get-tuple-element.36.late_ref, bf16[96,1024]{1,0:T(8,128)(2,1)S(1)} %collective-permute-done.11.refs_0_, ...), custom_call_target="tpu_custom_call" | custom-call | flops 131072 | bytes 1835020 | tf_op jit(solution)/shard_map/pallas_call | solution.py:24
Async XLA Ops:
  0.0 21.6 %collective-permute-start.5 = (bf16[64,4096]{1,0:T(8,128)(2,1)}, bf16[64,4096]{1,0:T(8,128)(2,1)S(1)}, u32[]{:S(2)}, u32[]{:S(2)}) collective-permute-start(bf16[64,4096]{1,0:T(8,128)(2,1)} %bitcast.11), channel_id=1, source_target_pairs={{4,8},{8,4},{5,9},{9,5},{6,10},{10,6},{7,11},{11,7},{20,24},{24,20... | collective-permute-start | bytes 1572872 | tf_op jit(solution)/shard_map/ppermute | solution.py:382
  0.7 22.2 %collective-permute-start.4 = (bf16[64,4096]{1,0:T(8,128)(2,1)}, bf16[64,4096]{1,0:T(8,128)(2,1)S(1)}, u32[]{:S(2)}, u32[]{:S(2)}) collective-permute-start(bf16[64,4096]{1,0:T(8,128)(2,1)} %bitcast.12), channel_id=1, source_target_pairs={{0,4},{4,0},{8,12},{12,8},{1,5},{5,1},{9,13},{13,9},{2,6},{6,2},{1... | collective-permute-start | bytes 1572872 | tf_op jit(solution)/shard_map/ppermute | solution.py:383
  8.0 1.2 %collective-permute-start = (f32[12,128]{1,0:T(8,128)S(1)}, f32[12,128]{1,0:T(8,128)S(1)}, u32[]{:S(2)}, u32[]{:S(2)}) collective-permute-start(f32[12,128]{1,0:T(8,128)S(1)} %pad_maximum_fusion.1), channel_id=1, source_target_pairs={{0,1},{1,0},{2,3},{3,2},{4,5},{5,4},{6,7},{7,6},{8,9},{9,8},{10,11... | collective-permute-start | bytes 18440 | tf_op jit(solution)/shard_map/ppermute | solution.py:390
  9.8 10.2 %collective-permute-start.1 = (f32[24,128]{1,0:T(8,128)S(1)}, f32[24,128]{1,0:T(8,128)S(1)}, u32[]{:S(2)}, u32[]{:S(2)}) collective-permute-start(f32[24,128]{1,0:T(8,128)S(1)} %pad_maximum_fusion.refs_0_), channel_id=1, source_target_pairs={{0,4},{4,8},{8,12},{12,0},{1,5},{5,9},{9,13},{13,1},{2,6},{6,10},{... | collective-permute-start | bytes 36872 | tf_op jit(solution)/shard_map/ppermute | solution.py:394
  9.9 10.2 %collective-permute-start.2 = (f32[24,128]{1,0:T(8,128)S(1)}, f32[24,128]{1,0:T(8,128)S(1)}, u32[]{:S(2)}, u32[]{:S(2)}) collective-permute-start(f32[24,128]{1,0:T(8,128)S(1)} %pad_maximum_fusion.refs_0_), channel_id=1, source_target_pairs={{0,8},{4,12},{8,0},{12,4},{1,9},{5,13},{9,1},{13,5},{2,10},{6,14},... | collective-permute-start | bytes 36872 | tf_op jit(solution)/shard_map/ppermute | solution.py:394
  11.7 8.3 %collective-permute-start.3 = (f32[24,128]{1,0:T(8,128)S(1)}, f32[24,128]{1,0:T(8,128)S(1)}, u32[]{:S(2)}, u32[]{:S(2)}) collective-permute-start(f32[24,128]{1,0:T(8,128)S(1)} %pad_maximum_fusion.refs_0_), channel_id=1, source_target_pairs={{0,12},{4,0},{8,4},{12,8},{1,13},{5,1},{9,5},{13,9},{2,14},{6,2},{... | collective-permute-start | bytes 36872 | tf_op jit(solution)/shard_map/ppermute | solution.py:394
  13.7 3.4 %copy-start = (bf16[1,1024,4096]{2,1,0:T(8,128)(2,1)S(1)}, bf16[1,1024,4096]{2,1,0:T(8,128)(2,1)}, u32[]{:S(2)}) copy-start(bf16[1,1024,4096]{2,1,0:T(8,128)(2,1)} %param.4) | copy-start | bytes 25165828
  17.1 9.3 %copy-start.1 = (bf16[1,1,64,4096]{3,2,1,0:T(8,128)(2,1)S(1)}, bf16[1,1,64,4096]{3,2,1,0:T(8,128)(2,1)}, u32[]{:S(2)}) copy-start(bf16[1,1,64,4096]{3,2,1,0:T(8,128)(2,1)} %param.5) | copy-start | bytes 1572868
  21.6 13.9 %collective-permute-start.6 = (bf16[64,4096]{1,0:T(8,128)(2,1)S(1)}, bf16[64,4096]{1,0:T(8,128)(2,1)S(1)}, u32[]{:S(2)}, u32[]{:S(2)}) collective-permute-start(bf16[64,4096]{1,0:T(8,128)(2,1)S(1)} %collective-permute-done.5.refs_0_), channel_id=1, source_target_pairs={{4,0},{8,12},{5,1},{9,13},{6,2},{10,14},{7,3},{11,15},{20,16},{24,... | collective-permute-start | bytes 1572872 | tf_op jit(solution)/shard_map/ppermute | solution.py:398
  25.1 3.6 %collective-permute-start.7 = (bf16[32,4096]{1,0:T(8,128)(2,1)S(1)}, bf16[32,4096]{1,0:T(8,128)(2,1)S(1)}, u32[]{:S(2)}, u32[]{:S(2)}) collective-permute-start(bf16[32,4096]{1,0:T(8,128)(2,1)S(1)} %get-tuple-element.30), channel_id=1, source_target_pairs={{4,8},{8,4},{5,9},{9,5},{6,10},{10,6},{7,11},{11,7},{20,24},{24,20... | collective-permute-start | bytes 786440 | tf_op jit(solution)/shard_map/ppermute | solution.py:418
  25.8 4.2 %collective-permute-start.9 = (bf16[32,4096]{1,0:T(8,128)(2,1)S(1)}, bf16[32,4096]{1,0:T(8,128)(2,1)S(1)}, u32[]{:S(2)}, u32[]{:S(2)}) collective-permute-start(bf16[32,4096]{1,0:T(8,128)(2,1)S(1)} %get-tuple-element.34), channel_id=1, source_target_pairs={{4,8},{8,4},{5,9},{9,5},{6,10},{10,6},{7,11},{11,7},{20,24},{24,20... | collective-permute-start | bytes 786440 | tf_op jit(solution)/shard_map/ppermute | solution.py:418
  28.7 17.5 %collective-permute-start.8 = (bf16[32,4096]{1,0:T(8,128)(2,1)S(1)}, bf16[32,4096]{1,0:T(8,128)(2,1)S(1)}, u32[]{:S(2)}, u32[]{:S(2)}) collective-permute-start(bf16[32,4096]{1,0:T(8,128)(2,1)S(1)} %collective-permute-done.7.refs_3_), channel_id=1, source_target_pairs={{4,0},{8,12},{5,1},{9,13},{6,2},{10,14},{7,3},{11,15},{20,16},{24,... | collective-permute-start | bytes 786440 | tf_op jit(solution)/shard_map/ppermute | solution.py:418
  30.0 21.0 %collective-permute-start.10 = (bf16[32,4096]{1,0:T(8,128)(2,1)S(1)}, bf16[32,4096]{1,0:T(8,128)(2,1)S(1)}, u32[]{:S(2)}, u32[]{:S(2)}) collective-permute-start(bf16[32,4096]{1,0:T(8,128)(2,1)S(1)} %collective-permute-done.9.refs_0_), channel_id=1, source_target_pairs={{4,0},{8,12},{5,1},{9,13},{6,2},{10,14},{7,3},{11,15},{20,16},{24,... | collective-permute-start | bytes 786440 | tf_op jit(solution)/shard_map/ppermute | solution.py:418
  49.4 8.8 %collective-permute-start.11 = (bf16[96,1024]{1,0:T(8,128)(2,1)S(1)}, bf16[96,1024]{1,0:T(8,128)(2,1)S(1)}, u32[]{:S(2)}, u32[]{:S(2)}) collective-permute-start(bf16[96,1024]{1,0:T(8,128)(2,1)S(1)} %get-tuple-element.37), channel_id=1, source_target_pairs={{0,2},{2,0},{1,3},{3,1},{4,6},{6,4},{5,7},{7,5},{8,10},{10,8},{9,1... | collective-permute-start | bytes 589832 | tf_op jit(solution)/shard_map/ppermute | solution.py:452
  53.9 4.3 %collective-permute-start.12 = (bf16[32,1024]{1,0:T(8,128)(2,1)S(1)}, bf16[32,1024]{1,0:T(8,128)(2,1)S(1)}, u32[]{:S(2)}, u32[]{:S(2)}) collective-permute-start(bf16[32,1024]{1,0:T(8,128)(2,1)S(1)} %get-tuple-element.38), channel_id=1, source_target_pairs={{0,2},{2,0},{1,3},{3,1},{4,6},{6,4},{5,7},{7,5},{8,10},{10,8},{9,1... | collective-permute-start | bytes 196616 | tf_op jit(solution)/shard_map/ppermute | solution.py:452
where the time goes:
time: 60 us; the launch traced here: 59.6 us
  waiting for transfers between devices  19.8 us (33%)
  starting transfers between devices  17.8 us (30%)
  Pallas kernels  16.3 us (27%)
  local copies, waits for them, and re-layouts  3.39 us (6%)
  other arithmetic  2.13 us (4%)
    pallas_call x7, Pallas kernels, call(): pl.pallas_call(kernel, out_shape=out_shape, in_specs=in_specs, out_specs=...  15.7 us
    ppermute x4, waiting for transfers between devices, steps(): lax.ppermute(w, 'blk', plan[step, parity])  8.5 us
    ppermute x1, starting transfers between devices, steps(): raw[1, 0] = lax.ppermute(own, 'blk', plan[1, 0])  5.91 us
    ppermute x1, waiting for transfers between devices, steps(): raw[2, 0] = lax.ppermute(raw[1, 1], 'blk', plan[2, 0])  4.16 us
    ppermute x4, starting transfers between devices, steps(): lax.ppermute(w, 'blk', plan[step, parity])  3.94 us
    ppermute x3, starting transfers between devices, steps(): lax.ppermute(pair, 'blk', [(a, (a + d) % blocks) for a in range(blocks)])  3.83 us
    ppermute x2, waiting for transfers between devices, shifted(): lax.ppermute(s, 'layer', [(o, (o + d) % layers) for o in range(layers)])  3.72 us
    unnamed x4, local copies, waits for them, and re-layouts  3.39 us
  transfers between devices with their start and end apart: 13, of which 5 were waited for; matrix products, arithmetic and copies ran while one was open for 4% of the time, Pallas kernels for 25%

commit v1 on v0

--- a/solution.py
+++ b/solution.py
@@ -155,14 +155,29 @@
     )
 
 
-def rotate_kernel(sources, choice, splits, here_ref, *refs):
+def pack_kernel(bases_ref, eigen_ref, out_ref):
+    rows = bases_ref.shape[0]
+    out_ref[:rows, :] = bases_ref[...].astype(F32)
+    out_ref[rows:, :] = eigen_ref[...]
+
+
+def head_kernel(rows_ref, out_ref):
+    out_ref[...] = rows_ref[: out_ref.shape[0], :]
+
+
+def head(value, rows):
+    shape = jax.ShapeDtypeStruct((rows, value.shape[1]), value.dtype)
+    return call(head_kernel, shape, [IN_VMEM], [], (value,), flops=0, grant=4 << 20)
+
+
+def rotate_kernel(sources, choice, split, here_ref, *refs):
     inputs, refs = refs[:sources], refs[sources:]
     w1_ref, but_ref, bu_ref, w5_ref, inv_ref = refs[:5]
-    outs = refs[5 : 6 + splits]
-    tall, first, second = refs[6 + splits :]
+    out_ref, *rest = refs[5:]
+    tall, first, second = rest[-3:]
+    size = but_ref.shape[0] // HALF
+    lanes = 2 * size
     fold = inputs[0].shape[0] // TILE
-    lanes = w1_ref.shape[0] // fold
-    size = lanes // 2
     pairs = size // 2
     half = size * fold
 
@@ -179,17 +194,25 @@
         which = lookup(choice, here_ref[0])
         for i in range(sources):
             pl.when(which == i)(functools.partial(gather_rows, inputs[i]))
+    full = w1_ref.shape[0] // 2
+    if half == full:
+        w1, w5, inverse = w1_ref[...], w5_ref[...], inv_ref[...]
+    else:
+        wide = fold * lanes
+        w1 = jnp.concatenate([w1_ref[:wide, k * full : k * full + half] for k in range(2)], axis=1)
+        w5 = jnp.concatenate([w5_ref[k * full : k * full + half, :wide] for k in range(2)], axis=0)
+        inverse = inv_ref[:, :half]
     chunk = 8
     parts = TILE // HALF
     for a0 in range(0, pairs, chunk):
-        rows = dot(tall[a0 * TILE : (a0 + chunk) * TILE, :], w1_ref[...])
+        rows = dot(tall[a0 * TILE : (a0 + chunk) * TILE, :], w1)
         for a in range(a0, a0 + chunk):
             for part in range(parts):
                 low = (a - a0) * TILE + part * HALF
                 for odd in range(2):
                     at = (2 * a + odd) * HALF
                     first[part, at : at + HALF, :] = rows[low : low + HALF, odd * half : (odd + 1) * half]
-    but, bu, inverse = but_ref[...], bu_ref[...], inv_ref[...]
+    but, bu = but_ref[...], bu_ref[...]
     for part in range(parts):
         scaled = (dot(but, first[part].astype(BF16)) * inverse).astype(BF16)
         second[part] = dot(bu, scaled)
@@ -199,30 +222,29 @@
             value = jnp.concatenate([second[part, at : at + HALF, :] for part in range(parts)], axis=0)
             tall[a * TILE : (a + 1) * TILE, odd * half : (odd + 1) * half] = value.astype(BF16)
     for a0 in range(0, pairs, chunk):
-        rows = dot(tall[a0 * TILE : (a0 + chunk) * TILE, :], w5_ref[...]).astype(BF16)
+        rows = dot(tall[a0 * TILE : (a0 + chunk) * TILE, :], w5).astype(BF16)
         for a in range(a0, a0 + chunk):
             for h in range(fold):
                 value = rows[(a - a0) * TILE : (a - a0 + 1) * TILE, h * lanes : (h + 1) * lanes]
-                outs[0][h * TILE : (h + 1) * TILE, a * lanes : (a + 1) * lanes] = value
-                if splits:
-                    per = fold // splits
-                    low = (h % per) * TILE
-                    outs[1 + h // per][low : low + TILE, a * lanes : (a + 1) * lanes] = value
-
-
-def rotate(here, choice, inputs, constants, splits=0):
+                out_ref[h * TILE : (h + 1) * TILE, a * lanes : (a + 1) * lanes] = value
+                low = h * TILE - split
+                if split and low >= 0:
+                    rest[0][low : low + TILE, a * lanes : (a + 1) * lanes] = value
+
+
+def rotate(here, choice, inputs, constants, split=0):
     rows, width = inputs[0].shape
     fold = rows // TILE
-    wide = constants[0].shape[0]
-    size = wide // (2 * fold)
+    size = constants[1].shape[0] // HALF
     shapes = [jax.ShapeDtypeStruct((rows, width), BF16)]
-    shapes += [jax.ShapeDtypeStruct((rows // splits, width), BF16)] * splits if splits else []
+    if split:
+        shapes.append(jax.ShapeDtypeStruct((rows - split, width), BF16))
     return call(
-        functools.partial(rotate_kernel, len(inputs), choice, splits),
+        functools.partial(rotate_kernel, len(inputs), choice, split),
         shapes,
         [IN_SMEM] + [IN_VMEM] * (len(inputs) + 5),
         [
-            pltpu.VMEM((size // 2 * TILE, wide), BF16),
+            pltpu.VMEM((size // 2 * TILE, 2 * size * fold), BF16),
             pltpu.VMEM((TILE // HALF, size * HALF, size * fold), F32),
             pltpu.VMEM((TILE // HALF, size * HALF, size * fold), F32),
         ],
@@ -377,14 +399,23 @@
     plan, arrivals = line_plan(blocks)
     here = jnp.stack([z, x, rep]).astype(jnp.int32)
     splits = 2
-
-    raw, turned = {}, {}
+    piece = rows // splits
+
+    raw, mixed = {}, {}
     raw[1, 1] = lax.ppermute(own, "blk", plan[1, 1])
     raw[1, 0] = lax.ppermute(own, "blk", plan[1, 0])
 
     eigen = eigenvalues.reshape(-1, lanes)
     eigen_rows = eigen.shape[0]
-    packed = jnp.concatenate([bases[0].astype(F32), eigen], axis=0)
+    packed = call(
+        pack_kernel,
+        jax.ShapeDtypeStruct((base_rows + eigen_rows, lanes), F32),
+        [IN_VMEM] * 2,
+        [],
+        (bases[0], eigen),
+        flops=0,
+        grant=4 << 20,
+    )
     pair = [packed]
     for e in range(1, reps):
         pair.append(lax.ppermute(packed, "rep", [(r, (r + e) % reps) for r in range(reps)]))
@@ -392,50 +423,64 @@
     parts = [pair]
     for d in range(1, blocks):
         parts.append(lax.ppermute(pair, "blk", [(a, (a + d) % blocks) for a in range(blocks)]))
-    train, _ = lax.optimization_barrier((train, pair))
+    train, here, _ = lax.optimization_barrier((train, here, pair))
     train = resident(train)
     raw[1, 1], train = lax.optimization_barrier((raw[1, 1], train))
     raw[2, 0] = lax.ppermute(raw[1, 1], "blk", plan[2, 0])
 
     constants = rotation_constants(parts, here, reps, base_rows, eigen_rows, size, fold)
     alone = [0] * blocks
-    whole_first, *turned[1, 0] = rotate(here, alone, [raw[1, 0]], constants, splits)
-    whole_own, = rotate(here, alone, [own], constants)
-
     block_of = [list(range(blocks))] + [[a[j][2] for a in arrivals] for j in range(blocks - 1)]
     source_of = [None] + [[a[j][:2] for a in arrivals] for j in range(blocks - 1)]
+
+    def hop(step, parity, value):
+        return lax.ppermute(value, "blk", plan[step, parity])
+
+    mixed[2, 1] = [hop(2, 1, head(raw[1, 0], piece))] if (2, 1) in plan else []
+    whole_first, last = rotate(here, alone, [raw[1, 0]], constants, piece)
+    if mixed[2, 1]:
+        mixed[2, 1].append(hop(2, 1, last))
+        if (3, 0) in plan:
+            mixed[3, 0] = [hop(3, 0, mixed[2, 1][0])]
+    whole_own, = rotate(here, alone, [own], constants)
     units, choices = [[whole_own], [whole_first]], [alone, alone]
+
+    turned_last = {}
+
+    def last_rows(name):
+        if name in mixed:
+            return mixed[name][1]
+        if name not in turned_last:
+            turned_last[name] = rotate(here, alone, [raw[name]], constants, piece)[1]
+        return turned_last[name]
+
+    def first_rows(name):
+        return mixed[name][0] if name in mixed else head(raw[name], piece)
+
     gate = whole_own
-    for step, parity in plan:
-        if step == 1 or (step, parity) in raw:
-            continue
-        before = (step - 1, 1 - parity)
-        if before not in turned:
-            turned[before] = rotate(here, alone, [raw[before]], constants, splits)[1:]
-        pieces = turned[before]
-        if step > 2:
-            pieces = [lax.optimization_barrier((w, gate))[0] for w in pieces]
-        turned[step, parity] = [lax.ppermute(w, "blk", plan[step, parity]) for w in pieces]
-
     for j in range(2, blocks):
         names = sorted(set(source_of[j]))
-        fresh = [n for n in names if n in raw and n not in turned]
-        ready = [n for n in names if n not in fresh]
-        if fresh:
-            choice = [fresh.index(s) if s in fresh else 0 for s in source_of[j]]
-            wide = rotate(here, choice, [raw[n] for n in fresh], constants, splits if ready else 0)
-        if not ready:
-            units.append([wide[0]])
-            choices.append(alone)
+        choice = [names.index(s) for s in source_of[j]]
+        if all(n in raw for n in names):
+            whole, = rotate(here, choice, [raw[n] for n in names], constants)
+            units.append([whole])
+            choices.append(choice if len(units[-1]) > 1 else alone)
+            gate = whole
             continue
-        for part in range(splits):
-            candidates = [wide[1 + part]] if fresh else []
-            offset = len(candidates)
-            candidates += [turned[n][part] for n in ready]
-            units.append(candidates)
-            choices.append([0 if s in fresh else offset + ready.index(s) for s in source_of[j]])
-
-    piece = rows // splits
+        for step, parity in plan:
+            if step > j or (step, parity) in raw:
+                continue
+            parts = mixed.setdefault((step, parity), [])
+            before = (step - 1, 1 - parity)
+            while len(parts) < splits:
+                value = last_rows(before) if parts else first_rows(before)
+                if step > 2:
+                    value, _ = lax.optimization_barrier((value, gate))
+                parts.append(hop(step, parity, value))
+        early_rows, = rotate(here, choice, [first_rows(n) for n in names], constants)
+        units += [[early_rows], [last_rows(n) for n in names]]
+        choices += [alone, choice]
+
     count = per_owner * splits
     table = [[[0] * layers for _ in range(blocks)] for _ in range(count)]
     places = [[[0] * layers for _ in range(blocks)] for _ in range(count)]

time: 60 us -> 60.4 us (level)
  waiting for transfers between devices: 19.8 us -> 15.4 us
  starting transfers between devices: 17.8 us -> 21.6 us
  other arithmetic: 2.13 us -> 0.08 us
  Pallas kernels: 16.3 us -> 18.1 us
  local copies, waits for them, and re-layouts: 3.39 us -> 4.74 us
    ppermute x4, waiting for transfers between devices: 8.5 us -> 1.45 us  [hop(): return lax.ppermute(value, 'blk', plan[step, parity])]
    ppermute x1, waiting for transfers between devices: 4.16 us -> 0.01 us  [steps(): raw[2, 0] = lax.ppermute(raw[1, 1], 'blk', plan[2, 0])]
    ppermute x1, waiting for transfers between devices: 0.01 us -> 3.96 us  [steps(): raw[1, 0] = lax.ppermute(own, 'blk', plan[1, 0])]
    ppermute x3, starting transfers between devices: 3.83 us -> 7.41 us  [steps(): lax.ppermute(pair, 'blk', [(a, (a + d) % blocks) for a in range(blocks)])]
    ppermute x3, waiting for transfers between devices: 2.27 us -> 5.36 us  [steps(): lax.ppermute(pair, 'blk', [(a, (a + d) % blocks) for a in range(blocks)])]
    pallas_call x7 -> x10, Pallas kernels: 15.7 us -> 17.5 us  [call(): pl.pallas_call(kernel, out_shape=out_shape, in_specs=in_specs, out_specs=...]
    unnamed x4 -> x8, local copies, waits for them, and re-layouts: 3.39 us -> 4.74 us
    concatenate x1 -> x0, other arithmetic: 0.69 us -> none  [steps(): packed = jnp.concatenate([bases[0].astype(F32), eigen], axis=0)]
  transfers between devices with their start and end apart: 13 -> 13, of which waited for: 5 -> 7; matrix products, arithmetic and copies ran while one was open for 4% -> 0% of each run, Pallas kernels for 25% -> 28%
where the time goes in v1:
time: 60.4 us; the launch traced here: 60.1 us
  starting transfers between devices  21.6 us (36%)
  Pallas kernels  18.1 us (30%)
  waiting for transfers between devices  15.4 us (25%)
  local copies, waits for them, and re-layouts  4.74 us (8%)
    pallas_call x10, Pallas kernels, call(): pl.pallas_call(kernel, out_shape=out_shape, in_specs=in_specs, out_specs=...  17.5 us
    ppermute x3, starting transfers between devices, steps(): lax.ppermute(pair, 'blk', [(a, (a + d) % blocks) for a in range(blocks)])  7.41 us
    ppermute x1, starting transfers between devices, steps(): raw[1, 0] = lax.ppermute(own, 'blk', plan[1, 0])  5.91 us
    ppermute x3, waiting for transfers between devices, steps(): lax.ppermute(pair, 'blk', [(a, (a + d) % blocks) for a in range(blocks)])  5.36 us
    unnamed x8, local copies, waits for them, and re-layouts  4.74 us
    ppermute x1, waiting for transfers between devices, steps(): raw[1, 0] = lax.ppermute(own, 'blk', plan[1, 0])  3.96 us
    ppermute x4, starting transfers between devices, hop(): return lax.ppermute(value, 'blk', plan[step, parity])  3.94 us
    ppermute x2, waiting for transfers between devices, shifted(): lax.ppermute(s, 'layer', [(o, (o + d) % layers) for o in range(layers)])  3.57 us
  transfers between devices with their start and end apart: 13, of which 7 were waited for; matrix products, arithmetic and copies ran while one was open for 0% of the time, Pallas kernels for 28%

profile of v1, /device:TPU:0, one launch (start us, length us, event | category | flops | bytes accessed | tf_op | source)
XLA Modules:
  0.0 60.1 jit_solution(14078408876106570011)
XLA Ops:
  0.0 0.7 %collective-permute-start.5 = (bf16[64,4096]{1,0:T(8,128)(2,1)}, bf16[64,4096]{1,0:T(8,128)(2,1)S(1)}, u32[]{:S(2)}, u32[]{:S(2)}) collective-permute-start(bf16[64,4096]{1,0:T(8,128)(2,1)} %bitcast.9), channel_id=1, source_target_pairs={{4,8},{8,4},{5,9},{9,5},{6,10},{10,6},{7,11},{11,7},{20,24},{24,20... | collective-permute-start | bytes 1572872 | tf_op jit(solution)/shard_map/ppermute | solution.py:405
  0.7 5.9 %collective-permute-start.4 = (bf16[64,4096]{1,0:T(8,128)(2,1)}, bf16[64,4096]{1,0:T(8,128)(2,1)S(1)}, u32[]{:S(2)}, u32[]{:S(2)}) collective-permute-start(bf16[64,4096]{1,0:T(8,128)(2,1)} %bitcast.10), channel_id=1, source_target_pairs={{0,4},{4,0},{8,12},{12,8},{1,5},{5,1},{9,13},{13,9},{2,6},{6,2},{1... | collective-permute-start | bytes 1572872 | tf_op jit(solution)/shard_map/ppermute | solution.py:406
  6.6 0.0 copy-start.2
  6.6 0.7 %copy-done.2 = bf16[1,8,128]{2,1,0:T(8,128)(2,1)S(1)} copy-done((bf16[1,8,128]{2,1,0:T(8,128)(2,1)S(1)}, bf16[1,8,128]{2,1,0:T(8,128)(2,1)}, u32[]{:S(2)}) %copy-start.2) | copy-done | bytes 2072
  7.3 0.0 copy-start.3
  7.3 0.7 %copy-done.3 = f32[1,512]{1,0:T(1,128)S(1)} copy-done((f32[1,512]{1,0:T(1,128)S(1)}, f32[1,512]{1,0:T(1,128)}, u32[]{:S(2)}) %copy-start.3) | copy-done | bytes 2072
  8.0 0.0 collective-permute-start
  8.0 0.1 pad_add_fusion.here_ref
  8.0 1.1 %collective-permute-done = f32[12,128]{1,0:T(8,128)S(1)} collective-permute-done((f32[12,128]{1,0:T(8,128)S(1)}, f32[12,128]{1,0:T(8,128)S(1)}, u32[]{:S(2)}, u32[]{:S(2)}) %collective-permute-start) | collective-permute-done | bytes 6176 | tf_op jit(solution)/shard_map/ppermute | solution.py:421
  9.1 0.0 copy-start
  9.2 3.4 %copy-done = bf16[1,1024,4096]{2,1,0:T(8,128)(2,1)S(1)} copy-done((bf16[1,1024,4096]{2,1,0:T(8,128)(2,1)S(1)}, bf16[1,1024,4096]{2,1,0:T(8,128)(2,1)}, u32[]{:S(2)}) %copy-start) | copy-done | bytes 8388632
  12.5 0.0 copy-start.1
  12.5 0.6 %shard_map.50.refs_4_.refs_2_ = bf16[1024,4096]{1,0:T(8,128)(2,1)S(1)} custom-call(bf16[1024,4096]{1,0:T(8,128)(2,1)S(1)} %bitcast.8), custom_call_target="tpu_custom_call" | custom-call | bytes 16777216 | tf_op jit(solution)/shard_map/pallas_call | solution.py:375
  13.2 0.0 collective-permute-done.5.refs_0_
  13.2 1.3 %collective-permute-start.6 = (bf16[64,4096]{1,0:T(8,128)(2,1)S(1)}, bf16[64,4096]{1,0:T(8,128)(2,1)S(1)}, u32[]{:S(2)}, u32[]{:S(2)}) collective-permute-start(bf16[64,4096]{1,0:T(8,128)(2,1)S(1)} %collective-permute-done.5.refs_0_), channel_id=1, source_target_pairs={{4,0},{8,12},{5,1},{9,13},{6,2},{10,14},{7,3},{11,15},{20,16},{24,... | collective-permute-start | bytes 1572872 | tf_op jit(solution)/shard_map/ppermute | solution.py:429
  14.5 4.0 %collective-permute-done.4.refs_0_.rows_ref = bf16[64,4096]{1,0:T(8,128)(2,1)S(1)} collective-permute-done((bf16[64,4096]{1,0:T(8,128)(2,1)}, bf16[64,4096]{1,0:T(8,128)(2,1)S(1)}, u32[]{:S(2)}, u32[]{:S(2)}) %collective-permute-start.4) | collective-permute-done | bytes 524320 | tf_op jit(solution)/shard_map/ppermute | solution.py:406
  18.5 0.7 %collective-permute-start.7 = (bf16[32,4096]{1,0:T(8,128)(2,1)S(1)}, bf16[32,4096]{1,0:T(8,128)(2,1)S(1)}, u32[]{:S(2)}, u32[]{:S(2)}) collective-permute-start(bf16[32,4096]{1,0:T(8,128)(2,1)S(1)} %shard_map.52), channel_id=1, source_target_pairs={{4,8},{8,4},{5,9},{9,5},{6,10},{10,6},{7,11},{11,7},{20,24},{24,20... | collective-permute-start | bytes 786440 | tf_op jit(solution)/shard_map/ppermute | solution.py:437
  19.2 4.5 %collective-permute-start.1 = (f32[24,128]{1,0:T(8,128)S(1)}, f32[24,128]{1,0:T(8,128)S(1)}, u32[]{:S(2)}, u32[]{:S(2)}) collective-permute-start(f32[24,128]{1,0:T(8,128)S(1)} %pad_maximum_fusion.refs_0_), channel_id=1, source_target_pairs={{0,4},{4,8},{8,12},{12,0},{1,5},{5,9},{9,13},{13,1},{2,6},{6,10},{... | collective-permute-start | bytes 36872 | tf_op jit(solution)/shard_map/ppermute | solution.py:425
  23.7 0.0 collective-permute-start.2
  23.7 2.8 %collective-permute-start.3 = (f32[24,128]{1,0:T(8,128)S(1)}, f32[24,128]{1,0:T(8,128)S(1)}, u32[]{:S(2)}, u32[]{:S(2)}) collective-permute-start(f32[24,128]{1,0:T(8,128)S(1)} %pad_maximum_fusion.refs_0_), channel_id=1, source_target_pairs={{0,12},{4,0},{8,4},{12,8},{1,13},{5,1},{9,5},{13,9},{2,14},{6,2},{... | collective-permute-start | bytes 36872 | tf_op jit(solution)/shard_map/ppermute | solution.py:425
  26.6 0.0 collective-permute-done.1.refs_1_
  26.6 3.0 %collective-permute-done.2.refs_2_ = f32[24,128]{1,0:T(8,128)S(1)} collective-permute-done((f32[24,128]{1,0:T(8,128)S(1)}, f32[24,128]{1,0:T(8,128)S(1)}, u32[]{:S(2)}, u32[]{:S(2)}) %collective-permute-start.2) | collective-permute-done | bytes 12320 | tf_op jit(solution)/shard_map/ppermute | solution.py:425
  29.6 2.4 %collective-permute-done.3.refs_3_ = f32[24,128]{1,0:T(8,128)S(1)} collective-permute-done((f32[24,128]{1,0:T(8,128)S(1)}, f32[24,128]{1,0:T(8,128)S(1)}, u32[]{:S(2)}, u32[]{:S(2)}) %collective-permute-start.3) | collective-permute-done | bytes 12320 | tf_op jit(solution)/shard_map/ppermute | solution.py:425
  31.9 1.5 %shard_map.47 = (bf16[512,512]{1,0:T(8,128)(2,1)S(1)}, bf16[512,512]{1,0:T(8,128)(2,1)S(1)}, bf16[512,512]{1,0:T(8,128)(2,1)S(1)}, bf16[512,512]{1,0:T(8,128)(2,1)S(1)}, f32[512,256]{1,0:T(8,128)S(1)}) custom-call(s32[3]{0:T(128)S(1)} %pad_add_fusion.here_ref, f32[24,128]{1,0:T(8,128)S(1)} %pad_maximum_fusion.refs_0_, ...), custom_call_target="tpu_custom_call" | custom-call | flops 67108864 | bytes 2670604 | tf_op jit(solution)/shard_map/pallas_call | solution.py:24
  33.4 2.2 %shard_map.49 = (bf16[64,4096]{1,0:T(8,128)(2,1)S(1)}, bf16[32,4096]{1,0:T(8,128)(2,1)S(1)}) custom-call(s32[3]{0:T(128)S(1)} %pad_add_fusion.here_ref, bf16[64,4096]{1,0:T(8,128)(2,1)S(1)} %collective-permute-done.4.refs_0_.rows_ref, bf16[512,512]{1,0:T(8,128)(2,1)S(1)} %get-tuple-element.22.refs_1_.refs_2_, ...), custom_call_target="tpu_custom_call" | custom-call | flops 536870912 | bytes 3932172 | tf_op jit(solution)/shard_map/pallas_call | solution.py:24
  35.6 0.7 %collective-permute-start.9 = (bf16[32,4096]{1,0:T(8,128)(2,1)S(1)}, bf16[32,4096]{1,0:T(8,128)(2,1)S(1)}, u32[]{:S(2)}, u32[]{:S(2)}) collective-permute-start(bf16[32,4096]{1,0:T(8,128)(2,1)S(1)} %get-tuple-element.32), channel_id=1, source_target_pairs={{4,8},{8,4},{5,9},{9,5},{6,10},{10,6},{7,11},{11,7},{20,24},{24,20... | collective-permute-start | bytes 786440 | tf_op jit(solution)/shard_map/ppermute | solution.py:437
  36.3 0.0 collective-permute-done.7.refs_0_
  36.3 1.3 %collective-permute-start.8 = (bf16[32,4096]{1,0:T(8,128)(2,1)S(1)}, bf16[32,4096]{1,0:T(8,128)(2,1)S(1)}, u32[]{:S(2)}, u32[]{:S(2)}) collective-permute-start(bf16[32,4096]{1,0:T(8,128)(2,1)S(1)} %collective-permute-done.7.refs_0_), channel_id=1, source_target_pairs={{4,0},{8,12},{5,1},{9,13},{6,2},{10,14},{7,3},{11,15},{20,16},{24,... | collective-permute-start | bytes 786440 | tf_op jit(solution)/shard_map/ppermute | solution.py:437
  37.6 0.0 copy-done.1
  37.6 2.2 %shard_map.48.refs_0_ = bf16[64,4096]{1,0:T(8,128)(2,1)S(1)} custom-call(s32[3]{0:T(128)S(1)} %pad_add_fusion.here_ref, bf16[64,4096]{1,0:T(8,128)(2,1)S(1)} %bitcast.11, bf16[512,512]{1,0:T(8,128)(2,1)S(1)} %get-tuple-element.22.refs_1_.refs_2_, bf16[512,512]{1,0:T(8,128)(2,1)S(1)} %get-tuple-element.23.refs_2_.refs_3_, ...), custom_call_target="tpu_custom_call" | custom-call | flops 536870912 | bytes 3670028 | tf_op jit(solution)/shard_map/pallas_call | solution.py:24
  39.8 0.0 collective-permute-done.6.refs_1_
  39.8 2.3 %shard_map.51.refs_2_ = bf16[64,4096]{1,0:T(8,128)(2,1)S(1)} custom-call(s32[3]{0:T(128)S(1)} %pad_add_fusion.here_ref, bf16[64,4096]{1,0:T(8,128)(2,1)S(1)} %collective-permute-done.5.refs_0_, bf16[64,4096]{1,0:T(8,128)(2,1)S(1)} %collective-permute-done.6.refs_1_, bf16[512,512]{1,0:T(8,128)(2,1)S(1)} %get-tuple-element.22.refs_1_.refs_2_, ...), custom_call_target="tpu_custom_call" | custom-call | flops 536870912 | bytes 4194316 | tf_op jit(solution)/shard_map/pallas_call | solution.py:24
  42.1 0.0 collective-permute-done.9.refs_0_
  42.1 1.3 %collective-permute-start.10 = (bf16[32,4096]{1,0:T(8,128)(2,1)S(1)}, bf16[32,4096]{1,0:T(8,128)(2,1)S(1)}, u32[]{:S(2)}, u32[]{:S(2)}) collective-permute-start(bf16[32,4096]{1,0:T(8,128)(2,1)S(1)} %collective-permute-done.9.refs_0_), channel_id=1, source_target_pairs={{4,0},{8,12},{5,1},{9,13},{6,2},{10,14},{7,3},{11,15},{20,16},{24,... | collective-permute-start | bytes 786440 | tf_op jit(solution)/shard_map/ppermute | solution.py:437
  43.4 1.4 %collective-permute-done.8.refs_1_ = bf16[32,4096]{1,0:T(8,128)(2,1)S(1)} collective-permute-done((bf16[32,4096]{1,0:T(8,128)(2,1)S(1)}, bf16[32,4096]{1,0:T(8,128)(2,1)S(1)}, u32[]{:S(2)}, u32[]{:S(2)}) %collective-permute-start.8) | collective-permute-done | bytes 262176 | tf_op jit(solution)/shard_map/ppermute | solution.py:437
  44.8 2.0 %shard_map.53.refs_3_ = bf16[32,4096]{1,0:T(8,128)(2,1)S(1)} custom-call(s32[3]{0:T(128)S(1)} %pad_add_fusion.here_ref, bf16[32,4096]{1,0:T(8,128)(2,1)S(1)} %collective-permute-done.7.refs_0_, bf16[32,4096]{1,0:T(8,128)(2,1)S(1)} %collective-permute-done.8.refs_1_, bf16[512,512]{1,0:T(8,128)(2,1)S(1)} %get-tuple-element.22.refs_1_.refs_2_, ...), custom_call_target="tpu_custom_call" | custom-call | flops 134217728 | bytes 3407884 | tf_op jit(solution)/shard_map/pallas_call | solution.py:24
  46.8 3.1 %shard_map.54 = (f32[224,1024]{1,0:T(8,128)S(1)}, bf16[96,1024]{1,0:T(8,128)(2,1)S(1)}) custom-call(s32[3]{0:T(128)S(1)} %pad_add_fusion.here_ref, bf16[64,4096]{1,0:T(8,128)(2,1)S(1)} %shard_map.48.refs_0_, bf16[64,4096]{1,0:T(8,128)(2,1)S(1)} %get-tuple-element.27.refs_1_, bf16[64,4096]{1,0:T(8,128)(2,1)S(1)} %shard_map.51.refs_2_, ...), custom_call_target="tpu_custom_call" | custom-call | flops 1879048192 | bytes 11337740 | tf_op jit(solution)/shard_map/pallas_call | solution.py:24
  49.9 1.6 %collective-permute-start.11 = (bf16[96,1024]{1,0:T(8,128)(2,1)S(1)}, bf16[96,1024]{1,0:T(8,128)(2,1)S(1)}, u32[]{:S(2)}, u32[]{:S(2)}) collective-permute-start(bf16[96,1024]{1,0:T(8,128)(2,1)S(1)} %get-tuple-element.35), channel_id=1, source_target_pairs={{0,2},{2,0},{1,3},{3,1},{4,6},{6,4},{5,7},{7,5},{8,10},{10,8},{9,1... | collective-permute-start | bytes 589832 | tf_op jit(solution)/shard_map/ppermute | solution.py:497
  51.4 0.0 collective-permute-done.10.refs_1_
  51.4 2.9 %shard_map.55 = (f32[32,1024]{1,0:T(8,128)S(1)}, bf16[32,1024]{1,0:T(8,128)(2,1)S(1)}) custom-call(s32[3]{0:T(128)S(1)} %pad_add_fusion.here_ref, bf16[32,4096]{1,0:T(8,128)(2,1)S(1)} %collective-permute-done.9.refs_0_, bf16[32,4096]{1,0:T(8,128)(2,1)S(1)} %collective-permute-done.10.refs_1_, bf16[1024,4096]{1,0:T(8,128)(2,1)S(1)} %shard_map.50.refs_4_.refs_2_, ...), custom_call_target="tpu_custom_call" | custom-call | flops 268435456 | bytes 10027020 | tf_op jit(solution)/shard_map/pallas_call | solution.py:24
  54.4 0.8 %collective-permute-start.12 = (bf16[32,1024]{1,0:T(8,128)(2,1)S(1)}, bf16[32,1024]{1,0:T(8,128)(2,1)S(1)}, u32[]{:S(2)}, u32[]{:S(2)}) collective-permute-start(bf16[32,1024]{1,0:T(8,128)(2,1)S(1)} %get-tuple-element.36), channel_id=1, source_target_pairs={{0,2},{2,0},{1,3},{3,1},{4,6},{6,4},{5,7},{7,5},{8,10},{10,8},{9,1... | collective-permute-start | bytes 196616 | tf_op jit(solution)/shard_map/ppermute | solution.py:497
  55.1 1.2 %collective-permute-done.11.refs_0_ = bf16[96,1024]{1,0:T(8,128)(2,1)S(1)} collective-permute-done((bf16[96,1024]{1,0:T(8,128)(2,1)S(1)}, bf16[96,1024]{1,0:T(8,128)(2,1)S(1)}, u32[]{:S(2)}, u32[]{:S(2)}) %collective-permute-start.11) | collective-permute-done | bytes 196640 | tf_op jit(solution)/shard_map/ppermute | solution.py:497
  56.3 2.4 %collective-permute-done.12.refs_1_ = bf16[32,1024]{1,0:T(8,128)(2,1)S(1)} collective-permute-done((bf16[32,1024]{1,0:T(8,128)(2,1)S(1)}, bf16[32,1024]{1,0:T(8,128)(2,1)S(1)}, u32[]{:S(2)}, u32[]{:S(2)}) %collective-permute-start.12) | collective-permute-done | bytes 65568 | tf_op jit(solution)/shard_map/ppermute | solution.py:497
  58.7 1.4 %shard_map.56 = f32[128,1024]{1,0:T(8,128)} custom-call(s32[3]{0:T(128)S(1)} %pad_add_fusion.here_ref, f32[224,1024]{1,0:T(8,128)S(1)} %get-tuple-element.31.refs_3_.early_ref, f32[32,1024]{1,0:T(8,128)S(1)} %get-tuple-element.34.late_ref, bf16[96,1024]{1,0:T(8,128)(2,1)S(1)} %collective-permute-done.11.refs_0_, ...), custom_call_target="tpu_custom_call" | custom-call | flops 131072 | bytes 1835020 | tf_op jit(solution)/shard_map/pallas_call | solution.py:24
  (3 shorter events, 0.0 us)
Async XLA Ops:
  0.0 13.2 %collective-permute-start.5 = (bf16[64,4096]{1,0:T(8,128)(2,1)}, bf16[64,4096]{1,0:T(8,128)(2,1)S(1)}, u32[]{:S(2)}, u32[]{:S(2)}) collective-permute-start(bf16[64,4096]{1,0:T(8,128)(2,1)} %bitcast.9), channel_id=1, source_target_pairs={{4,8},{8,4},{5,9},{9,5},{6,10},{10,6},{7,11},{11,7},{20,24},{24,20... | collective-permute-start | bytes 1572872 | tf_op jit(solution)/shard_map/ppermute | solution.py:405
  0.7 17.8 %collective-permute-start.4 = (bf16[64,4096]{1,0:T(8,128)(2,1)}, bf16[64,4096]{1,0:T(8,128)(2,1)S(1)}, u32[]{:S(2)}, u32[]{:S(2)}) collective-permute-start(bf16[64,4096]{1,0:T(8,128)(2,1)} %bitcast.10), channel_id=1, source_target_pairs={{0,4},{4,0},{8,12},{12,8},{1,5},{5,1},{9,13},{13,9},{2,6},{6,2},{1... | collective-permute-start | bytes 1572872 | tf_op jit(solution)/shard_map/ppermute | solution.py:406
  6.6 0.7 %copy-start.2 = (bf16[1,8,128]{2,1,0:T(8,128)(2,1)S(1)}, bf16[1,8,128]{2,1,0:T(8,128)(2,1)}, u32[]{:S(2)}) copy-start(bf16[1,8,128]{2,1,0:T(8,128)(2,1)} %param.6) | copy-start | bytes 6148
  7.3 0.7 %copy-start.3 = (f32[1,512]{1,0:T(1,128)S(1)}, f32[1,512]{1,0:T(1,128)}, u32[]{:S(2)}) copy-start(f32[1,512]{1,0:T(1,128)} %param.7) | copy-start | bytes 6148
  8.0 1.2 %collective-permute-start = (f32[12,128]{1,0:T(8,128)S(1)}, f32[12,128]{1,0:T(8,128)S(1)}, u32[]{:S(2)}, u32[]{:S(2)}) collective-permute-start(f32[12,128]{1,0:T(8,128)S(1)} %shard_map.46), channel_id=1, source_target_pairs={{0,1},{1,0},{2,3},{3,2},{4,5},{5,4},{6,7},{7,6},{8,9},{9,8},{10,11... | collective-permute-start | bytes 18440 | tf_op jit(solution)/shard_map/ppermute | solution.py:421
  9.1 3.4 %copy-start = (bf16[1,1024,4096]{2,1,0:T(8,128)(2,1)S(1)}, bf16[1,1024,4096]{2,1,0:T(8,128)(2,1)}, u32[]{:S(2)}) copy-start(bf16[1,1024,4096]{2,1,0:T(8,128)(2,1)} %param.4) | copy-start | bytes 25165828
  12.5 25.1 %copy-start.1 = (bf16[1,1,64,4096]{3,2,1,0:T(8,128)(2,1)S(1)}, bf16[1,1,64,4096]{3,2,1,0:T(8,128)(2,1)}, u32[]{:S(2)}) copy-start(bf16[1,1,64,4096]{3,2,1,0:T(8,128)(2,1)} %param.5) | copy-start | bytes 1572868
  13.2 26.6 %collective-permute-start.6 = (bf16[64,4096]{1,0:T(8,128)(2,1)S(1)}, bf16[64,4096]{1,0:T(8,128)(2,1)S(1)}, u32[]{:S(2)}, u32[]{:S(2)}) collective-permute-start(bf16[64,4096]{1,0:T(8,128)(2,1)S(1)} %collective-permute-done.5.refs_0_), channel_id=1, source_target_pairs={{4,0},{8,12},{5,1},{9,13},{6,2},{10,14},{7,3},{11,15},{20,16},{24,... | collective-permute-start | bytes 1572872 | tf_op jit(solution)/shard_map/ppermute | solution.py:429
  18.5 17.8 %collective-permute-start.7 = (bf16[32,4096]{1,0:T(8,128)(2,1)S(1)}, bf16[32,4096]{1,0:T(8,128)(2,1)S(1)}, u32[]{:S(2)}, u32[]{:S(2)}) collective-permute-start(bf16[32,4096]{1,0:T(8,128)(2,1)S(1)} %shard_map.52), channel_id=1, source_target_pairs={{4,8},{8,4},{5,9},{9,5},{6,10},{10,6},{7,11},{11,7},{20,24},{24,20... | collective-permute-start | bytes 786440 | tf_op jit(solution)/shard_map/ppermute | solution.py:437
  19.2 7.4 %collective-permute-start.1 = (f32[24,128]{1,0:T(8,128)S(1)}, f32[24,128]{1,0:T(8,128)S(1)}, u32[]{:S(2)}, u32[]{:S(2)}) collective-permute-start(f32[24,128]{1,0:T(8,128)S(1)} %pad_maximum_fusion.refs_0_), channel_id=1, source_target_pairs={{0,4},{4,8},{8,12},{12,0},{1,5},{5,9},{9,13},{13,1},{2,6},{6,10},{... | collective-permute-start | bytes 36872 | tf_op jit(solution)/shard_map/ppermute | solution.py:425
  23.7 5.9 %collective-permute-start.2 = (f32[24,128]{1,0:T(8,128)S(1)}, f32[24,128]{1,0:T(8,128)S(1)}, u32[]{:S(2)}, u32[]{:S(2)}) collective-permute-start(f32[24,128]{1,0:T(8,128)S(1)} %pad_maximum_fusion.refs_0_), channel_id=1, source_target_pairs={{0,8},{4,12},{8,0},{12,4},{1,9},{5,13},{9,1},{13,5},{2,10},{6,14},... | collective-permute-start | bytes 36872 | tf_op jit(solution)/shard_map/ppermute | solution.py:425
  23.7 8.2 %collective-permute-start.3 = (f32[24,128]{1,0:T(8,128)S(1)}, f32[24,128]{1,0:T(8,128)S(1)}, u32[]{:S(2)}, u32[]{:S(2)}) collective-permute-start(f32[24,128]{1,0:T(8,128)S(1)} %pad_maximum_fusion.refs_0_), channel_id=1, source_target_pairs={{0,12},{4,0},{8,4},{12,8},{1,13},{5,1},{9,5},{13,9},{2,14},{6,2},{... | collective-permute-start | bytes 36872 | tf_op jit(solution)/shard_map/ppermute | solution.py:425
  35.6 6.5 %collective-permute-start.9 = (bf16[32,4096]{1,0:T(8,128)(2,1)S(1)}, bf16[32,4096]{1,0:T(8,128)(2,1)S(1)}, u32[]{:S(2)}, u32[]{:S(2)}) collective-permute-start(bf16[32,4096]{1,0:T(8,128)(2,1)S(1)} %get-tuple-element.32), channel_id=1, source_target_pairs={{4,8},{8,4},{5,9},{9,5},{6,10},{10,6},{7,11},{11,7},{20,24},{24,20... | collective-permute-start | bytes 786440 | tf_op jit(solution)/shard_map/ppermute | solution.py:437
  36.3 8.5 %collective-permute-start.8 = (bf16[32,4096]{1,0:T(8,128)(2,1)S(1)}, bf16[32,4096]{1,0:T(8,128)(2,1)S(1)}, u32[]{:S(2)}, u32[]{:S(2)}) collective-permute-start(bf16[32,4096]{1,0:T(8,128)(2,1)S(1)} %collective-permute-done.7.refs_0_), channel_id=1, source_target_pairs={{4,0},{8,12},{5,1},{9,13},{6,2},{10,14},{7,3},{11,15},{20,16},{24,... | collective-permute-start | bytes 786440 | tf_op jit(solution)/shard_map/ppermute | solution.py:437
  42.1 9.3 %collective-permute-start.10 = (bf16[32,4096]{1,0:T(8,128)(2,1)S(1)}, bf16[32,4096]{1,0:T(8,128)(2,1)S(1)}, u32[]{:S(2)}, u32[]{:S(2)}) collective-permute-start(bf16[32,4096]{1,0:T(8,128)(2,1)S(1)} %collective-permute-done.9.refs_0_), channel_id=1, source_target_pairs={{4,0},{8,12},{5,1},{9,13},{6,2},{10,14},{7,3},{11,15},{20,16},{24,... | collective-permute-start | bytes 786440 | tf_op jit(solution)/shard_map/ppermute | solution.py:437
  49.9 6.4 %collective-permute-start.11 = (bf16[96,1024]{1,0:T(8,128)(2,1)S(1)}, bf16[96,1024]{1,0:T(8,128)(2,1)S(1)}, u32[]{:S(2)}, u32[]{:S(2)}) collective-permute-start(bf16[96,1024]{1,0:T(8,128)(2,1)S(1)} %get-tuple-element.35), channel_id=1, source_target_pairs={{0,2},{2,0},{1,3},{3,1},{4,6},{6,4},{5,7},{7,5},{8,10},{10,8},{9,1... | collective-permute-start | bytes 589832 | tf_op jit(solution)/shard_map/ppermute | solution.py:497
  54.4 4.3 %collective-permute-start.12 = (bf16[32,1024]{1,0:T(8,128)(2,1)S(1)}, bf16[32,1024]{1,0:T(8,128)(2,1)S(1)}, u32[]{:S(2)}, u32[]{:S(2)}) collective-permute-start(bf16[32,1024]{1,0:T(8,128)(2,1)S(1)} %get-tuple-element.36), channel_id=1, source_target_pairs={{0,2},{2,0},{1,3},{3,1},{4,6},{6,4},{5,7},{7,5},{8,10},{10,8},{9,1... | collective-permute-start | bytes 196616 | tf_op jit(solution)/shard_map/ppermute | solution.py:497

commit v2 on v1

--- a/solution.py
+++ b/solution.py
@@ -170,11 +170,9 @@
     return call(head_kernel, shape, [IN_VMEM], [], (value,), flops=0, grant=4 << 20)
 
 
-def rotate_kernel(sources, choice, split, here_ref, *refs):
-    inputs, refs = refs[:sources], refs[sources:]
-    w1_ref, but_ref, bu_ref, w5_ref, inv_ref = refs[:5]
-    out_ref, *rest = refs[5:]
-    tall, first, second = rest[-3:]
+def turn(inputs, choice, here_ref, constants, scratch, write):
+    w1_ref, but_ref, bu_ref, w5_ref, inv_ref = constants
+    tall, first, second = scratch
     size = but_ref.shape[0] // HALF
     lanes = 2 * size
     fold = inputs[0].shape[0] // TILE
@@ -188,11 +186,11 @@
                     h * TILE : (h + 1) * TILE, a * lanes : (a + 1) * lanes
                 ]
 
-    if sources == 1:
+    if len(inputs) == 1:
         gather_rows(inputs[0])
     else:
         which = lookup(choice, here_ref[0])
-        for i in range(sources):
+        for i in range(len(inputs)):
             pl.when(which == i)(functools.partial(gather_rows, inputs[i]))
     full = w1_ref.shape[0] // 2
     if half == full:
@@ -226,10 +224,30 @@
         for a in range(a0, a0 + chunk):
             for h in range(fold):
                 value = rows[(a - a0) * TILE : (a - a0 + 1) * TILE, h * lanes : (h + 1) * lanes]
-                out_ref[h * TILE : (h + 1) * TILE, a * lanes : (a + 1) * lanes] = value
-                low = h * TILE - split
-                if split and low >= 0:
-                    rest[0][low : low + TILE, a * lanes : (a + 1) * lanes] = value
+                write(h * TILE, a * lanes, value)
+
+
+def rotate_kernel(sources, choice, split, here_ref, *refs):
+    inputs, refs = refs[:sources], refs[sources:]
+    out_ref, *rest = refs[5:]
+
+    def write(row, lane, value):
+        rows, lanes = value.shape
+        out_ref[row : row + rows, lane : lane + lanes] = value
+        if split and row >= split:
+            rest[0][row - split : row - split + rows, lane : lane + lanes] = value
+
+    turn(inputs, choice, here_ref, refs[:5], rest[-3:], write)
+
+
+def turn_scratch(rows, constants):
+    size = constants[1].shape[0] // HALF
+    fold = rows // TILE
+    return [
+        pltpu.VMEM((size // 2 * TILE, 2 * size * fold), BF16),
+        pltpu.VMEM((TILE // HALF, size * HALF, size * fold), F32),
+        pltpu.VMEM((TILE // HALF, size * HALF, size * fold), F32),
+    ]
 
 
 def rotate(here, choice, inputs, constants, split=0):
@@ -243,11 +261,7 @@
         functools.partial(rotate_kernel, len(inputs), choice, split),
         shapes,
         [IN_SMEM] + [IN_VMEM] * (len(inputs) + 5),
-        [
-            pltpu.VMEM((size // 2 * TILE, 2 * size * fold), BF16),
-            pltpu.VMEM((TILE // HALF, size * HALF, size * fold), F32),
-            pltpu.VMEM((TILE // HALF, size * HALF, size * fold), F32),
-        ],
+        turn_scratch(rows, constants),
         (here, *inputs, *constants),
         flops=8 * rows * width * size * fold,
         grant=12 << 20,
@@ -291,12 +305,22 @@
     return pl.ds(pl.multiple_of(start, rows), rows)
 
 
-def early_kernel(shape, choices, table, piece, here_ref, *refs):
+def early_kernel(shape, choices, table, piece, raw_choice, here_ref, *refs):
     refs = list(refs)
     units = [[refs.pop(0) for _ in range(n)] for n in shape]
-    x_ref, kept_ref, *sent = refs[:-1]
-    held = refs[-1]
+    x_ref = refs.pop(0)
+    inputs = [refs.pop(0) for _ in range(len(set(raw_choice)))]
+    constants = [refs.pop(0) for _ in range(5)]
+    *scratch, held = refs[-4:]
+    kept_ref, *sent = refs[:-4]
     fill(held, units, choices, here_ref)
+    base = held.shape[0] - piece
+
+    def write(row, lane, value):
+        rows, lanes = value.shape
+        held[base + row : base + row + rows, lane : lane + lanes] = value
+
+    turn(inputs, raw_choice, here_ref, constants, scratch, write)
     products(held, x_ref, kept_ref)
     z, x = here_ref[0], here_ref[1]
     layers = len(sent) + 1
@@ -329,33 +353,37 @@
             sent_ref[...] = early_ref[aligned(start, piece), :].astype(BF16)
 
 
-def finish_kernel(table, places, piece, layers, here_ref, early_ref, late_ref, *refs):
+def first_finish_kernel(table, places, piece, here_ref, early_ref, *refs):
     *received, out_ref = refs
     z, x = here_ref[0], here_ref[1]
-    shifts = layers - 1
-    first, second = received[:shifts], received[shifts:]
+    for p in range(len(table) - 1):
+        value = early_ref[aligned(grid_lookup(table[p], z, x), piece), :]
+        for ref in received:
+            value = value + ref[p * piece : (p + 1) * piece, :].astype(F32)
+        out_ref[aligned(grid_lookup(places[p], z, x), piece), :] = value
+
+
+def last_finish_kernel(table, places, piece, here_ref, _, early_ref, late_ref, *refs):
+    *received, out_ref, total, sem = refs
+    z, x = here_ref[0], here_ref[1]
+    start = grid_lookup(table[-1], z, x)
     last = early_ref.shape[0]
-    count = len(table)
-    for p in range(count):
-        start = grid_lookup(table[p], z, x)
-        place = aligned(grid_lookup(places[p], z, x), piece)
-        if p < count - 1:
-            value = early_ref[aligned(start, piece), :]
-            for ref in first:
-                value = value + ref[p * piece : (p + 1) * piece, :].astype(F32)
-            out_ref[place, :] = value
-            continue
-        other = second[0][...].astype(F32)
-        for ref in second[1:]:
-            other = other + ref[...].astype(F32)
-
-        @pl.when(start == last)
-        def _():
-            out_ref[place, :] = late_ref[...] + other
-
-        @pl.when(start != last)
-        def _():
-            out_ref[place, :] = early_ref[aligned(start, piece), :] + other
+    other = received[0][...].astype(F32)
+    for ref in received[1:]:
+        other = other + ref[...].astype(F32)
+
+    @pl.when(start == last)
+    def _():
+        total[...] = late_ref[...] + other
+
+    @pl.when(start != last)
+    def _():
+        total[...] = early_ref[aligned(start, piece), :] + other
+
+    place = aligned(grid_lookup(places[-1], z, x), piece)
+    copy = pltpu.make_async_copy(total, out_ref.at[place], sem)
+    copy.start()
+    copy.wait()
 
 
 def load_kernel(x_ref, out_ref, sem):
@@ -458,6 +486,7 @@
         return mixed[name][0] if name in mixed else head(raw[name], piece)
 
     gate = whole_own
+    late_raw = []
     for j in range(2, blocks):
         names = sorted(set(source_of[j]))
         choice = [names.index(s) for s in source_of[j]]
@@ -477,9 +506,15 @@
                 if step > 2:
                     value, _ = lax.optimization_barrier((value, gate))
                 parts.append(hop(step, parity, value))
-        early_rows, = rotate(here, choice, [first_rows(n) for n in names], constants)
-        units += [[early_rows], [last_rows(n) for n in names]]
+        late_raw.append((j, choice, [first_rows(n) for n in names]))
+        units += [None, [last_rows(n) for n in names]]
         choices += [alone, choice]
+    for j, choice, values in late_raw[:-1]:
+        turned_piece, = rotate(here, choice, values, constants)
+        units[units.index(None)] = [turned_piece]
+    raw_choice, raw_values = late_raw[-1][1:]
+    units.remove(None)
+    choices.pop(-2)
 
     count = per_owner * splits
     table = [[[0] * layers for _ in range(blocks)] for _ in range(count)]
@@ -498,34 +533,58 @@
             for d, s in enumerate(sent, 1)
         ]
 
-    def scores(kernel, units, choices, inputs, sent_rows, grant):
-        held = sum(u[0].shape[0] for u in units)
-        total, width = train.shape
-        flat = [w for u in units for w in u] + [train] + inputs
+    total, width = train.shape
+
+    def scores(kernel, units, choices, extra, held, sent_rows, scratch, grant):
+        flat = [w for u in units for w in u] + [train] + extra
         sent_shape = jax.ShapeDtypeStruct((sent_rows, total), BF16)
         return call(
             functools.partial(kernel, [len(u) for u in units], choices, table, piece),
             [jax.ShapeDtypeStruct((held, total), F32)] + [sent_shape] * (layers - 1),
             [IN_SMEM] + [IN_VMEM] * len(flat),
-            [pltpu.VMEM((held, width), BF16)],
+            scratch + [pltpu.VMEM((held, width), BF16)],
             (here, *flat),
             flops=2 * held * total * width,
             grant=grant,
         )
 
-    early, *sent = scores(early_kernel, units[:-1], choices[:-1], [], (count - 1) * piece, 16 << 20)
+    early, *sent = scores(
+        lambda shape, choices, table, piece, *refs: early_kernel(
+            shape, choices, table, piece, raw_choice, *refs
+        ),
+        units[:-1],
+        choices[:-1],
+        [*raw_values, *constants],
+        blocks * rows - piece,
+        (count - 1) * piece,
+        turn_scratch(piece, constants),
+        16 << 20,
+    )
     first = shifted(sent)
-    late, *sent = scores(late_kernel, units[-1:], choices[-1:], [early], piece, 12 << 20)
+    late, *sent = scores(
+        late_kernel, units[-1:], choices[-1:], [early], piece, piece, [], 12 << 20
+    )
     second = shifted(sent)
+    out_shape = jax.ShapeDtypeStruct((per_owner * rows, total), F32)
     out = call(
-        functools.partial(finish_kernel, table, places, piece, layers),
-        jax.ShapeDtypeStruct((per_owner * rows, train.shape[0]), F32),
-        [IN_SMEM] + [IN_VMEM] * (2 + 2 * (layers - 1)),
+        functools.partial(first_finish_kernel, table, places, piece),
+        out_shape,
+        [IN_SMEM] + [IN_VMEM] * layers,
         [],
-        (here, early, late, *first, *second),
-        flops=per_owner * rows * train.shape[0],
-        grant=12 << 20,
-    )
+        (here, early, *first),
+        flops=per_owner * rows * total,
+        grant=8 << 20,
+    )
+    in_hbm = pl.BlockSpec(memory_space=pltpu.HBM)
+    out = pl.pallas_call(
+        functools.partial(last_finish_kernel, table, places, piece),
+        out_shape=out_shape,
+        in_specs=[IN_SMEM, in_hbm] + [IN_VMEM] * (1 + layers),
+        out_specs=in_hbm,
+        scratch_shapes=[pltpu.VMEM((piece, total), F32), pltpu.SemaphoreType.DMA],
+        input_output_aliases={1: 0},
+        compiler_params=pltpu.CompilerParams(vmem_limit_bytes=8 << 20),
+    )(here, out, early, late, *second)
     return out[None]
 
 

time: 60.4 us -> 59.5 us (0.985)
  waiting for transfers between devices: 15.4 us -> 14.2 us
    ppermute x2, waiting for transfers between devices: 3.57 us -> 1.58 us  [shifted(): lax.ppermute(s, 'layer', [(o, (o + d) % layers) for o in range(layers)])]
    pallas_call x0 -> x1, Pallas kernels: none -> 1.23 us  [steps(): pl.pallas_call(functools.partial(last_finish_kernel, table, places, piece...]
    ppermute x3, waiting for transfers between devices: 5.36 us -> 6.26 us  [steps(): lax.ppermute(pair, 'blk', [(a, (a + d) % blocks) for a in range(blocks)])]
    ppermute x3, starting transfers between devices: 7.41 us -> 6.51 us  [steps(): lax.ppermute(pair, 'blk', [(a, (a + d) % blocks) for a in range(blocks)])]
    pallas_call x10 -> x9, Pallas kernels: 17.5 us -> 16.8 us  [call(): pl.pallas_call(kernel, out_shape=out_shape, in_specs=in_specs, out_specs=...]
  transfers between devices with their start and end apart: 13 -> 13, of which waited for: 7 -> 6; matrix products, arithmetic and copies ran while one was open for 0% -> 0% of each run, Pallas kernels for 28% -> 30%
where the time goes in v2:
time: 59.5 us; the launch traced here: 59.2 us
  starting transfers between devices  21.3 us (36%)
  Pallas kernels  18.7 us (31%)
  waiting for transfers between devices  14.2 us (24%)
  local copies, waits for them, and re-layouts  4.74 us (8%)
    pallas_call x9, Pallas kernels, call(): pl.pallas_call(kernel, out_shape=out_shape, in_specs=in_specs, out_specs=...  16.8 us
    ppermute x3, starting transfers between devices, steps(): lax.ppermute(pair, 'blk', [(a, (a + d) % blocks) for a in range(blocks)])  6.51 us
    ppermute x3, waiting for transfers between devices, steps(): lax.ppermute(pair, 'blk', [(a, (a + d) % blocks) for a in range(blocks)])  6.26 us
    ppermute x1, starting transfers between devices, steps(): raw[1, 0] = lax.ppermute(own, 'blk', plan[1, 0])  5.91 us
    unnamed x8, local copies, waits for them, and re-layouts  4.74 us
    ppermute x1, waiting for transfers between devices, steps(): raw[1, 0] = lax.ppermute(own, 'blk', plan[1, 0])  3.96 us
    ppermute x4, starting transfers between devices, hop(): return lax.ppermute(value, 'blk', plan[step, parity])  3.94 us
    ppermute x2, starting transfers between devices, shifted(): lax.ppermute(s, 'layer', [(o, (o + d) % layers) for o in range(layers)])  2.93 us
  transfers between devices with their start and end apart: 13, of which 6 were waited for; matrix products, arithmetic and copies ran while one was open for 0% of the time, Pallas kernels for 30%

profile of v2, /device:TPU:0, one launch (start us, length us, event | category | flops | bytes accessed | tf_op | source)
XLA Modules:
  0.0 59.2 jit_solution(2594765388746661823)
XLA Ops:
  0.0 0.7 %collective-permute-start.5 = (bf16[64,4096]{1,0:T(8,128)(2,1)}, bf16[64,4096]{1,0:T(8,128)(2,1)S(1)}, u32[]{:S(2)}, u32[]{:S(2)}) collective-permute-start(bf16[64,4096]{1,0:T(8,128)(2,1)} %bitcast.9), channel_id=1, source_target_pairs={{4,8},{8,4},{5,9},{9,5},{6,10},{10,6},{7,11},{11,7},{20,24},{24,20... | collective-permute-start | bytes 1572872 | tf_op jit(solution)/shard_map/ppermute | solution.py:433
  0.7 5.9 %collective-permute-start.4 = (bf16[64,4096]{1,0:T(8,128)(2,1)}, bf16[64,4096]{1,0:T(8,128)(2,1)S(1)}, u32[]{:S(2)}, u32[]{:S(2)}) collective-permute-start(bf16[64,4096]{1,0:T(8,128)(2,1)} %bitcast.10), channel_id=1, source_target_pairs={{0,4},{4,0},{8,12},{12,8},{1,5},{5,1},{9,13},{13,9},{2,6},{6,2},{1... | collective-permute-start | bytes 1572872 | tf_op jit(solution)/shard_map/ppermute | solution.py:434
  6.6 0.0 copy-start.2
  6.6 0.7 %copy-done.2 = bf16[1,8,128]{2,1,0:T(8,128)(2,1)S(1)} copy-done((bf16[1,8,128]{2,1,0:T(8,128)(2,1)S(1)}, bf16[1,8,128]{2,1,0:T(8,128)(2,1)}, u32[]{:S(2)}) %copy-start.2) | copy-done | bytes 2072
  7.3 0.0 copy-start.3
  7.3 0.7 %copy-done.3 = f32[1,512]{1,0:T(1,128)S(1)} copy-done((f32[1,512]{1,0:T(1,128)S(1)}, f32[1,512]{1,0:T(1,128)}, u32[]{:S(2)}) %copy-start.3) | copy-done | bytes 2072
  8.0 0.0 collective-permute-start
  8.0 0.1 pad_add_fusion.here_ref.refs_0_
  8.0 1.1 %collective-permute-done = f32[12,128]{1,0:T(8,128)S(1)} collective-permute-done((f32[12,128]{1,0:T(8,128)S(1)}, f32[12,128]{1,0:T(8,128)S(1)}, u32[]{:S(2)}, u32[]{:S(2)}) %collective-permute-start) | collective-permute-done | bytes 6176 | tf_op jit(solution)/shard_map/ppermute | solution.py:449
  9.1 0.0 copy-start
  9.2 3.4 %copy-done = bf16[1,1024,4096]{2,1,0:T(8,128)(2,1)S(1)} copy-done((bf16[1,1024,4096]{2,1,0:T(8,128)(2,1)S(1)}, bf16[1,1024,4096]{2,1,0:T(8,128)(2,1)}, u32[]{:S(2)}) %copy-start) | copy-done | bytes 8388632
  12.5 0.0 copy-start.1
  12.5 0.6 %shard_map.50.refs_4_.refs_2_ = bf16[1024,4096]{1,0:T(8,128)(2,1)S(1)} custom-call(bf16[1024,4096]{1,0:T(8,128)(2,1)S(1)} %bitcast.8), custom_call_target="tpu_custom_call" | custom-call | bytes 16777216 | tf_op jit(solution)/shard_map/pallas_call | solution.py:403
  13.2 0.0 collective-permute-done.5.refs_0_
  13.2 1.3 %collective-permute-start.6 = (bf16[64,4096]{1,0:T(8,128)(2,1)S(1)}, bf16[64,4096]{1,0:T(8,128)(2,1)S(1)}, u32[]{:S(2)}, u32[]{:S(2)}) collective-permute-start(bf16[64,4096]{1,0:T(8,128)(2,1)S(1)} %collective-permute-done.5.refs_0_), channel_id=1, source_target_pairs={{4,0},{8,12},{5,1},{9,13},{6,2},{10,14},{7,3},{11,15},{20,16},{24,... | collective-permute-start | bytes 1572872 | tf_op jit(solution)/shard_map/ppermute | solution.py:457
  14.5 4.0 %collective-permute-done.4.refs_0_.rows_ref = bf16[64,4096]{1,0:T(8,128)(2,1)S(1)} collective-permute-done((bf16[64,4096]{1,0:T(8,128)(2,1)}, bf16[64,4096]{1,0:T(8,128)(2,1)S(1)}, u32[]{:S(2)}, u32[]{:S(2)}) %collective-permute-start.4) | collective-permute-done | bytes 524320 | tf_op jit(solution)/shard_map/ppermute | solution.py:434
  18.5 0.7 %collective-permute-start.7 = (bf16[32,4096]{1,0:T(8,128)(2,1)S(1)}, bf16[32,4096]{1,0:T(8,128)(2,1)S(1)}, u32[]{:S(2)}, u32[]{:S(2)}) collective-permute-start(bf16[32,4096]{1,0:T(8,128)(2,1)S(1)} %shard_map.52), channel_id=1, source_target_pairs={{4,8},{8,4},{5,9},{9,5},{6,10},{10,6},{7,11},{11,7},{20,24},{24,20... | collective-permute-start | bytes 786440 | tf_op jit(solution)/shard_map/ppermute | solution.py:465
  19.2 1.4 %collective-permute-start.3 = (f32[24,128]{1,0:T(8,128)S(1)}, f32[24,128]{1,0:T(8,128)S(1)}, u32[]{:S(2)}, u32[]{:S(2)}) collective-permute-start(f32[24,128]{1,0:T(8,128)S(1)} %pad_maximum_fusion.refs_0_), channel_id=1, source_target_pairs={{0,12},{4,0},{8,4},{12,8},{1,13},{5,1},{9,5},{13,9},{2,14},{6,2},{... | collective-permute-start | bytes 36872 | tf_op jit(solution)/shard_map/ppermute | solution.py:453
  20.6 4.6 %collective-permute-start.2 = (f32[24,128]{1,0:T(8,128)S(1)}, f32[24,128]{1,0:T(8,128)S(1)}, u32[]{:S(2)}, u32[]{:S(2)}) collective-permute-start(f32[24,128]{1,0:T(8,128)S(1)} %pad_maximum_fusion.refs_0_), channel_id=1, source_target_pairs={{0,8},{4,12},{8,0},{12,4},{1,9},{5,13},{9,1},{13,5},{2,10},{6,14},... | collective-permute-start | bytes 36872 | tf_op jit(solution)/shard_map/ppermute | solution.py:453
  25.2 0.5 collective-permute-start.1
  25.7 6.3 %collective-permute-done.3.refs_3_ = f32[24,128]{1,0:T(8,128)S(1)} collective-permute-done((f32[24,128]{1,0:T(8,128)S(1)}, f32[24,128]{1,0:T(8,128)S(1)}, u32[]{:S(2)}, u32[]{:S(2)}) %collective-permute-start.3) | collective-permute-done | bytes 12320 | tf_op jit(solution)/shard_map/ppermute | solution.py:453
  31.9 0.0 collective-permute-done.2.refs_2_
  31.9 0.0 collective-permute-done.1.refs_1_
  31.9 1.5 %shard_map.47 = (bf16[512,512]{1,0:T(8,128)(2,1)S(1)}, bf16[512,512]{1,0:T(8,128)(2,1)S(1)}, bf16[512,512]{1,0:T(8,128)(2,1)S(1)}, bf16[512,512]{1,0:T(8,128)(2,1)S(1)}, f32[512,256]{1,0:T(8,128)S(1)}) custom-call(s32[3]{0:T(128)S(1)} %pad_add_fusion.here_ref.refs_0_, f32[24,128]{1,0:T(8,128)S(1)} %pad_maximum_fusion.refs_0_, ...), custom_call_target="tpu_custom_call" | custom-call | flops 67108864 | bytes 2670604 | tf_op jit(solution)/shard_map/pallas_call | solution.py:24
  33.5 2.2 %shard_map.49 = (bf16[64,4096]{1,0:T(8,128)(2,1)S(1)}, bf16[32,4096]{1,0:T(8,128)(2,1)S(1)}) custom-call(s32[3]{0:T(128)S(1)} %pad_add_fusion.here_ref.refs_0_, bf16[64,4096]{1,0:T(8,128)(2,1)S(1)} %collective-permute-done.4.refs_0_.rows_ref, bf16[512,512]{1,0:T(8,128)(2,1)S(1)} %get-tuple-element.22.refs_1_.refs_2_.refs_7_, ...), custom_call_target="tpu_custom_call" | custom-call | flops 536870912 | bytes 3932172 | tf_op jit(solution)/shard_map/pallas_call | solution.py:24
  35.6 0.7 %collective-permute-start.10 = (bf16[32,4096]{1,0:T(8,128)(2,1)S(1)}, bf16[32,4096]{1,0:T(8,128)(2,1)S(1)}, u32[]{:S(2)}, u32[]{:S(2)}) collective-permute-start(bf16[32,4096]{1,0:T(8,128)(2,1)S(1)} %get-tuple-element.33), channel_id=1, source_target_pairs={{4,8},{8,4},{5,9},{9,5},{6,10},{10,6},{7,11},{11,7},{20,24},{24,20... | collective-permute-start | bytes 786440 | tf_op jit(solution)/shard_map/ppermute | solution.py:465
  36.3 0.0 collective-permute-done.7.refs_5_
  36.3 1.3 %collective-permute-start.8 = (bf16[32,4096]{1,0:T(8,128)(2,1)S(1)}, bf16[32,4096]{1,0:T(8,128)(2,1)S(1)}, u32[]{:S(2)}, u32[]{:S(2)}) collective-permute-start(bf16[32,4096]{1,0:T(8,128)(2,1)S(1)} %collective-permute-done.7.refs_5_), channel_id=1, source_target_pairs={{4,0},{8,12},{5,1},{9,13},{6,2},{10,14},{7,3},{11,15},{20,16},{24,... | collective-permute-start | bytes 786440 | tf_op jit(solution)/shard_map/ppermute | solution.py:465
  37.6 0.0 copy-done.1
  37.6 2.2 %shard_map.48.refs_1_ = bf16[64,4096]{1,0:T(8,128)(2,1)S(1)} custom-call(s32[3]{0:T(128)S(1)} %pad_add_fusion.here_ref.refs_0_, bf16[64,4096]{1,0:T(8,128)(2,1)S(1)} %bitcast.11, bf16[512,512]{1,0:T(8,128)(2,1)S(1)} %get-tuple-element.22.refs_1_.refs_2_.refs_7_, bf16[512,512]{1,0:T(8,128)(2,1)S(1)} %get-tuple-element.23.refs_2_.refs_3_.refs_8_, ...), custom_call_target="tpu_custom_call" | custom-call | flops 536870912 | bytes 3670028 | tf_op jit(solution)/shard_map/pallas_call | solution.py:24
  39.8 0.0 collective-permute-done.6.refs_1_
  39.8 2.3 %shard_map.51.refs_3_ = bf16[64,4096]{1,0:T(8,128)(2,1)S(1)} custom-call(s32[3]{0:T(128)S(1)} %pad_add_fusion.here_ref.refs_0_, bf16[64,4096]{1,0:T(8,128)(2,1)S(1)} %collective-permute-done.5.refs_0_, bf16[64,4096]{1,0:T(8,128)(2,1)S(1)} %collective-permute-done.6.refs_1_, bf16[512,512]{1,0:T(8,128)(2,1)S(1)} %get-tuple-element.22.refs_1_.refs_2_.refs_7_, ...), custom_call_target="tpu_custom_call" | custom-call | flops 536870912 | bytes 4194316 | tf_op jit(solution)/shard_map/pallas_call | solution.py:24
  42.1 0.0 collective-permute-done.10.refs_0_
  42.1 1.3 %collective-permute-start.11 = (bf16[32,4096]{1,0:T(8,128)(2,1)S(1)}, bf16[32,4096]{1,0:T(8,128)(2,1)S(1)}, u32[]{:S(2)}, u32[]{:S(2)}) collective-permute-start(bf16[32,4096]{1,0:T(8,128)(2,1)S(1)} %collective-permute-done.10.refs_0_), channel_id=1, source_target_pairs={{4,0},{8,12},{5,1},{9,13},{6,2},{10,14},{7,3},{11,15},{20,16},{24,... | collective-permute-start | bytes 786440 | tf_op jit(solution)/shard_map/ppermute | solution.py:465
  43.4 1.3 %collective-permute-done.8.refs_6_ = bf16[32,4096]{1,0:T(8,128)(2,1)S(1)} collective-permute-done((bf16[32,4096]{1,0:T(8,128)(2,1)S(1)}, bf16[32,4096]{1,0:T(8,128)(2,1)S(1)}, u32[]{:S(2)}, u32[]{:S(2)}) %collective-permute-start.8) | collective-permute-done | bytes 262176 | tf_op jit(solution)/shard_map/ppermute | solution.py:465
  44.7 4.4 %shard_map.53 = (f32[224,1024]{1,0:T(8,128)S(1)}, bf16[96,1024]{1,0:T(8,128)(2,1)S(1)}) custom-call(s32[3]{0:T(128)S(1)} %pad_add_fusion.here_ref.refs_0_, bf16[64,4096]{1,0:T(8,128)(2,1)S(1)} %shard_map.48.refs_1_, bf16[64,4096]{1,0:T(8,128)(2,1)S(1)} %get-tuple-element.27.refs_2_, bf16[64,4096]{1,0:T(8,128)(2,1)S(1)} %shard_map.51.refs_3_, ...), custom_call_target="tpu_custom_call" | custom-call | flops 1879048192 | bytes 14221324 | tf_op jit(solution)/shard_map/pallas_call | solution.py:24
  49.1 1.6 %collective-permute-start.9 = (bf16[96,1024]{1,0:T(8,128)(2,1)S(1)}, bf16[96,1024]{1,0:T(8,128)(2,1)S(1)}, u32[]{:S(2)}, u32[]{:S(2)}) collective-permute-start(bf16[96,1024]{1,0:T(8,128)(2,1)S(1)} %get-tuple-element.32), channel_id=1, source_target_pairs={{0,2},{2,0},{1,3},{3,1},{4,6},{6,4},{5,7},{7,5},{8,10},{10,8},{9,1... | collective-permute-start | bytes 589832 | tf_op jit(solution)/shard_map/ppermute | solution.py:532
  50.7 0.0 collective-permute-done.11.refs_1_
  50.7 2.9 %shard_map.55 = (f32[32,1024]{1,0:T(8,128)S(1)}, bf16[32,1024]{1,0:T(8,128)(2,1)S(1)}) custom-call(s32[3]{0:T(128)S(1)} %pad_add_fusion.here_ref.refs_0_, bf16[32,4096]{1,0:T(8,128)(2,1)S(1)} %collective-permute-done.10.refs_0_, bf16[32,4096]{1,0:T(8,128)(2,1)S(1)} %collective-permute-done.11.refs_1_, bf16[1024,4096]{1,0:T(8,128)(2,1)S(1)} %shard_map.50.refs_4_.refs_2_, ...), custom_call_target="tpu_custom_call" | custom-call | flops 268435456 | bytes 10027020 | tf_op jit(solution)/shard_map/pallas_call | solution.py:24
  53.6 1.4 %collective-permute-start.12 = (bf16[32,1024]{1,0:T(8,128)(2,1)S(1)}, bf16[32,1024]{1,0:T(8,128)(2,1)S(1)}, u32[]{:S(2)}, u32[]{:S(2)}) collective-permute-start(bf16[32,1024]{1,0:T(8,128)(2,1)S(1)} %get-tuple-element.36), channel_id=1, source_target_pairs={{0,2},{2,0},{1,3},{3,1},{4,6},{6,4},{5,7},{7,5},{8,10},{10,8},{9,1... | collective-permute-start | bytes 196616 | tf_op jit(solution)/shard_map/ppermute | solution.py:532
  55.0 0.6 collective-permute-done.9.refs_0_
  55.6 1.4 %shard_map.54._ = f32[128,1024]{1,0:T(8,128)} custom-call(s32[3]{0:T(128)S(1)} %pad_add_fusion.here_ref.refs_0_, f32[224,1024]{1,0:T(8,128)S(1)} %get-tuple-element.31.early_ref.refs_3_, bf16[96,1024]{1,0:T(8,128)(2,1)S(1)} %collective-permute-done.9.refs_0_), custom_call_target="tpu_custom_call" | custom-call | flops 131072 | bytes 1638412 | tf_op jit(solution)/shard_map/pallas_call | solution.py:24
  56.9 1.0 %collective-permute-done.12.refs_0_ = bf16[32,1024]{1,0:T(8,128)(2,1)S(1)} collective-permute-done((bf16[32,1024]{1,0:T(8,128)(2,1)S(1)}, bf16[32,1024]{1,0:T(8,128)(2,1)S(1)}, u32[]{:S(2)}, u32[]{:S(2)}) %collective-permute-start.12) | collective-permute-done | bytes 65568 | tf_op jit(solution)/shard_map/ppermute | solution.py:532
  58.0 1.2 %shard_map.56 = f32[128,1024]{1,0:T(8,128)} custom-call(s32[3]{0:T(128)S(1)} %pad_add_fusion.here_ref.refs_0_, f32[128,1024]{1,0:T(8,128)} %shard_map.54._, f32[224,1024]{1,0:T(8,128)S(1)} %get-tuple-element.31.early_ref.refs_3_, f32[32,1024]{1,0:T(8,128)S(1)} %get-tuple-element.35.late_ref, ...), custom_call_target="tpu_custom_call", output_to_operand_aliasing={{}: (1, {})} | custom-call | tf_op jit(solution)/shard_map/pallas_call | solution.py:579
  (3 shorter events, 0.0 us)
Async XLA Ops:
  0.0 13.2 %collective-permute-start.5 = (bf16[64,4096]{1,0:T(8,128)(2,1)}, bf16[64,4096]{1,0:T(8,128)(2,1)S(1)}, u32[]{:S(2)}, u32[]{:S(2)}) collective-permute-start(bf16[64,4096]{1,0:T(8,128)(2,1)} %bitcast.9), channel_id=1, source_target_pairs={{4,8},{8,4},{5,9},{9,5},{6,10},{10,6},{7,11},{11,7},{20,24},{24,20... | collective-permute-start | bytes 1572872 | tf_op jit(solution)/shard_map/ppermute | solution.py:433
  0.7 17.8 %collective-permute-start.4 = (bf16[64,4096]{1,0:T(8,128)(2,1)}, bf16[64,4096]{1,0:T(8,128)(2,1)S(1)}, u32[]{:S(2)}, u32[]{:S(2)}) collective-permute-start(bf16[64,4096]{1,0:T(8,128)(2,1)} %bitcast.10), channel_id=1, source_target_pairs={{0,4},{4,0},{8,12},{12,8},{1,5},{5,1},{9,13},{13,9},{2,6},{6,2},{1... | collective-permute-start | bytes 1572872 | tf_op jit(solution)/shard_map/ppermute | solution.py:434
  6.6 0.7 %copy-start.2 = (bf16[1,8,128]{2,1,0:T(8,128)(2,1)S(1)}, bf16[1,8,128]{2,1,0:T(8,128)(2,1)}, u32[]{:S(2)}) copy-start(bf16[1,8,128]{2,1,0:T(8,128)(2,1)} %param.6) | copy-start | bytes 6148
  7.3 0.7 %copy-start.3 = (f32[1,512]{1,0:T(1,128)S(1)}, f32[1,512]{1,0:T(1,128)}, u32[]{:S(2)}) copy-start(f32[1,512]{1,0:T(1,128)} %param.7) | copy-start | bytes 6148
  8.0 1.2 %collective-permute-start = (f32[12,128]{1,0:T(8,128)S(1)}, f32[12,128]{1,0:T(8,128)S(1)}, u32[]{:S(2)}, u32[]{:S(2)}) collective-permute-start(f32[12,128]{1,0:T(8,128)S(1)} %shard_map.46), channel_id=1, source_target_pairs={{0,1},{1,0},{2,3},{3,2},{4,5},{5,4},{6,7},{7,6},{8,9},{9,8},{10,11... | collective-permute-start | bytes 18440 | tf_op jit(solution)/shard_map/ppermute | solution.py:449
  9.1 3.4 %copy-start = (bf16[1,1024,4096]{2,1,0:T(8,128)(2,1)S(1)}, bf16[1,1024,4096]{2,1,0:T(8,128)(2,1)}, u32[]{:S(2)}) copy-start(bf16[1,1024,4096]{2,1,0:T(8,128)(2,1)} %param.4) | copy-start | bytes 25165828
  12.5 25.1 %copy-start.1 = (bf16[1,1,64,4096]{3,2,1,0:T(8,128)(2,1)S(1)}, bf16[1,1,64,4096]{3,2,1,0:T(8,128)(2,1)}, u32[]{:S(2)}) copy-start(bf16[1,1,64,4096]{3,2,1,0:T(8,128)(2,1)} %param.5) | copy-start | bytes 1572868
  13.2 26.6 %collective-permute-start.6 = (bf16[64,4096]{1,0:T(8,128)(2,1)S(1)}, bf16[64,4096]{1,0:T(8,128)(2,1)S(1)}, u32[]{:S(2)}, u32[]{:S(2)}) collective-permute-start(bf16[64,4096]{1,0:T(8,128)(2,1)S(1)} %collective-permute-done.5.refs_0_), channel_id=1, source_target_pairs={{4,0},{8,12},{5,1},{9,13},{6,2},{10,14},{7,3},{11,15},{20,16},{24,... | collective-permute-start | bytes 1572872 | tf_op jit(solution)/shard_map/ppermute | solution.py:457
  18.5 17.8 %collective-permute-start.7 = (bf16[32,4096]{1,0:T(8,128)(2,1)S(1)}, bf16[32,4096]{1,0:T(8,128)(2,1)S(1)}, u32[]{:S(2)}, u32[]{:S(2)}) collective-permute-start(bf16[32,4096]{1,0:T(8,128)(2,1)S(1)} %shard_map.52), channel_id=1, source_target_pairs={{4,8},{8,4},{5,9},{9,5},{6,10},{10,6},{7,11},{11,7},{20,24},{24,20... | collective-permute-start | bytes 786440 | tf_op jit(solution)/shard_map/ppermute | solution.py:465
  19.2 12.8 %collective-permute-start.3 = (f32[24,128]{1,0:T(8,128)S(1)}, f32[24,128]{1,0:T(8,128)S(1)}, u32[]{:S(2)}, u32[]{:S(2)}) collective-permute-start(f32[24,128]{1,0:T(8,128)S(1)} %pad_maximum_fusion.refs_0_), channel_id=1, source_target_pairs={{0,12},{4,0},{8,4},{12,8},{1,13},{5,1},{9,5},{13,9},{2,14},{6,2},{... | collective-permute-start | bytes 36872 | tf_op jit(solution)/shard_map/ppermute | solution.py:453
  20.6 11.4 %collective-permute-start.2 = (f32[24,128]{1,0:T(8,128)S(1)}, f32[24,128]{1,0:T(8,128)S(1)}, u32[]{:S(2)}, u32[]{:S(2)}) collective-permute-start(f32[24,128]{1,0:T(8,128)S(1)} %pad_maximum_fusion.refs_0_), channel_id=1, source_target_pairs={{0,8},{4,12},{8,0},{12,4},{1,9},{5,13},{9,1},{13,5},{2,10},{6,14},... | collective-permute-start | bytes 36872 | tf_op jit(solution)/shard_map/ppermute | solution.py:453
  25.2 6.8 %collective-permute-start.1 = (f32[24,128]{1,0:T(8,128)S(1)}, f32[24,128]{1,0:T(8,128)S(1)}, u32[]{:S(2)}, u32[]{:S(2)}) collective-permute-start(f32[24,128]{1,0:T(8,128)S(1)} %pad_maximum_fusion.refs_0_), channel_id=1, source_target_pairs={{0,4},{4,8},{8,12},{12,0},{1,5},{5,9},{9,13},{13,1},{2,6},{6,10},{... | collective-permute-start | bytes 36872 | tf_op jit(solution)/shard_map/ppermute | solution.py:453
  35.6 6.4 %collective-permute-start.10 = (bf16[32,4096]{1,0:T(8,128)(2,1)S(1)}, bf16[32,4096]{1,0:T(8,128)(2,1)S(1)}, u32[]{:S(2)}, u32[]{:S(2)}) collective-permute-start(bf16[32,4096]{1,0:T(8,128)(2,1)S(1)} %get-tuple-element.33), channel_id=1, source_target_pairs={{4,8},{8,4},{5,9},{9,5},{6,10},{10,6},{7,11},{11,7},{20,24},{24,20... | collective-permute-start | bytes 786440 | tf_op jit(solution)/shard_map/ppermute | solution.py:465
  36.3 8.4 %collective-permute-start.8 = (bf16[32,4096]{1,0:T(8,128)(2,1)S(1)}, bf16[32,4096]{1,0:T(8,128)(2,1)S(1)}, u32[]{:S(2)}, u32[]{:S(2)}) collective-permute-start(bf16[32,4096]{1,0:T(8,128)(2,1)S(1)} %collective-permute-done.7.refs_5_), channel_id=1, source_target_pairs={{4,0},{8,12},{5,1},{9,13},{6,2},{10,14},{7,3},{11,15},{20,16},{24,... | collective-permute-start | bytes 786440 | tf_op jit(solution)/shard_map/ppermute | solution.py:465
  42.1 8.6 %collective-permute-start.11 = (bf16[32,4096]{1,0:T(8,128)(2,1)S(1)}, bf16[32,4096]{1,0:T(8,128)(2,1)S(1)}, u32[]{:S(2)}, u32[]{:S(2)}) collective-permute-start(bf16[32,4096]{1,0:T(8,128)(2,1)S(1)} %collective-permute-done.10.refs_0_), channel_id=1, source_target_pairs={{4,0},{8,12},{5,1},{9,13},{6,2},{10,14},{7,3},{11,15},{20,16},{24,... | collective-permute-start | bytes 786440 | tf_op jit(solution)/shard_map/ppermute | solution.py:465
  49.1 6.4 %collective-permute-start.9 = (bf16[96,1024]{1,0:T(8,128)(2,1)S(1)}, bf16[96,1024]{1,0:T(8,128)(2,1)S(1)}, u32[]{:S(2)}, u32[]{:S(2)}) collective-permute-start(bf16[96,1024]{1,0:T(8,128)(2,1)S(1)} %get-tuple-element.32), channel_id=1, source_target_pairs={{0,2},{2,0},{1,3},{3,1},{4,6},{6,4},{5,7},{7,5},{8,10},{10,8},{9,1... | collective-permute-start | bytes 589832 | tf_op jit(solution)/shard_map/ppermute | solution.py:532
  53.6 4.3 %collective-permute-start.12 = (bf16[32,1024]{1,0:T(8,128)(2,1)S(1)}, bf16[32,1024]{1,0:T(8,128)(2,1)S(1)}, u32[]{:S(2)}, u32[]{:S(2)}) collective-permute-start(bf16[32,1024]{1,0:T(8,128)(2,1)S(1)} %get-tuple-element.36), channel_id=1, source_target_pairs={{0,2},{2,0},{1,3},{3,1},{4,6},{6,4},{5,7},{7,5},{8,10},{10,8},{9,1... | collective-permute-start | bytes 196616 | tf_op jit(solution)/shard_map/ppermute | solution.py:532

commit v3 on v2

--- a/solution.py
+++ b/solution.py
@@ -11,7 +11,14 @@
 HALF = 8
 BF16, F32 = jnp.bfloat16, jnp.float32
 IN_VMEM = pl.BlockSpec(memory_space=pltpu.VMEM)
-IN_SMEM = pl.BlockSpec(memory_space=pltpu.SMEM)
+
+
+class Place:
+    def __getitem__(self, axis):
+        return lax.axis_index(("blk", "layer", "rep")[axis])
+
+
+PLACE = Place()
 
 
 def dot(a, b):
@@ -128,12 +135,12 @@
             inv_ref[i * HALF : (i + 1) * HALF, h * 2 * size : (h + 1) * 2 * size] = row
 
 
-def rotation_constants(parts, here, reps, base_rows, eigen_rows, size, fold):
+def rotation_constants(parts, reps, base_rows, eigen_rows, size, fold):
     count = len(parts)
     wide, tall = 2 * size * fold, HALF * size
     shard = count * reps
     return call(
-        functools.partial(prep_kernel, (count, reps, base_rows, eigen_rows, fold)),
+        functools.partial(prep_kernel, (count, reps, base_rows, eigen_rows, fold), PLACE),
         [
             jax.ShapeDtypeStruct((wide, wide), BF16),
             jax.ShapeDtypeStruct((tall, tall), BF16),
@@ -141,7 +148,7 @@
             jax.ShapeDtypeStruct((wide, wide), BF16),
             jax.ShapeDtypeStruct((tall, size * fold), F32),
         ],
-        [IN_SMEM] + [IN_VMEM] * count,
+        [IN_VMEM] * count,
         [
             pltpu.VMEM((shard, base_rows, 2 * size), F32),
             pltpu.VMEM((shard, eigen_rows, 2 * size), F32),
@@ -149,7 +156,7 @@
             pltpu.VMEM((size // 2, 2 * size), F32),
             pltpu.VMEM((size, 2 * size), F32),
         ],
-        (here, *parts),
+        tuple(parts),
         flops=2 * wide * wide * 2 * size,
         grant=12 << 20,
     )
@@ -250,7 +257,7 @@
     ]
 
 
-def rotate(here, choice, inputs, constants, split=0):
+def rotate(choice, inputs, constants, split=0):
     rows, width = inputs[0].shape
     fold = rows // TILE
     size = constants[1].shape[0] // HALF
@@ -258,11 +265,11 @@
     if split:
         shapes.append(jax.ShapeDtypeStruct((rows - split, width), BF16))
     return call(
-        functools.partial(rotate_kernel, len(inputs), choice, split),
+        functools.partial(rotate_kernel, len(inputs), choice, split, PLACE),
         shapes,
-        [IN_SMEM] + [IN_VMEM] * (len(inputs) + 5),
+        [IN_VMEM] * (len(inputs) + 5),
         turn_scratch(rows, constants),
-        (here, *inputs, *constants),
+        (*inputs, *constants),
         flops=8 * rows * width * size * fold,
         grant=12 << 20,
     )
@@ -415,7 +422,6 @@
 
 def steps(train_grads, queries, bases, eigenvalues):
     blocks, layers, reps = lax.axis_size("blk"), lax.axis_size("layer"), lax.axis_size("rep")
-    z, x, rep = lax.axis_index("blk"), lax.axis_index("layer"), lax.axis_index("rep")
     train = train_grads[0]
     own = queries[0, 0]
     base_rows, lanes = bases.shape[1:]
@@ -425,7 +431,6 @@
     per_owner = blocks // layers
 
     plan, arrivals = line_plan(blocks)
-    here = jnp.stack([z, x, rep]).astype(jnp.int32)
     splits = 2
     piece = rows // splits
 
@@ -451,12 +456,12 @@
     parts = [pair]
     for d in range(1, blocks):
         parts.append(lax.ppermute(pair, "blk", [(a, (a + d) % blocks) for a in range(blocks)]))
-    train, here, _ = lax.optimization_barrier((train, here, pair))
+    train, _ = lax.optimization_barrier((train, pair))
     train = resident(train)
     raw[1, 1], train = lax.optimization_barrier((raw[1, 1], train))
     raw[2, 0] = lax.ppermute(raw[1, 1], "blk", plan[2, 0])
 
-    constants = rotation_constants(parts, here, reps, base_rows, eigen_rows, size, fold)
+    constants = rotation_constants(parts, reps, base_rows, eigen_rows, size, fold)
     alone = [0] * blocks
     block_of = [list(range(blocks))] + [[a[j][2] for a in arrivals] for j in range(blocks - 1)]
     source_of = [None] + [[a[j][:2] for a in arrivals] for j in range(blocks - 1)]
@@ -465,12 +470,12 @@
         return lax.ppermute(value, "blk", plan[step, parity])
 
     mixed[2, 1] = [hop(2, 1, head(raw[1, 0], piece))] if (2, 1) in plan else []
-    whole_first, last = rotate(here, alone, [raw[1, 0]], constants, piece)
+    whole_first, last = rotate(alone, [raw[1, 0]], constants, piece)
     if mixed[2, 1]:
         mixed[2, 1].append(hop(2, 1, last))
         if (3, 0) in plan:
             mixed[3, 0] = [hop(3, 0, mixed[2, 1][0])]
-    whole_own, = rotate(here, alone, [own], constants)
+    whole_own, = rotate(alone, [own], constants)
     units, choices = [[whole_own], [whole_first]], [alone, alone]
 
     turned_last = {}
@@ -479,7 +484,7 @@
         if name in mixed:
             return mixed[name][1]
         if name not in turned_last:
-            turned_last[name] = rotate(here, alone, [raw[name]], constants, piece)[1]
+            turned_last[name] = rotate(alone, [raw[name]], constants, piece)[1]
         return turned_last[name]
 
     def first_rows(name):
@@ -491,7 +496,7 @@
         names = sorted(set(source_of[j]))
         choice = [names.index(s) for s in source_of[j]]
         if all(n in raw for n in names):
-            whole, = rotate(here, choice, [raw[n] for n in names], constants)
+            whole, = rotate(choice, [raw[n] for n in names], constants)
             units.append([whole])
             choices.append(choice if len(units[-1]) > 1 else alone)
             gate = whole
@@ -510,7 +515,7 @@
         units += [None, [last_rows(n) for n in names]]
         choices += [alone, choice]
     for j, choice, values in late_raw[:-1]:
-        turned_piece, = rotate(here, choice, values, constants)
+        turned_piece, = rotate(choice, values, constants)
         units[units.index(None)] = [turned_piece]
     raw_choice, raw_values = late_raw[-1][1:]
     units.remove(None)
@@ -539,11 +544,11 @@
         flat = [w for u in units for w in u] + [train] + extra
         sent_shape = jax.ShapeDtypeStruct((sent_rows, total), BF16)
         return call(
-            functools.partial(kernel, [len(u) for u in units], choices, table, piece),
+            functools.partial(kernel, [len(u) for u in units], choices, table, piece, PLACE),
             [jax.ShapeDtypeStruct((held, total), F32)] + [sent_shape] * (layers - 1),
-            [IN_SMEM] + [IN_VMEM] * len(flat),
+            [IN_VMEM] * len(flat),
             scratch + [pltpu.VMEM((held, width), BF16)],
-            (here, *flat),
+            tuple(flat),
             flops=2 * held * total * width,
             grant=grant,
         )
@@ -567,24 +572,24 @@
     second = shifted(sent)
     out_shape = jax.ShapeDtypeStruct((per_owner * rows, total), F32)
     out = call(
-        functools.partial(first_finish_kernel, table, places, piece),
+        functools.partial(first_finish_kernel, table, places, piece, PLACE),
         out_shape,
-        [IN_SMEM] + [IN_VMEM] * layers,
+        [IN_VMEM] * layers,
         [],
-        (here, early, *first),
+        (early, *first),
         flops=per_owner * rows * total,
         grant=8 << 20,
     )
     in_hbm = pl.BlockSpec(memory_space=pltpu.HBM)
     out = pl.pallas_call(
-        functools.partial(last_finish_kernel, table, places, piece),
+        functools.partial(last_finish_kernel, table, places, piece, PLACE),
         out_shape=out_shape,
-        in_specs=[IN_SMEM, in_hbm] + [IN_VMEM] * (1 + layers),
+        in_specs=[in_hbm] + [IN_VMEM] * (1 + layers),
         out_specs=in_hbm,
         scratch_shapes=[pltpu.VMEM((piece, total), F32), pltpu.SemaphoreType.DMA],
-        input_output_aliases={1: 0},
+        input_output_aliases={0: 0},
         compiler_params=pltpu.CompilerParams(vmem_limit_bytes=8 << 20),
-    )(here, out, early, late, *second)
+    )(out, early, late, *second)
     return out[None]
 
 

time: 59.5 us -> 57.6 us (0.968)
  Pallas kernels: 18.7 us -> 14.3 us
  waiting for transfers between devices: 14.2 us -> 17.4 us
  starting transfers between devices: 21.3 us -> 20.7 us
    pallas_call x9, Pallas kernels: 16.8 us -> 13 us  [call(): pl.pallas_call(kernel, out_shape=out_shape, in_specs=in_specs, out_specs=...]
    ppermute x4, waiting for transfers between devices: 1.32 us -> 3.38 us  [hop(): return lax.ppermute(value, 'blk', plan[step, parity])]
    ppermute x2, waiting for transfers between devices: 1.58 us -> 2.65 us  [shifted(): lax.ppermute(s, 'layer', [(o, (o + d) % layers) for o in range(layers)])]
  transfers between devices with their start and end apart: 13 -> 13, of which waited for: 6 -> 6; matrix products, arithmetic and copies ran while one was open for 0% -> 0% of each run, Pallas kernels for 30% -> 24%
where the time goes in v3:
time: 57.6 us; the launch traced here: 57.3 us
  starting transfers between devices  20.7 us (36%)
  waiting for transfers between devices  17.4 us (30%)
  Pallas kernels  14.3 us (25%)
  local copies, waits for them, and re-layouts  4.74 us (8%)
    pallas_call x9, Pallas kernels, call(): pl.pallas_call(kernel, out_shape=out_shape, in_specs=in_specs, out_specs=...  13 us
    ppermute x3, starting transfers between devices, steps(): lax.ppermute(pair, 'blk', [(a, (a + d) % blocks) for a in range(blocks)])  6.51 us
    ppermute x3, waiting for transfers between devices, steps(): lax.ppermute(pair, 'blk', [(a, (a + d) % blocks) for a in range(blocks)])  6.26 us
    ppermute x1, starting transfers between devices, steps(): raw[1, 0] = lax.ppermute(own, 'blk', plan[1, 0])  5.91 us
    unnamed x8, local copies, waits for them, and re-layouts  4.74 us
    ppermute x1, waiting for transfers between devices, steps(): raw[1, 0] = lax.ppermute(own, 'blk', plan[1, 0])  3.96 us
    ppermute x4, starting transfers between devices, hop(): return lax.ppermute(value, 'blk', plan[step, parity])  3.94 us
    ppermute x4, waiting for transfers between devices, hop(): return lax.ppermute(value, 'blk', plan[step, parity])  3.38 us
  transfers between devices with their start and end apart: 13, of which 6 were waited for; matrix products, arithmetic and copies ran while one was open for 0% of the time, Pallas kernels for 24%

profile of v3, /device:TPU:0, one launch (start us, length us, event | category | flops | bytes accessed | tf_op | source)
XLA Modules:
  0.0 57.3 jit_solution(491654191793153890)
XLA Ops:
  0.0 0.7 %collective-permute-start.5 = (bf16[64,4096]{1,0:T(8,128)(2,1)}, bf16[64,4096]{1,0:T(8,128)(2,1)S(1)}, u32[]{:S(2)}, u32[]{:S(2)}) collective-permute-start(bf16[64,4096]{1,0:T(8,128)(2,1)} %bitcast.6), channel_id=1, source_target_pairs={{4,8},{8,4},{5,9},{9,5},{6,10},{10,6},{7,11},{11,7},{20,24},{24,20... | collective-permute-start | bytes 1572872 | tf_op jit(solution)/shard_map/ppermute | solution.py:438
  0.7 5.9 %collective-permute-start.4 = (bf16[64,4096]{1,0:T(8,128)(2,1)}, bf16[64,4096]{1,0:T(8,128)(2,1)S(1)}, u32[]{:S(2)}, u32[]{:S(2)}) collective-permute-start(bf16[64,4096]{1,0:T(8,128)(2,1)} %bitcast.7), channel_id=1, source_target_pairs={{0,4},{4,0},{8,12},{12,8},{1,5},{5,1},{9,13},{13,9},{2,6},{6,2},{1... | collective-permute-start | bytes 1572872 | tf_op jit(solution)/shard_map/ppermute | solution.py:439
  6.6 0.0 copy-start.2
  6.6 0.7 %copy-done.2 = bf16[1,8,128]{2,1,0:T(8,128)(2,1)S(1)} copy-done((bf16[1,8,128]{2,1,0:T(8,128)(2,1)S(1)}, bf16[1,8,128]{2,1,0:T(8,128)(2,1)}, u32[]{:S(2)}) %copy-start.2) | copy-done | bytes 2072
  7.3 0.0 copy-start.3
  7.3 0.7 %copy-done.3 = f32[1,512]{1,0:T(1,128)S(1)} copy-done((f32[1,512]{1,0:T(1,128)S(1)}, f32[1,512]{1,0:T(1,128)}, u32[]{:S(2)}) %copy-start.3) | copy-done | bytes 2072
  8.0 0.0 collective-permute-start
  8.0 1.2 %collective-permute-done = f32[12,128]{1,0:T(8,128)S(1)} collective-permute-done((f32[12,128]{1,0:T(8,128)S(1)}, f32[12,128]{1,0:T(8,128)S(1)}, u32[]{:S(2)}, u32[]{:S(2)}) %collective-permute-start) | collective-permute-done | bytes 6176 | tf_op jit(solution)/shard_map/ppermute | solution.py:454
  9.1 0.0 copy-start
  9.2 3.4 %copy-done = bf16[1,1024,4096]{2,1,0:T(8,128)(2,1)S(1)} copy-done((bf16[1,1024,4096]{2,1,0:T(8,128)(2,1)S(1)}, bf16[1,1024,4096]{2,1,0:T(8,128)(2,1)}, u32[]{:S(2)}) %copy-start) | copy-done | bytes 8388632
  12.5 0.0 copy-start.1
  12.5 0.6 %shard_map.50.refs_3_.refs_2_ = bf16[1024,4096]{1,0:T(8,128)(2,1)S(1)} custom-call(bf16[1024,4096]{1,0:T(8,128)(2,1)S(1)} %bitcast.5), custom_call_target="tpu_custom_call" | custom-call | bytes 16777216 | tf_op jit(solution)/shard_map/pallas_call | solution.py:410
  13.2 0.0 collective-permute-done.5.refs_0_
  13.2 1.3 %collective-permute-start.6 = (bf16[64,4096]{1,0:T(8,128)(2,1)S(1)}, bf16[64,4096]{1,0:T(8,128)(2,1)S(1)}, u32[]{:S(2)}, u32[]{:S(2)}) collective-permute-start(bf16[64,4096]{1,0:T(8,128)(2,1)S(1)} %collective-permute-done.5.refs_0_), channel_id=1, source_target_pairs={{4,0},{8,12},{5,1},{9,13},{6,2},{10,14},{7,3},{11,15},{20,16},{24,... | collective-permute-start | bytes 1572872 | tf_op jit(solution)/shard_map/ppermute | solution.py:462
  14.5 4.0 %collective-permute-done.4.refs_0_.rows_ref = bf16[64,4096]{1,0:T(8,128)(2,1)S(1)} collective-permute-done((bf16[64,4096]{1,0:T(8,128)(2,1)}, bf16[64,4096]{1,0:T(8,128)(2,1)S(1)}, u32[]{:S(2)}, u32[]{:S(2)}) %collective-permute-start.4) | collective-permute-done | bytes 524320 | tf_op jit(solution)/shard_map/ppermute | solution.py:439
  18.5 0.7 %collective-permute-start.7 = (bf16[32,4096]{1,0:T(8,128)(2,1)S(1)}, bf16[32,4096]{1,0:T(8,128)(2,1)S(1)}, u32[]{:S(2)}, u32[]{:S(2)}) collective-permute-start(bf16[32,4096]{1,0:T(8,128)(2,1)S(1)} %shard_map.52), channel_id=1, source_target_pairs={{4,8},{8,4},{5,9},{9,5},{6,10},{10,6},{7,11},{11,7},{20,24},{24,20... | collective-permute-start | bytes 786440 | tf_op jit(solution)/shard_map/ppermute | solution.py:470
  19.2 1.4 %collective-permute-start.3 = (f32[24,128]{1,0:T(8,128)S(1)}, f32[24,128]{1,0:T(8,128)S(1)}, u32[]{:S(2)}, u32[]{:S(2)}) collective-permute-start(f32[24,128]{1,0:T(8,128)S(1)} %pad_maximum_fusion.refs_0_), channel_id=1, source_target_pairs={{0,12},{4,0},{8,4},{12,8},{1,13},{5,1},{9,5},{13,9},{2,14},{6,2},{... | collective-permute-start | bytes 36872 | tf_op jit(solution)/shard_map/ppermute | solution.py:458
  20.6 4.6 %collective-permute-start.2 = (f32[24,128]{1,0:T(8,128)S(1)}, f32[24,128]{1,0:T(8,128)S(1)}, u32[]{:S(2)}, u32[]{:S(2)}) collective-permute-start(f32[24,128]{1,0:T(8,128)S(1)} %pad_maximum_fusion.refs_0_), channel_id=1, source_target_pairs={{0,8},{4,12},{8,0},{12,4},{1,9},{5,13},{9,1},{13,5},{2,10},{6,14},... | collective-permute-start | bytes 36872 | tf_op jit(solution)/shard_map/ppermute | solution.py:458
  25.2 0.5 collective-permute-start.1
  25.7 6.3 %collective-permute-done.3.refs_3_ = f32[24,128]{1,0:T(8,128)S(1)} collective-permute-done((f32[24,128]{1,0:T(8,128)S(1)}, f32[24,128]{1,0:T(8,128)S(1)}, u32[]{:S(2)}, u32[]{:S(2)}) %collective-permute-start.3) | collective-permute-done | bytes 12320 | tf_op jit(solution)/shard_map/ppermute | solution.py:458
  31.9 0.0 collective-permute-done.2.refs_2_
  31.9 0.0 collective-permute-done.1.refs_1_
  31.9 1.0 %shard_map.47 = (bf16[512,512]{1,0:T(8,128)(2,1)S(1)}, bf16[512,512]{1,0:T(8,128)(2,1)S(1)}, bf16[512,512]{1,0:T(8,128)(2,1)S(1)}, bf16[512,512]{1,0:T(8,128)(2,1)S(1)}, f32[512,256]{1,0:T(8,128)S(1)}) custom-call(f32[24,128]{1,0:T(8,128)S(1)} %pad_maximum_fusion.refs_0_, f32[24,128]{1,0:T(8,128)S(1)} %collective-permute-done.1.refs_1_, ...), custom_call_target="tpu_custom_call" | custom-call | flops 67108864 | bytes 2670592 | tf_op jit(solution)/shard_map/pallas_call | solution.py:31
  32.9 1.6 %shard_map.49 = (bf16[64,4096]{1,0:T(8,128)(2,1)S(1)}, bf16[32,4096]{1,0:T(8,128)(2,1)S(1)}) custom-call(bf16[64,4096]{1,0:T(8,128)(2,1)S(1)} %collective-permute-done.4.refs_0_.rows_ref, bf16[512,512]{1,0:T(8,128)(2,1)S(1)} %get-tuple-element.20.refs_1_.refs_2_.refs_6_, bf16[512,512]{1,0:T(8,128)(2,1)S(1)} %get-tuple-element.21.refs_2_.refs_3_.refs_7_, ...), custom_call_target="tpu_custom_call" | custom-call | flops 536870912 | bytes 3932160 | tf_op jit(solution)/shard_map/pallas_call | solution.py:31
  34.5 0.7 %collective-permute-start.10 = (bf16[32,4096]{1,0:T(8,128)(2,1)S(1)}, bf16[32,4096]{1,0:T(8,128)(2,1)S(1)}, u32[]{:S(2)}, u32[]{:S(2)}) collective-permute-start(bf16[32,4096]{1,0:T(8,128)(2,1)S(1)} %get-tuple-element.31), channel_id=1, source_target_pairs={{4,8},{8,4},{5,9},{9,5},{6,10},{10,6},{7,11},{11,7},{20,24},{24,20... | collective-permute-start | bytes 786440 | tf_op jit(solution)/shard_map/ppermute | solution.py:470
  35.2 0.0 collective-permute-done.7.refs_4_
  35.2 1.3 %collective-permute-start.8 = (bf16[32,4096]{1,0:T(8,128)(2,1)S(1)}, bf16[32,4096]{1,0:T(8,128)(2,1)S(1)}, u32[]{:S(2)}, u32[]{:S(2)}) collective-permute-start(bf16[32,4096]{1,0:T(8,128)(2,1)S(1)} %collective-permute-done.7.refs_4_), channel_id=1, source_target_pairs={{4,0},{8,12},{5,1},{9,13},{6,2},{10,14},{7,3},{11,15},{20,16},{24,... | collective-permute-start | bytes 786440 | tf_op jit(solution)/shard_map/ppermute | solution.py:470
  36.5 0.0 copy-done.1
  36.5 1.6 %shard_map.48.refs_0_ = bf16[64,4096]{1,0:T(8,128)(2,1)S(1)} custom-call(bf16[64,4096]{1,0:T(8,128)(2,1)S(1)} %bitcast.8, bf16[512,512]{1,0:T(8,128)(2,1)S(1)} %get-tuple-element.20.refs_1_.refs_2_.refs_6_, bf16[512,512]{1,0:T(8,128)(2,1)S(1)} %get-tuple-element.21.refs_2_.refs_3_.refs_7_, bf16[512,512]{1,0:T(8,128)(2,1)S(1)} %get-tuple-element.22.refs_3_.refs_4_.refs_8_, ...), custom_call_target="tpu_custom_call" | custom-call | flops 536870912 | bytes 3670016 | tf_op jit(solution)/shard_map/pallas_call | solution.py:31
  38.1 0.0 collective-permute-done.6.refs_1_
  38.2 1.7 %shard_map.51.refs_2_ = bf16[64,4096]{1,0:T(8,128)(2,1)S(1)} custom-call(bf16[64,4096]{1,0:T(8,128)(2,1)S(1)} %collective-permute-done.5.refs_0_, bf16[64,4096]{1,0:T(8,128)(2,1)S(1)} %collective-permute-done.6.refs_1_, bf16[512,512]{1,0:T(8,128)(2,1)S(1)} %get-tuple-element.20.refs_1_.refs_2_.refs_6_, ...), custom_call_target="tpu_custom_call" | custom-call | flops 536870912 | bytes 4194304 | tf_op jit(solution)/shard_map/pallas_call | solution.py:31
  39.9 0.0 collective-permute-done.10.refs_0_
  39.9 1.3 %collective-permute-start.11 = (bf16[32,4096]{1,0:T(8,128)(2,1)S(1)}, bf16[32,4096]{1,0:T(8,128)(2,1)S(1)}, u32[]{:S(2)}, u32[]{:S(2)}) collective-permute-start(bf16[32,4096]{1,0:T(8,128)(2,1)S(1)} %collective-permute-done.10.refs_0_), channel_id=1, source_target_pairs={{4,0},{8,12},{5,1},{9,13},{6,2},{10,14},{7,3},{11,15},{20,16},{24,... | collective-permute-start | bytes 786440 | tf_op jit(solution)/shard_map/ppermute | solution.py:470
  41.2 3.4 %collective-permute-done.8.refs_5_ = bf16[32,4096]{1,0:T(8,128)(2,1)S(1)} collective-permute-done((bf16[32,4096]{1,0:T(8,128)(2,1)S(1)}, bf16[32,4096]{1,0:T(8,128)(2,1)S(1)}, u32[]{:S(2)}, u32[]{:S(2)}) %collective-permute-start.8) | collective-permute-done | bytes 262176 | tf_op jit(solution)/shard_map/ppermute | solution.py:470
  44.5 3.8 %shard_map.53 = (f32[224,1024]{1,0:T(8,128)S(1)}, bf16[96,1024]{1,0:T(8,128)(2,1)S(1)}) custom-call(bf16[64,4096]{1,0:T(8,128)(2,1)S(1)} %shard_map.48.refs_0_, bf16[64,4096]{1,0:T(8,128)(2,1)S(1)} %get-tuple-element.25.refs_1_, bf16[64,4096]{1,0:T(8,128)(2,1)S(1)} %shard_map.51.refs_2_, bf16[1024,4096]{1,0:T(8,128)(2,1)S(1)} %shard_map.50.refs_3_.refs_2_, ...), custom_call_target="tpu_custom_call" | custom-call | flops 1879048192 | bytes 14221312 | tf_op jit(solution)/shard_map/pallas_call | solution.py:31
  48.4 1.6 %collective-permute-start.9 = (bf16[96,1024]{1,0:T(8,128)(2,1)S(1)}, bf16[96,1024]{1,0:T(8,128)(2,1)S(1)}, u32[]{:S(2)}, u32[]{:S(2)}) collective-permute-start(bf16[96,1024]{1,0:T(8,128)(2,1)S(1)} %get-tuple-element.30), channel_id=1, source_target_pairs={{0,2},{2,0},{1,3},{3,1},{4,6},{6,4},{5,7},{7,5},{8,10},{10,8},{9,1... | collective-permute-start | bytes 589832 | tf_op jit(solution)/shard_map/ppermute | solution.py:537
  49.9 0.0 collective-permute-done.11.refs_1_
  49.9 2.4 %shard_map.55 = (f32[32,1024]{1,0:T(8,128)S(1)}, bf16[32,1024]{1,0:T(8,128)(2,1)S(1)}) custom-call(bf16[32,4096]{1,0:T(8,128)(2,1)S(1)} %collective-permute-done.10.refs_0_, bf16[32,4096]{1,0:T(8,128)(2,1)S(1)} %collective-permute-done.11.refs_1_, bf16[1024,4096]{1,0:T(8,128)(2,1)S(1)} %shard_map.50.refs_3_.refs_2_, ...), custom_call_target="tpu_custom_call" | custom-call | flops 268435456 | bytes 10027008 | tf_op jit(solution)/shard_map/pallas_call | solution.py:31
  52.3 0.8 %collective-permute-start.12 = (bf16[32,1024]{1,0:T(8,128)(2,1)S(1)}, bf16[32,1024]{1,0:T(8,128)(2,1)S(1)}, u32[]{:S(2)}, u32[]{:S(2)}) collective-permute-start(bf16[32,1024]{1,0:T(8,128)(2,1)S(1)} %get-tuple-element.34), channel_id=1, source_target_pairs={{0,2},{2,0},{1,3},{3,1},{4,6},{6,4},{5,7},{7,5},{8,10},{10,8},{9,1... | collective-permute-start | bytes 196616 | tf_op jit(solution)/shard_map/ppermute | solution.py:537
  53.2 1.6 %collective-permute-done.9.refs_0_ = bf16[96,1024]{1,0:T(8,128)(2,1)S(1)} collective-permute-done((bf16[96,1024]{1,0:T(8,128)(2,1)S(1)}, bf16[96,1024]{1,0:T(8,128)(2,1)S(1)}, u32[]{:S(2)}, u32[]{:S(2)}) %collective-permute-start.9) | collective-permute-done | bytes 196640 | tf_op jit(solution)/shard_map/ppermute | solution.py:537
  54.8 0.8 %shard_map.54._ = f32[128,1024]{1,0:T(8,128)} custom-call(f32[224,1024]{1,0:T(8,128)S(1)} %get-tuple-element.29.early_ref.refs_3_, bf16[96,1024]{1,0:T(8,128)(2,1)S(1)} %collective-permute-done.9.refs_0_), custom_call_target="tpu_custom_call" | custom-call | flops 131072 | bytes 1638400 | tf_op jit(solution)/shard_map/pallas_call | solution.py:31
  55.7 1.0 %collective-permute-done.12.refs_0_ = bf16[32,1024]{1,0:T(8,128)(2,1)S(1)} collective-permute-done((bf16[32,1024]{1,0:T(8,128)(2,1)S(1)}, bf16[32,1024]{1,0:T(8,128)(2,1)S(1)}, u32[]{:S(2)}, u32[]{:S(2)}) %collective-permute-start.12) | collective-permute-done | bytes 65568 | tf_op jit(solution)/shard_map/ppermute | solution.py:537
  56.7 0.7 %shard_map.56 = f32[128,1024]{1,0:T(8,128)} custom-call(f32[128,1024]{1,0:T(8,128)} %shard_map.54._, f32[224,1024]{1,0:T(8,128)S(1)} %get-tuple-element.29.early_ref.refs_3_, f32[32,1024]{1,0:T(8,128)S(1)} %get-tuple-element.33.late_ref, bf16[32,1024]{1,0:T(8,128)(2,1)S(1)} %collective-permute-done.12.refs_0_), custom_call_target="tpu_custom_call", output_to_operand_aliasing={{}: (0, {})} | custom-call | tf_op jit(solution)/shard_map/pallas_call | solution.py:584
  (3 shorter events, 0.0 us)
Async XLA Ops:
  0.0 13.2 %collective-permute-start.5 = (bf16[64,4096]{1,0:T(8,128)(2,1)}, bf16[64,4096]{1,0:T(8,128)(2,1)S(1)}, u32[]{:S(2)}, u32[]{:S(2)}) collective-permute-start(bf16[64,4096]{1,0:T(8,128)(2,1)} %bitcast.6), channel_id=1, source_target_pairs={{4,8},{8,4},{5,9},{9,5},{6,10},{10,6},{7,11},{11,7},{20,24},{24,20... | collective-permute-start | bytes 1572872 | tf_op jit(solution)/shard_map/ppermute | solution.py:438
  0.7 17.8 %collective-permute-start.4 = (bf16[64,4096]{1,0:T(8,128)(2,1)}, bf16[64,4096]{1,0:T(8,128)(2,1)S(1)}, u32[]{:S(2)}, u32[]{:S(2)}) collective-permute-start(bf16[64,4096]{1,0:T(8,128)(2,1)} %bitcast.7), channel_id=1, source_target_pairs={{0,4},{4,0},{8,12},{12,8},{1,5},{5,1},{9,13},{13,9},{2,6},{6,2},{1... | collective-permute-start | bytes 1572872 | tf_op jit(solution)/shard_map/ppermute | solution.py:439
  6.6 0.7 %copy-start.2 = (bf16[1,8,128]{2,1,0:T(8,128)(2,1)S(1)}, bf16[1,8,128]{2,1,0:T(8,128)(2,1)}, u32[]{:S(2)}) copy-start(bf16[1,8,128]{2,1,0:T(8,128)(2,1)} %param.6) | copy-start | bytes 6148
  7.3 0.7 %copy-start.3 = (f32[1,512]{1,0:T(1,128)S(1)}, f32[1,512]{1,0:T(1,128)}, u32[]{:S(2)}) copy-start(f32[1,512]{1,0:T(1,128)} %param.7) | copy-start | bytes 6148
  8.0 1.2 %collective-permute-start = (f32[12,128]{1,0:T(8,128)S(1)}, f32[12,128]{1,0:T(8,128)S(1)}, u32[]{:S(2)}, u32[]{:S(2)}) collective-permute-start(f32[12,128]{1,0:T(8,128)S(1)} %shard_map.46), channel_id=1, source_target_pairs={{0,1},{1,0},{2,3},{3,2},{4,5},{5,4},{6,7},{7,6},{8,9},{9,8},{10,11... | collective-permute-start | bytes 18440 | tf_op jit(solution)/shard_map/ppermute | solution.py:454
  9.1 3.4 %copy-start = (bf16[1,1024,4096]{2,1,0:T(8,128)(2,1)S(1)}, bf16[1,1024,4096]{2,1,0:T(8,128)(2,1)}, u32[]{:S(2)}) copy-start(bf16[1,1024,4096]{2,1,0:T(8,128)(2,1)} %param.4) | copy-start | bytes 25165828
  12.5 24.0 %copy-start.1 = (bf16[1,1,64,4096]{3,2,1,0:T(8,128)(2,1)S(1)}, bf16[1,1,64,4096]{3,2,1,0:T(8,128)(2,1)}, u32[]{:S(2)}) copy-start(bf16[1,1,64,4096]{3,2,1,0:T(8,128)(2,1)} %param.5) | copy-start | bytes 1572868
  13.2 24.9 %collective-permute-start.6 = (bf16[64,4096]{1,0:T(8,128)(2,1)S(1)}, bf16[64,4096]{1,0:T(8,128)(2,1)S(1)}, u32[]{:S(2)}, u32[]{:S(2)}) collective-permute-start(bf16[64,4096]{1,0:T(8,128)(2,1)S(1)} %collective-permute-done.5.refs_0_), channel_id=1, source_target_pairs={{4,0},{8,12},{5,1},{9,13},{6,2},{10,14},{7,3},{11,15},{20,16},{24,... | collective-permute-start | bytes 1572872 | tf_op jit(solution)/shard_map/ppermute | solution.py:462
  18.5 16.7 %collective-permute-start.7 = (bf16[32,4096]{1,0:T(8,128)(2,1)S(1)}, bf16[32,4096]{1,0:T(8,128)(2,1)S(1)}, u32[]{:S(2)}, u32[]{:S(2)}) collective-permute-start(bf16[32,4096]{1,0:T(8,128)(2,1)S(1)} %shard_map.52), channel_id=1, source_target_pairs={{4,8},{8,4},{5,9},{9,5},{6,10},{10,6},{7,11},{11,7},{20,24},{24,20... | collective-permute-start | bytes 786440 | tf_op jit(solution)/shard_map/ppermute | solution.py:470
  19.2 12.8 %collective-permute-start.3 = (f32[24,128]{1,0:T(8,128)S(1)}, f32[24,128]{1,0:T(8,128)S(1)}, u32[]{:S(2)}, u32[]{:S(2)}) collective-permute-start(f32[24,128]{1,0:T(8,128)S(1)} %pad_maximum_fusion.refs_0_), channel_id=1, source_target_pairs={{0,12},{4,0},{8,4},{12,8},{1,13},{5,1},{9,5},{13,9},{2,14},{6,2},{... | collective-permute-start | bytes 36872 | tf_op jit(solution)/shard_map/ppermute | solution.py:458
  20.6 11.4 %collective-permute-start.2 = (f32[24,128]{1,0:T(8,128)S(1)}, f32[24,128]{1,0:T(8,128)S(1)}, u32[]{:S(2)}, u32[]{:S(2)}) collective-permute-start(f32[24,128]{1,0:T(8,128)S(1)} %pad_maximum_fusion.refs_0_), channel_id=1, source_target_pairs={{0,8},{4,12},{8,0},{12,4},{1,9},{5,13},{9,1},{13,5},{2,10},{6,14},... | collective-permute-start | bytes 36872 | tf_op jit(solution)/shard_map/ppermute | solution.py:458
  25.2 6.8 %collective-permute-start.1 = (f32[24,128]{1,0:T(8,128)S(1)}, f32[24,128]{1,0:T(8,128)S(1)}, u32[]{:S(2)}, u32[]{:S(2)}) collective-permute-start(f32[24,128]{1,0:T(8,128)S(1)} %pad_maximum_fusion.refs_0_), channel_id=1, source_target_pairs={{0,4},{4,8},{8,12},{12,0},{1,5},{5,9},{9,13},{13,1},{2,6},{6,10},{... | collective-permute-start | bytes 36872 | tf_op jit(solution)/shard_map/ppermute | solution.py:458
  34.5 5.3 %collective-permute-start.10 = (bf16[32,4096]{1,0:T(8,128)(2,1)S(1)}, bf16[32,4096]{1,0:T(8,128)(2,1)S(1)}, u32[]{:S(2)}, u32[]{:S(2)}) collective-permute-start(bf16[32,4096]{1,0:T(8,128)(2,1)S(1)} %get-tuple-element.31), channel_id=1, source_target_pairs={{4,8},{8,4},{5,9},{9,5},{6,10},{10,6},{7,11},{11,7},{20,24},{24,20... | collective-permute-start | bytes 786440 | tf_op jit(solution)/shard_map/ppermute | solution.py:470
  35.2 9.3 %collective-permute-start.8 = (bf16[32,4096]{1,0:T(8,128)(2,1)S(1)}, bf16[32,4096]{1,0:T(8,128)(2,1)S(1)}, u32[]{:S(2)}, u32[]{:S(2)}) collective-permute-start(bf16[32,4096]{1,0:T(8,128)(2,1)S(1)} %collective-permute-done.7.refs_4_), channel_id=1, source_target_pairs={{4,0},{8,12},{5,1},{9,13},{6,2},{10,14},{7,3},{11,15},{20,16},{24,... | collective-permute-start | bytes 786440 | tf_op jit(solution)/shard_map/ppermute | solution.py:470
  39.9 10.1 %collective-permute-start.11 = (bf16[32,4096]{1,0:T(8,128)(2,1)S(1)}, bf16[32,4096]{1,0:T(8,128)(2,1)S(1)}, u32[]{:S(2)}, u32[]{:S(2)}) collective-permute-start(bf16[32,4096]{1,0:T(8,128)(2,1)S(1)} %collective-permute-done.10.refs_0_), channel_id=1, source_target_pairs={{4,0},{8,12},{5,1},{9,13},{6,2},{10,14},{7,3},{11,15},{20,16},{24,... | collective-permute-start | bytes 786440 | tf_op jit(solution)/shard_map/ppermute | solution.py:470
  48.4 6.4 %collective-permute-start.9 = (bf16[96,1024]{1,0:T(8,128)(2,1)S(1)}, bf16[96,1024]{1,0:T(8,128)(2,1)S(1)}, u32[]{:S(2)}, u32[]{:S(2)}) collective-permute-start(bf16[96,1024]{1,0:T(8,128)(2,1)S(1)} %get-tuple-element.30), channel_id=1, source_target_pairs={{0,2},{2,0},{1,3},{3,1},{4,6},{6,4},{5,7},{7,5},{8,10},{10,8},{9,1... | collective-permute-start | bytes 589832 | tf_op jit(solution)/shard_map/ppermute | solution.py:537
  52.3 4.3 %collective-permute-start.12 = (bf16[32,1024]{1,0:T(8,128)(2,1)S(1)}, bf16[32,1024]{1,0:T(8,128)(2,1)S(1)}, u32[]{:S(2)}, u32[]{:S(2)}) collective-permute-start(bf16[32,1024]{1,0:T(8,128)(2,1)S(1)} %get-tuple-element.34), channel_id=1, source_target_pairs={{0,2},{2,0},{1,3},{3,1},{4,6},{6,4},{5,7},{7,5},{8,10},{10,8},{9,1... | collective-permute-start | bytes 196616 | tf_op jit(solution)/shard_map/ppermute | solution.py:537

commit v4 on v3

--- a/solution.py
+++ b/solution.py
@@ -1,4 +1,5 @@
 import functools
+import math
 
 import jax
 import jax.numpy as jnp
@@ -11,6 +12,7 @@
 HALF = 8
 BF16, F32 = jnp.bfloat16, jnp.float32
 IN_VMEM = pl.BlockSpec(memory_space=pltpu.VMEM)
+IN_HBM = pl.BlockSpec(memory_space=pltpu.HBM)
 
 
 class Place:
@@ -27,12 +29,12 @@
 
 def call(kernel, out_shape, in_specs, scratch, args, flops, grant):
     outs = out_shape if isinstance(out_shape, (list, tuple)) else [out_shape]
-    moved = sum(a.size * a.dtype.itemsize for a in list(args) + list(outs))
+    moved = sum(math.prod(a.shape) * a.dtype.itemsize for a in list(args) + list(outs))
     return pl.pallas_call(
         kernel,
         out_shape=out_shape,
         in_specs=in_specs,
-        out_specs=jax.tree.map(lambda _: IN_VMEM, out_shape),
+        out_specs=[IN_VMEM] * len(outs) if outs is out_shape else IN_VMEM,
         scratch_shapes=scratch,
         compiler_params=pltpu.CompilerParams(vmem_limit_bytes=grant),
         cost_estimate=pl.CostEstimate(flops=flops, bytes_accessed=moved, transcendentals=0),
@@ -97,8 +99,10 @@
 
 def prep_kernel(shape, here_ref, *refs):
     count, reps, base_rows, eigen_rows, fold = shape
-    parts = refs[:count]
-    w1_ref, but_ref, bu_ref, w5_ref, inv_ref, base3, eigen3, base, eigen, pad = refs[count:]
+    parts, train_ref, refs = refs[:count], refs[count], refs[count + 1 :]
+    w1_ref, but_ref, bu_ref, w5_ref, inv_ref, x_ref, base3, eigen3, base, eigen, pad, sem = refs
+    load = pltpu.make_async_copy(train_ref.at[pl.ds(0, x_ref.shape[0])], x_ref, sem)
+    load.start()
     z, rep = here_ref[0], here_ref[2]
     each = base_rows + eigen_rows
     for d in range(count):
@@ -133,9 +137,10 @@
         row = jnp.broadcast_to(pad[i : i + 1, :], (HALF, 2 * size))
         for h in range(fold // 2):
             inv_ref[i * HALF : (i + 1) * HALF, h * 2 * size : (h + 1) * 2 * size] = row
-
-
-def rotation_constants(parts, reps, base_rows, eigen_rows, size, fold):
+    load.wait()
+
+
+def rotation_constants(parts, train, taken, reps, base_rows, eigen_rows, size, fold):
     count = len(parts)
     wide, tall = 2 * size * fold, HALF * size
     shard = count * reps
@@ -147,16 +152,18 @@
             jax.ShapeDtypeStruct((tall, tall), BF16),
             jax.ShapeDtypeStruct((wide, wide), BF16),
             jax.ShapeDtypeStruct((tall, size * fold), F32),
+            pltpu.VMEM((taken, train.shape[1]), train.dtype),
         ],
-        [IN_VMEM] * count,
+        [IN_VMEM] * count + [IN_HBM],
         [
             pltpu.VMEM((shard, base_rows, 2 * size), F32),
             pltpu.VMEM((shard, eigen_rows, 2 * size), F32),
             pltpu.VMEM((size, 2 * size), F32),
             pltpu.VMEM((size // 2, 2 * size), F32),
             pltpu.VMEM((size, 2 * size), F32),
+            pltpu.SemaphoreType.DMA,
         ],
-        tuple(parts),
+        (*parts, pltpu.with_memory_space_constraint(train, pltpu.HBM)),
         flops=2 * wide * wide * 2 * size,
         grant=12 << 20,
     )
@@ -234,9 +241,16 @@
                 write(h * TILE, a * lanes, value)
 
 
-def rotate_kernel(sources, choice, split, here_ref, *refs):
+def rotate_kernel(sources, choice, split, start, here_ref, *refs):
     inputs, refs = refs[:sources], refs[sources:]
-    out_ref, *rest = refs[5:]
+    constants, refs = refs[:5], list(refs[5:])
+    load = None
+    if start is not None:
+        train_ref, sem = refs.pop(0), refs.pop()
+        x_ref = refs.pop(2 if split else 1)
+        load = pltpu.make_async_copy(train_ref.at[pl.ds(start, x_ref.shape[0])], x_ref, sem)
+        load.start()
+    out_ref, *rest = refs
 
     def write(row, lane, value):
         rows, lanes = value.shape
@@ -244,7 +258,9 @@
         if split and row >= split:
             rest[0][row - split : row - split + rows, lane : lane + lanes] = value
 
-    turn(inputs, choice, here_ref, refs[:5], rest[-3:], write)
+    turn(inputs, choice, here_ref, constants, rest[-3:], write)
+    if load is not None:
+        load.wait()
 
 
 def turn_scratch(rows, constants):
@@ -257,21 +273,29 @@
     ]
 
 
-def rotate(choice, inputs, constants, split=0):
+def rotate(choice, inputs, constants, split=0, load=None):
     rows, width = inputs[0].shape
     fold = rows // TILE
     size = constants[1].shape[0] // HALF
     shapes = [jax.ShapeDtypeStruct((rows, width), BF16)]
     if split:
         shapes.append(jax.ShapeDtypeStruct((rows - split, width), BF16))
+    specs, args = [IN_VMEM] * (len(inputs) + 5), [*inputs, *constants]
+    scratch, start = turn_scratch(rows, constants), None
+    if load is not None:
+        array, start, taken = load
+        shapes.append(pltpu.VMEM((taken, array.shape[1]), array.dtype))
+        specs.append(IN_HBM)
+        args.append(pltpu.with_memory_space_constraint(array, pltpu.HBM))
+        scratch = scratch + [pltpu.SemaphoreType.DMA]
     return call(
-        functools.partial(rotate_kernel, len(inputs), choice, split, PLACE),
+        functools.partial(rotate_kernel, len(inputs), choice, split, start, PLACE),
         shapes,
-        [IN_VMEM] * (len(inputs) + 5),
-        turn_scratch(rows, constants),
-        (*inputs, *constants),
+        specs,
+        scratch,
+        tuple(args),
         flops=8 * rows * width * size * fold,
-        grant=12 << 20,
+        grant=16 << 20,
     )
 
 
@@ -292,13 +316,14 @@
         at += rows
 
 
-def products(held, x_ref, kept_ref):
-    total = x_ref.shape[0]
-    step = min(256, total)
-    for t in range(0, total, step):
-        kept_ref[:, t : t + step] = lax.dot_general(
-            x_ref[t : t + step, :], held[...], (((1,), (1,)), ((), ())), preferred_element_type=F32
+def products(held, x_refs, kept_ref):
+    at = 0
+    for x_ref in x_refs:
+        total = x_ref.shape[0]
+        kept_ref[:, at : at + total] = lax.dot_general(
+            x_ref[...], held[...], (((1,), (1,)), ((), ())), preferred_element_type=F32
         ).T
+        at += total
 
 
 def grid_lookup(table, z, owner):
@@ -312,10 +337,10 @@
     return pl.ds(pl.multiple_of(start, rows), rows)
 
 
-def early_kernel(shape, choices, table, piece, raw_choice, here_ref, *refs):
+def early_kernel(shape, choices, table, piece, loaded, raw_choice, here_ref, *refs):
     refs = list(refs)
     units = [[refs.pop(0) for _ in range(n)] for n in shape]
-    x_ref = refs.pop(0)
+    x_refs = [refs.pop(0) for _ in range(loaded)]
     inputs = [refs.pop(0) for _ in range(len(set(raw_choice)))]
     constants = [refs.pop(0) for _ in range(5)]
     *scratch, held = refs[-4:]
@@ -328,7 +353,7 @@
         held[base + row : base + row + rows, lane : lane + lanes] = value
 
     turn(inputs, raw_choice, here_ref, constants, scratch, write)
-    products(held, x_ref, kept_ref)
+    products(held, x_refs, kept_ref)
     z, x = here_ref[0], here_ref[1]
     layers = len(sent) + 1
     for d, sent_ref in enumerate(sent, 1):
@@ -338,13 +363,14 @@
             sent_ref[p * piece : (p + 1) * piece, :] = kept_ref[aligned(start, piece), :].astype(BF16)
 
 
-def late_kernel(shape, choices, table, piece, here_ref, *refs):
+def late_kernel(shape, choices, table, piece, loaded, here_ref, *refs):
     refs = list(refs)
     units = [[refs.pop(0) for _ in range(n)] for n in shape]
-    x_ref, early_ref, kept_ref, *sent = refs[:-1]
+    x_refs = [refs.pop(0) for _ in range(loaded)]
+    early_ref, kept_ref, *sent = refs[:-1]
     held = refs[-1]
     fill(held, units, choices, here_ref)
-    products(held, x_ref, kept_ref)
+    products(held, x_refs, kept_ref)
     z, x = here_ref[0], here_ref[1]
     layers = len(sent) + 1
     for d, sent_ref in enumerate(sent, 1):
@@ -391,33 +417,6 @@
     copy = pltpu.make_async_copy(total, out_ref.at[place], sem)
     copy.start()
     copy.wait()
-
-
-def load_kernel(x_ref, out_ref, sem):
-    pieces = sem.shape[0]
-    step = x_ref.shape[0] // pieces
-    copies = []
-    for i in range(pieces):
-        rows = pl.ds(i * step, step)
-        copies.append(pltpu.make_async_copy(x_ref.at[rows], out_ref.at[rows], sem.at[i]))
-    for copy in copies:
-        copy.start()
-    for copy in copies:
-        copy.wait()
-
-
-def resident(x):
-    return pl.pallas_call(
-        load_kernel,
-        out_shape=pltpu.VMEM(x.shape, x.dtype),
-        in_specs=[pl.BlockSpec(memory_space=pltpu.HBM)],
-        out_specs=IN_VMEM,
-        scratch_shapes=[pltpu.SemaphoreType.DMA((8,))],
-        compiler_params=pltpu.CompilerParams(vmem_limit_bytes=12 << 20),
-        cost_estimate=pl.CostEstimate(
-            flops=0, bytes_accessed=2 * x.size * x.dtype.itemsize, transcendentals=0
-        ),
-    )(x)
 
 
 def steps(train_grads, queries, bases, eigenvalues):
@@ -456,12 +455,13 @@
     parts = [pair]
     for d in range(1, blocks):
         parts.append(lax.ppermute(pair, "blk", [(a, (a + d) % blocks) for a in range(blocks)]))
-    train, _ = lax.optimization_barrier((train, pair))
-    train = resident(train)
-    raw[1, 1], train = lax.optimization_barrier((raw[1, 1], train))
     raw[2, 0] = lax.ppermute(raw[1, 1], "blk", plan[2, 0])
 
-    constants = rotation_constants(parts, reps, base_rows, eigen_rows, size, fold)
+    quarter = train.shape[0] // 4
+    *constants, loaded = rotation_constants(
+        parts, train, quarter, reps, base_rows, eigen_rows, size, fold
+    )
+    loaded = [loaded]
     alone = [0] * blocks
     block_of = [list(range(blocks))] + [[a[j][2] for a in arrivals] for j in range(blocks - 1)]
     source_of = [None] + [[a[j][:2] for a in arrivals] for j in range(blocks - 1)]
@@ -470,12 +470,16 @@
         return lax.ppermute(value, "blk", plan[step, parity])
 
     mixed[2, 1] = [hop(2, 1, head(raw[1, 0], piece))] if (2, 1) in plan else []
-    whole_first, last = rotate(alone, [raw[1, 0]], constants, piece)
+    whole_first, last, part = rotate(
+        alone, [raw[1, 0]], constants, piece, (train, quarter, quarter)
+    )
+    loaded.append(part)
     if mixed[2, 1]:
         mixed[2, 1].append(hop(2, 1, last))
         if (3, 0) in plan:
             mixed[3, 0] = [hop(3, 0, mixed[2, 1][0])]
-    whole_own, = rotate(alone, [own], constants)
+    whole_own, part = rotate(alone, [own], constants, 0, (train, 2 * quarter, quarter))
+    loaded.append(part)
     units, choices = [[whole_own], [whole_first]], [alone, alone]
 
     turned_last = {}
@@ -496,7 +500,10 @@
         names = sorted(set(source_of[j]))
         choice = [names.index(s) for s in source_of[j]]
         if all(n in raw for n in names):
-            whole, = rotate(choice, [raw[n] for n in names], constants)
+            whole, part = rotate(
+                choice, [raw[n] for n in names], constants, 0, (train, 3 * quarter, quarter)
+            )
+            loaded.append(part)
             units.append([whole])
             choices.append(choice if len(units[-1]) > 1 else alone)
             gate = whole
@@ -541,10 +548,10 @@
     total, width = train.shape
 
     def scores(kernel, units, choices, extra, held, sent_rows, scratch, grant):
-        flat = [w for u in units for w in u] + [train] + extra
+        flat = [w for u in units for w in u] + loaded + extra
         sent_shape = jax.ShapeDtypeStruct((sent_rows, total), BF16)
         return call(
-            functools.partial(kernel, [len(u) for u in units], choices, table, piece, PLACE),
+            functools.partial(kernel, [len(u) for u in units], choices, table, piece, len(loaded), PLACE),
             [jax.ShapeDtypeStruct((held, total), F32)] + [sent_shape] * (layers - 1),
             [IN_VMEM] * len(flat),
             scratch + [pltpu.VMEM((held, width), BF16)],
@@ -554,8 +561,8 @@
         )
 
     early, *sent = scores(
-        lambda shape, choices, table, piece, *refs: early_kernel(
-            shape, choices, table, piece, raw_choice, *refs
+        lambda shape, choices, table, piece, loaded, *refs: early_kernel(
+            shape, choices, table, piece, loaded, raw_choice, *refs
         ),
         units[:-1],
         choices[:-1],
@@ -580,12 +587,11 @@
         flops=per_owner * rows * total,
         grant=8 << 20,
     )
-    in_hbm = pl.BlockSpec(memory_space=pltpu.HBM)
     out = pl.pallas_call(
         functools.partial(last_finish_kernel, table, places, piece, PLACE),
         out_shape=out_shape,
-        in_specs=[in_hbm] + [IN_VMEM] * (1 + layers),
-        out_specs=in_hbm,
+        in_specs=[IN_HBM] + [IN_VMEM] * (1 + layers),
+        out_specs=IN_HBM,
         scratch_shapes=[pltpu.VMEM((piece, total), F32), pltpu.SemaphoreType.DMA],
         input_output_aliases={0: 0},
         compiler_params=pltpu.CompilerParams(vmem_limit_bytes=8 << 20),

time: 57.6 us -> 59.5 us (1.033)
  local copies, waits for them, and re-layouts: 4.74 us -> 1.36 us
  waiting for transfers between devices: 17.4 us -> 20.5 us
  Pallas kernels: 14.3 us -> 15.4 us
  starting transfers between devices: 20.7 us -> 21.7 us
    ppermute x1, waiting for transfers between devices: 3.96 us -> 10.6 us  [steps(): raw[1, 0] = lax.ppermute(own, 'blk', plan[1, 0])]
    ppermute x3, waiting for transfers between devices: 6.26 us -> 2.86 us  [steps(): lax.ppermute(pair, 'blk', [(a, (a + d) % blocks) for a in range(blocks)])]
    unnamed x8 -> x6, local copies, waits for them, and re-layouts: 4.74 us -> 1.36 us
    pallas_call x9, Pallas kernels: 13 us -> 14.7 us  [call(): pl.pallas_call(kernel, out_shape=out_shape, in_specs=in_specs, out_specs=...]
    ppermute x3, starting transfers between devices: 6.51 us -> 7.36 us  [steps(): lax.ppermute(pair, 'blk', [(a, (a + d) % blocks) for a in range(blocks)])]
    pallas_call x1 -> x0, Pallas kernels: 0.64 us -> none  [resident(): pl.pallas_call(load_kernel, out_shape=pltpu.VMEM(x.shape, x.dtype), in_sp...]
  transfers between devices with their start and end apart: 13 -> 13, of which waited for: 6 -> 7; matrix products, arithmetic and copies ran while one was open for 0% -> 0% of each run, Pallas kernels for 24% -> 25%
where the time goes in v4:
time: 59.5 us; the launch traced here: 59.1 us
  starting transfers between devices  21.7 us (36%)
  waiting for transfers between devices  20.5 us (34%)
  Pallas kernels  15.4 us (26%)
  local copies, waits for them, and re-layouts  1.36 us (2%)
    pallas_call x9, Pallas kernels, call(): pl.pallas_call(kernel, out_shape=out_shape, in_specs=in_specs, out_specs=...  14.7 us
    ppermute x1, waiting for transfers between devices, steps(): raw[1, 0] = lax.ppermute(own, 'blk', plan[1, 0])  10.6 us
    ppermute x3, starting transfers between devices, steps(): lax.ppermute(pair, 'blk', [(a, (a + d) % blocks) for a in range(blocks)])  7.36 us
    ppermute x1, starting transfers between devices, steps(): raw[1, 0] = lax.ppermute(own, 'blk', plan[1, 0])  5.91 us
    ppermute x4, starting transfers between devices, hop(): return lax.ppermute(value, 'blk', plan[step, parity])  3.94 us
    ppermute x4, waiting for transfers between devices, hop(): return lax.ppermute(value, 'blk', plan[step, parity])  3.38 us
    ppermute x3, waiting for transfers between devices, steps(): lax.ppermute(pair, 'blk', [(a, (a + d) % blocks) for a in range(blocks)])  2.86 us
    ppermute x2, waiting for transfers between devices, shifted(): lax.ppermute(s, 'layer', [(o, (o + d) % layers) for o in range(layers)])  2.54 us
  transfers between devices with their start and end apart: 13, of which 7 were waited for; matrix products, arithmetic and copies ran while one was open for 0% of the time, Pallas kernels for 25%

profile of v4, /device:TPU:0, one launch (start us, length us, event | category | flops | bytes accessed | tf_op | source)
XLA Modules:
  0.0 59.1 jit_solution(10643347333138607801)
XLA Ops:
  0.0 0.7 %collective-permute-start.5 = (bf16[64,4096]{1,0:T(8,128)(2,1)}, bf16[64,4096]{1,0:T(8,128)(2,1)S(1)}, u32[]{:S(2)}, u32[]{:S(2)}) collective-permute-start(bf16[64,4096]{1,0:T(8,128)(2,1)} %bitcast.5), channel_id=1, source_target_pairs={{4,8},{8,4},{5,9},{9,5},{6,10},{10,6},{7,11},{11,7},{20,24},{24,20... | collective-permute-start | bytes 1572872 | tf_op jit(solution)/shard_map/ppermute | solution.py:437
  0.7 5.9 %collective-permute-start.4 = (bf16[64,4096]{1,0:T(8,128)(2,1)}, bf16[64,4096]{1,0:T(8,128)(2,1)S(1)}, u32[]{:S(2)}, u32[]{:S(2)}) collective-permute-start(bf16[64,4096]{1,0:T(8,128)(2,1)} %bitcast.6), channel_id=1, source_target_pairs={{0,4},{4,0},{8,12},{12,8},{1,5},{5,1},{9,13},{13,9},{2,6},{6,2},{1... | collective-permute-start | bytes 1572872 | tf_op jit(solution)/shard_map/ppermute | solution.py:438
  6.6 0.0 collective-permute-done.5.refs_0_
  6.6 1.3 %collective-permute-start.6 = (bf16[64,4096]{1,0:T(8,128)(2,1)S(1)}, bf16[64,4096]{1,0:T(8,128)(2,1)S(1)}, u32[]{:S(2)}, u32[]{:S(2)}) collective-permute-start(bf16[64,4096]{1,0:T(8,128)(2,1)S(1)} %collective-permute-done.5.refs_0_), channel_id=1, source_target_pairs={{4,0},{8,12},{5,1},{9,13},{6,2},{10,14},{7,3},{11,15},{20,16},{24,... | collective-permute-start | bytes 1572872 | tf_op jit(solution)/shard_map/ppermute | solution.py:458
  7.9 10.6 %collective-permute-done.4.refs_0_.rows_ref = bf16[64,4096]{1,0:T(8,128)(2,1)S(1)} collective-permute-done((bf16[64,4096]{1,0:T(8,128)(2,1)}, bf16[64,4096]{1,0:T(8,128)(2,1)S(1)}, u32[]{:S(2)}, u32[]{:S(2)}) %collective-permute-start.4) | collective-permute-done | bytes 524320 | tf_op jit(solution)/shard_map/ppermute | solution.py:438
  18.5 0.7 %collective-permute-start.7 = (bf16[32,4096]{1,0:T(8,128)(2,1)S(1)}, bf16[32,4096]{1,0:T(8,128)(2,1)S(1)}, u32[]{:S(2)}, u32[]{:S(2)}) collective-permute-start(bf16[32,4096]{1,0:T(8,128)(2,1)S(1)} %shard_map.51), channel_id=1, source_target_pairs={{4,8},{8,4},{5,9},{9,5},{6,10},{10,6},{7,11},{11,7},{20,24},{24,20... | collective-permute-start | bytes 786440 | tf_op jit(solution)/shard_map/ppermute | solution.py:470
  19.2 0.0 copy-start.1
  19.2 0.7 %copy-done.1 = bf16[1,8,128]{2,1,0:T(8,128)(2,1)S(1)} copy-done((bf16[1,8,128]{2,1,0:T(8,128)(2,1)S(1)}, bf16[1,8,128]{2,1,0:T(8,128)(2,1)}, u32[]{:S(2)}) %copy-start.1) | copy-done | bytes 2072
  19.8 0.0 copy-start.2
  19.9 0.7 %copy-done.2 = f32[1,512]{1,0:T(1,128)S(1)} copy-done((f32[1,512]{1,0:T(1,128)S(1)}, f32[1,512]{1,0:T(1,128)}, u32[]{:S(2)}) %copy-start.2) | copy-done | bytes 2072
  20.5 0.0 collective-permute-start
  20.5 1.2 %collective-permute-done = f32[12,128]{1,0:T(8,128)S(1)} collective-permute-done((f32[12,128]{1,0:T(8,128)S(1)}, f32[12,128]{1,0:T(8,128)S(1)}, u32[]{:S(2)}, u32[]{:S(2)}) %collective-permute-start) | collective-permute-done | bytes 6176 | tf_op jit(solution)/shard_map/ppermute | solution.py:453
  21.7 4.5 %collective-permute-start.1 = (f32[24,128]{1,0:T(8,128)S(1)}, f32[24,128]{1,0:T(8,128)S(1)}, u32[]{:S(2)}, u32[]{:S(2)}) collective-permute-start(f32[24,128]{1,0:T(8,128)S(1)} %pad_maximum_fusion.refs_0_), channel_id=1, source_target_pairs={{0,4},{4,8},{8,12},{12,0},{1,5},{5,9},{9,13},{13,1},{2,6},{6,10},{... | collective-permute-start | bytes 36872 | tf_op jit(solution)/shard_map/ppermute | solution.py:457
  26.2 0.0 collective-permute-start.2
  26.2 2.9 %collective-permute-start.3 = (f32[24,128]{1,0:T(8,128)S(1)}, f32[24,128]{1,0:T(8,128)S(1)}, u32[]{:S(2)}, u32[]{:S(2)}) collective-permute-start(f32[24,128]{1,0:T(8,128)S(1)} %pad_maximum_fusion.refs_0_), channel_id=1, source_target_pairs={{0,12},{4,0},{8,4},{12,8},{1,13},{5,1},{9,5},{13,9},{2,14},{6,2},{... | collective-permute-start | bytes 36872 | tf_op jit(solution)/shard_map/ppermute | solution.py:457
  29.1 0.0 collective-permute-done.1.refs_1_
  29.1 1.9 %collective-permute-done.2.refs_2_ = f32[24,128]{1,0:T(8,128)S(1)} collective-permute-done((f32[24,128]{1,0:T(8,128)S(1)}, f32[24,128]{1,0:T(8,128)S(1)}, u32[]{:S(2)}, u32[]{:S(2)}) %collective-permute-start.2) | collective-permute-done | bytes 12320 | tf_op jit(solution)/shard_map/ppermute | solution.py:457
  31.0 1.0 %collective-permute-done.3.refs_3_ = f32[24,128]{1,0:T(8,128)S(1)} collective-permute-done((f32[24,128]{1,0:T(8,128)S(1)}, f32[24,128]{1,0:T(8,128)S(1)}, u32[]{:S(2)}, u32[]{:S(2)}) %collective-permute-start.3) | collective-permute-done | bytes 12320 | tf_op jit(solution)/shard_map/ppermute | solution.py:457
  31.9 1.6 %shard_map.47 = (bf16[512,512]{1,0:T(8,128)(2,1)S(1)}, bf16[512,512]{1,0:T(8,128)(2,1)S(1)}, bf16[512,512]{1,0:T(8,128)(2,1)S(1)}, bf16[512,512]{1,0:T(8,128)(2,...) custom-call(f32[24,128]{1,0:T(8,128)S(1)} %pad_maximum_fusion.refs_0_, ...), custom_call_target="tpu_custom_call" | custom-call | flops 67108864 | bytes 13156352 | tf_op jit(solution)/shard_map/pallas_call | solution.py:33
  33.6 0.0 copy-start
  33.6 2.6 %shard_map.49 = (bf16[64,4096]{1,0:T(8,128)(2,1)S(1)}, bf16[32,4096]{1,0:T(8,128)(2,1)S(1)}, bf16[256,4096]{1,0:T(8,128)(2,1)S(1)}) custom-call(bf16[64,4096]{1,0:T(8,128)(2,1)S(1)} %collective-permute-done.4.refs_0_.rows_ref, bf16[512,512]{1,0:T(8,128)(2,1)S(1)} %get-tuple-element.23.refs_1_.refs_2_.refs_9_, ...), custom_call_target="tpu_custom_call" | custom-call | flops 536870912 | bytes 14417920 | tf_op jit(solution)/shard_map/pallas_call | solution.py:33
  36.2 0.7 %collective-permute-start.10 = (bf16[32,4096]{1,0:T(8,128)(2,1)S(1)}, bf16[32,4096]{1,0:T(8,128)(2,1)S(1)}, u32[]{:S(2)}, u32[]{:S(2)}) collective-permute-start(bf16[32,4096]{1,0:T(8,128)(2,1)S(1)} %get-tuple-element.37), channel_id=1, source_target_pairs={{4,8},{8,4},{5,9},{9,5},{6,10},{10,6},{7,11},{11,7},{20,24},{24,20... | collective-permute-start | bytes 786440 | tf_op jit(solution)/shard_map/ppermute | solution.py:470
  36.9 0.0 collective-permute-done.7.refs_7_
  36.9 1.3 %collective-permute-start.8 = (bf16[32,4096]{1,0:T(8,128)(2,1)S(1)}, bf16[32,4096]{1,0:T(8,128)(2,1)S(1)}, u32[]{:S(2)}, u32[]{:S(2)}) collective-permute-start(bf16[32,4096]{1,0:T(8,128)(2,1)S(1)} %collective-permute-done.7.refs_7_), channel_id=1, source_target_pairs={{4,0},{8,12},{5,1},{9,13},{6,2},{10,14},{7,3},{11,15},{20,16},{24,... | collective-permute-start | bytes 786440 | tf_op jit(solution)/shard_map/ppermute | solution.py:470
  38.2 0.0 copy-done
  38.2 1.7 %shard_map.48 = (bf16[64,4096]{1,0:T(8,128)(2,1)S(1)}, bf16[256,4096]{1,0:T(8,128)(2,1)S(1)}) custom-call(bf16[64,4096]{1,0:T(8,128)(2,1)S(1)} %bitcast.7, bf16[512,512]{1,0:T(8,128)(2,1)S(1)} %get-tuple-element.23.refs_1_.refs_2_.refs_9_, bf16[512,512]{1,0:T(8,128)(2,1)S(1)} %get-tuple-element.24.refs_2_.refs_3_.refs_10_, ...), custom_call_target="tpu_custom_call" | custom-call | flops 536870912 | bytes 14155776 | tf_op jit(solution)/shard_map/pallas_call | solution.py:33
  39.9 0.0 collective-permute-done.6.refs_1_
  39.9 1.7 %shard_map.50 = (bf16[64,4096]{1,0:T(8,128)(2,1)S(1)}, bf16[256,4096]{1,0:T(8,128)(2,1)S(1)}) custom-call(bf16[64,4096]{1,0:T(8,128)(2,1)S(1)} %collective-permute-done.5.refs_0_, bf16[64,4096]{1,0:T(8,128)(2,1)S(1)} %collective-permute-done.6.refs_1_, bf16[512,512]{1,0:T(8,128)(2,1)S(1)} %get-tuple-element.23.refs_1_.refs_2_.refs_9_, ...), custom_call_target="tpu_custom_call" | custom-call | flops 536870912 | bytes 14680064 | tf_op jit(solution)/shard_map/pallas_call | solution.py:33
  41.6 0.0 collective-permute-done.10.refs_0_
  41.7 1.3 %collective-permute-start.11 = (bf16[32,4096]{1,0:T(8,128)(2,1)S(1)}, bf16[32,4096]{1,0:T(8,128)(2,1)S(1)}, u32[]{:S(2)}, u32[]{:S(2)}) collective-permute-start(bf16[32,4096]{1,0:T(8,128)(2,1)S(1)} %collective-permute-done.10.refs_0_), channel_id=1, source_target_pairs={{4,0},{8,12},{5,1},{9,13},{6,2},{10,14},{7,3},{11,15},{20,16},{24,... | collective-permute-start | bytes 786440 | tf_op jit(solution)/shard_map/ppermute | solution.py:470
  43.0 3.4 %collective-permute-done.8.refs_8_ = bf16[32,4096]{1,0:T(8,128)(2,1)S(1)} collective-permute-done((bf16[32,4096]{1,0:T(8,128)(2,1)S(1)}, bf16[32,4096]{1,0:T(8,128)(2,1)S(1)}, u32[]{:S(2)}, u32[]{:S(2)}) %collective-permute-start.8) | collective-permute-done | bytes 262176 | tf_op jit(solution)/shard_map/ppermute | solution.py:470
  46.3 3.8 %shard_map.52 = (f32[224,1024]{1,0:T(8,128)S(1)}, bf16[96,1024]{1,0:T(8,128)(2,1)S(1)}) custom-call(bf16[64,4096]{1,0:T(8,128)(2,1)S(1)} %get-tuple-element.28.refs_0_, bf16[64,4096]{1,0:T(8,128)(2,1)S(1)} %get-tuple-element.29.refs_1_, bf16[64,4096]{1,0:T(8,128)(2,1)S(1)} %get-tuple-element.30.refs_2_, ...), custom_call_target="tpu_custom_call" | custom-call | flops 1879048192 | bytes 14221312 | tf_op jit(solution)/shard_map/pallas_call | solution.py:33
  50.2 1.6 %collective-permute-start.9 = (bf16[96,1024]{1,0:T(8,128)(2,1)S(1)}, bf16[96,1024]{1,0:T(8,128)(2,1)S(1)}, u32[]{:S(2)}, u32[]{:S(2)}) collective-permute-start(bf16[96,1024]{1,0:T(8,128)(2,1)S(1)} %get-tuple-element.36), channel_id=1, source_target_pairs={{0,2},{2,0},{1,3},{3,1},{4,6},{6,4},{5,7},{7,5},{8,10},{10,8},{9,1... | collective-permute-start | bytes 589832 | tf_op jit(solution)/shard_map/ppermute | solution.py:544
  51.7 0.0 collective-permute-done.11.refs_1_
  51.7 2.4 %shard_map.54 = (f32[32,1024]{1,0:T(8,128)S(1)}, bf16[32,1024]{1,0:T(8,128)(2,1)S(1)}) custom-call(bf16[32,4096]{1,0:T(8,128)(2,1)S(1)} %collective-permute-done.10.refs_0_, bf16[32,4096]{1,0:T(8,128)(2,1)S(1)} %collective-permute-done.11.refs_1_, bf16[256,4096]{1,0:T(8,128)(2,1)S(1)} %get-tuple-element.31.refs_3_.refs_2_, ...), custom_call_target="tpu_custom_call" | custom-call | flops 268435456 | bytes 10027008 | tf_op jit(solution)/shard_map/pallas_call | solution.py:33
  54.1 1.0 %collective-permute-start.12 = (bf16[32,1024]{1,0:T(8,128)(2,1)S(1)}, bf16[32,1024]{1,0:T(8,128)(2,1)S(1)}, u32[]{:S(2)}, u32[]{:S(2)}) collective-permute-start(bf16[32,1024]{1,0:T(8,128)(2,1)S(1)} %get-tuple-element.40), channel_id=1, source_target_pairs={{0,2},{2,0},{1,3},{3,1},{4,6},{6,4},{5,7},{7,5},{8,10},{10,8},{9,1... | collective-permute-start | bytes 196616 | tf_op jit(solution)/shard_map/ppermute | solution.py:544
  55.1 1.5 %collective-permute-done.9.refs_0_ = bf16[96,1024]{1,0:T(8,128)(2,1)S(1)} collective-permute-done((bf16[96,1024]{1,0:T(8,128)(2,1)S(1)}, bf16[96,1024]{1,0:T(8,128)(2,1)S(1)}, u32[]{:S(2)}, u32[]{:S(2)}) %collective-permute-start.9) | collective-permute-done | bytes 196640 | tf_op jit(solution)/shard_map/ppermute | solution.py:544
  56.6 0.8 %shard_map.53._ = f32[128,1024]{1,0:T(8,128)} custom-call(f32[224,1024]{1,0:T(8,128)S(1)} %get-tuple-element.35.early_ref.refs_6_, bf16[96,1024]{1,0:T(8,128)(2,1)S(1)} %collective-permute-done.9.refs_0_), custom_call_target="tpu_custom_call" | custom-call | flops 131072 | bytes 1638400 | tf_op jit(solution)/shard_map/pallas_call | solution.py:33
  57.4 1.0 %collective-permute-done.12.refs_0_ = bf16[32,1024]{1,0:T(8,128)(2,1)S(1)} collective-permute-done((bf16[32,1024]{1,0:T(8,128)(2,1)S(1)}, bf16[32,1024]{1,0:T(8,128)(2,1)S(1)}, u32[]{:S(2)}, u32[]{:S(2)}) %collective-permute-start.12) | collective-permute-done | bytes 65568 | tf_op jit(solution)/shard_map/ppermute | solution.py:544
  58.5 0.7 %shard_map.55 = f32[128,1024]{1,0:T(8,128)} custom-call(f32[128,1024]{1,0:T(8,128)} %shard_map.53._, f32[224,1024]{1,0:T(8,128)S(1)} %get-tuple-element.35.early_ref.refs_6_, f32[32,1024]{1,0:T(8,128)S(1)} %get-tuple-element.39.late_ref, bf16[32,1024]{1,0:T(8,128)(2,1)S(1)} %collective-permute-done.12.refs_0_), custom_call_target="tpu_custom_call", output_to_operand_aliasing={{}: (0, {})} | custom-call | tf_op jit(solution)/shard_map/pallas_call | solution.py:590
  (3 shorter events, 0.0 us)
Async XLA Ops:
  0.0 6.6 %collective-permute-start.5 = (bf16[64,4096]{1,0:T(8,128)(2,1)}, bf16[64,4096]{1,0:T(8,128)(2,1)S(1)}, u32[]{:S(2)}, u32[]{:S(2)}) collective-permute-start(bf16[64,4096]{1,0:T(8,128)(2,1)} %bitcast.5), channel_id=1, source_target_pairs={{4,8},{8,4},{5,9},{9,5},{6,10},{10,6},{7,11},{11,7},{20,24},{24,20... | collective-permute-start | bytes 1572872 | tf_op jit(solution)/shard_map/ppermute | solution.py:437
  0.7 17.8 %collective-permute-start.4 = (bf16[64,4096]{1,0:T(8,128)(2,1)}, bf16[64,4096]{1,0:T(8,128)(2,1)S(1)}, u32[]{:S(2)}, u32[]{:S(2)}) collective-permute-start(bf16[64,4096]{1,0:T(8,128)(2,1)} %bitcast.6), channel_id=1, source_target_pairs={{0,4},{4,0},{8,12},{12,8},{1,5},{5,1},{9,13},{13,9},{2,6},{6,2},{1... | collective-permute-start | bytes 1572872 | tf_op jit(solution)/shard_map/ppermute | solution.py:438
  6.6 33.3 %collective-permute-start.6 = (bf16[64,4096]{1,0:T(8,128)(2,1)S(1)}, bf16[64,4096]{1,0:T(8,128)(2,1)S(1)}, u32[]{:S(2)}, u32[]{:S(2)}) collective-permute-start(bf16[64,4096]{1,0:T(8,128)(2,1)S(1)} %collective-permute-done.5.refs_0_), channel_id=1, source_target_pairs={{4,0},{8,12},{5,1},{9,13},{6,2},{10,14},{7,3},{11,15},{20,16},{24,... | collective-permute-start | bytes 1572872 | tf_op jit(solution)/shard_map/ppermute | solution.py:458
  18.5 18.4 %collective-permute-start.7 = (bf16[32,4096]{1,0:T(8,128)(2,1)S(1)}, bf16[32,4096]{1,0:T(8,128)(2,1)S(1)}, u32[]{:S(2)}, u32[]{:S(2)}) collective-permute-start(bf16[32,4096]{1,0:T(8,128)(2,1)S(1)} %shard_map.51), channel_id=1, source_target_pairs={{4,8},{8,4},{5,9},{9,5},{6,10},{10,6},{7,11},{11,7},{20,24},{24,20... | collective-permute-start | bytes 786440 | tf_op jit(solution)/shard_map/ppermute | solution.py:470
  19.2 0.7 %copy-start.1 = (bf16[1,8,128]{2,1,0:T(8,128)(2,1)S(1)}, bf16[1,8,128]{2,1,0:T(8,128)(2,1)}, u32[]{:S(2)}) copy-start(bf16[1,8,128]{2,1,0:T(8,128)(2,1)} %param.6) | copy-start | bytes 6148
  19.8 0.7 %copy-start.2 = (f32[1,512]{1,0:T(1,128)S(1)}, f32[1,512]{1,0:T(1,128)}, u32[]{:S(2)}) copy-start(f32[1,512]{1,0:T(1,128)} %param.7) | copy-start | bytes 6148
  20.5 1.2 %collective-permute-start = (f32[12,128]{1,0:T(8,128)S(1)}, f32[12,128]{1,0:T(8,128)S(1)}, u32[]{:S(2)}, u32[]{:S(2)}) collective-permute-start(f32[12,128]{1,0:T(8,128)S(1)} %shard_map.46), channel_id=1, source_target_pairs={{0,1},{1,0},{2,3},{3,2},{4,5},{5,4},{6,7},{7,6},{8,9},{9,8},{10,11... | collective-permute-start | bytes 18440 | tf_op jit(solution)/shard_map/ppermute | solution.py:453
  21.7 7.4 %collective-permute-start.1 = (f32[24,128]{1,0:T(8,128)S(1)}, f32[24,128]{1,0:T(8,128)S(1)}, u32[]{:S(2)}, u32[]{:S(2)}) collective-permute-start(f32[24,128]{1,0:T(8,128)S(1)} %pad_maximum_fusion.refs_0_), channel_id=1, source_target_pairs={{0,4},{4,8},{8,12},{12,0},{1,5},{5,9},{9,13},{13,1},{2,6},{6,10},{... | collective-permute-start | bytes 36872 | tf_op jit(solution)/shard_map/ppermute | solution.py:457
  26.2 4.8 %collective-permute-start.2 = (f32[24,128]{1,0:T(8,128)S(1)}, f32[24,128]{1,0:T(8,128)S(1)}, u32[]{:S(2)}, u32[]{:S(2)}) collective-permute-start(f32[24,128]{1,0:T(8,128)S(1)} %pad_maximum_fusion.refs_0_), channel_id=1, source_target_pairs={{0,8},{4,12},{8,0},{12,4},{1,9},{5,13},{9,1},{13,5},{2,10},{6,14},... | collective-permute-start | bytes 36872 | tf_op jit(solution)/shard_map/ppermute | solution.py:457
  26.2 5.7 %collective-permute-start.3 = (f32[24,128]{1,0:T(8,128)S(1)}, f32[24,128]{1,0:T(8,128)S(1)}, u32[]{:S(2)}, u32[]{:S(2)}) collective-permute-start(f32[24,128]{1,0:T(8,128)S(1)} %pad_maximum_fusion.refs_0_), channel_id=1, source_target_pairs={{0,12},{4,0},{8,4},{12,8},{1,13},{5,1},{9,5},{13,9},{2,14},{6,2},{... | collective-permute-start | bytes 36872 | tf_op jit(solution)/shard_map/ppermute | solution.py:457
  33.6 4.6 %copy-start = (bf16[1,1,64,4096]{3,2,1,0:T(8,128)(2,1)S(1)}, bf16[1,1,64,4096]{3,2,1,0:T(8,128)(2,1)}, u32[]{:S(2)}) copy-start(bf16[1,1,64,4096]{3,2,1,0:T(8,128)(2,1)} %param.5) | copy-start | bytes 1572868
  36.2 5.5 %collective-permute-start.10 = (bf16[32,4096]{1,0:T(8,128)(2,1)S(1)}, bf16[32,4096]{1,0:T(8,128)(2,1)S(1)}, u32[]{:S(2)}, u32[]{:S(2)}) collective-permute-start(bf16[32,4096]{1,0:T(8,128)(2,1)S(1)} %get-tuple-element.37), channel_id=1, source_target_pairs={{4,8},{8,4},{5,9},{9,5},{6,10},{10,6},{7,11},{11,7},{20,24},{24,20... | collective-permute-start | bytes 786440 | tf_op jit(solution)/shard_map/ppermute | solution.py:470
  36.9 9.4 %collective-permute-start.8 = (bf16[32,4096]{1,0:T(8,128)(2,1)S(1)}, bf16[32,4096]{1,0:T(8,128)(2,1)S(1)}, u32[]{:S(2)}, u32[]{:S(2)}) collective-permute-start(bf16[32,4096]{1,0:T(8,128)(2,1)S(1)} %collective-permute-done.7.refs_7_), channel_id=1, source_target_pairs={{4,0},{8,12},{5,1},{9,13},{6,2},{10,14},{7,3},{11,15},{20,16},{24,... | collective-permute-start | bytes 786440 | tf_op jit(solution)/shard_map/ppermute | solution.py:470
  41.7 10.1 %collective-permute-start.11 = (bf16[32,4096]{1,0:T(8,128)(2,1)S(1)}, bf16[32,4096]{1,0:T(8,128)(2,1)S(1)}, u32[]{:S(2)}, u32[]{:S(2)}) collective-permute-start(bf16[32,4096]{1,0:T(8,128)(2,1)S(1)} %collective-permute-done.10.refs_0_), channel_id=1, source_target_pairs={{4,0},{8,12},{5,1},{9,13},{6,2},{10,14},{7,3},{11,15},{20,16},{24,... | collective-permute-start | bytes 786440 | tf_op jit(solution)/shard_map/ppermute | solution.py:470
  50.2 6.4 %collective-permute-start.9 = (bf16[96,1024]{1,0:T(8,128)(2,1)S(1)}, bf16[96,1024]{1,0:T(8,128)(2,1)S(1)}, u32[]{:S(2)}, u32[]{:S(2)}) collective-permute-start(bf16[96,1024]{1,0:T(8,128)(2,1)S(1)} %get-tuple-element.36), channel_id=1, source_target_pairs={{0,2},{2,0},{1,3},{3,1},{4,6},{6,4},{5,7},{7,5},{8,10},{10,8},{9,1... | collective-permute-start | bytes 589832 | tf_op jit(solution)/shard_map/ppermute | solution.py:544
  54.1 4.3 %collective-permute-start.12 = (bf16[32,1024]{1,0:T(8,128)(2,1)S(1)}, bf16[32,1024]{1,0:T(8,128)(2,1)S(1)}, u32[]{:S(2)}, u32[]{:S(2)}) collective-permute-start(bf16[32,1024]{1,0:T(8,128)(2,1)S(1)} %get-tuple-element.40), channel_id=1, source_target_pairs={{0,2},{2,0},{1,3},{3,1},{4,6},{6,4},{5,7},{7,5},{8,10},{10,8},{9,1... | collective-permute-start | bytes 196616 | tf_op jit(solution)/shard_map/ppermute | solution.py:544

commit v5 on v4

--- a/solution.py
+++ b/solution.py
@@ -184,7 +184,7 @@
     return call(head_kernel, shape, [IN_VMEM], [], (value,), flops=0, grant=4 << 20)
 
 
-def turn(inputs, choice, here_ref, constants, scratch, write):
+def turn(inputs, choice, here_ref, constants, scratch, write, beside=None):
     w1_ref, but_ref, bu_ref, w5_ref, inv_ref = constants
     tall, first, second = scratch
     size = but_ref.shape[0] // HALF
@@ -206,14 +206,15 @@
         which = lookup(choice, here_ref[0])
         for i in range(len(inputs)):
             pl.when(which == i)(functools.partial(gather_rows, inputs[i]))
+    if beside is not None:
+        beside()
     full = w1_ref.shape[0] // 2
     if half == full:
-        w1, w5, inverse = w1_ref[...], w5_ref[...], inv_ref[...]
+        w1, w5 = w1_ref[...], w5_ref[...]
     else:
         wide = fold * lanes
         w1 = jnp.concatenate([w1_ref[:wide, k * full : k * full + half] for k in range(2)], axis=1)
         w5 = jnp.concatenate([w5_ref[k * full : k * full + half, :wide] for k in range(2)], axis=0)
-        inverse = inv_ref[:, :half]
     chunk = 8
     parts = TILE // HALF
     for a0 in range(0, pairs, chunk):
@@ -225,9 +226,13 @@
                     at = (2 * a + odd) * HALF
                     first[part, at : at + HALF, :] = rows[low : low + HALF, odd * half : (odd + 1) * half]
     but, bu = but_ref[...], bu_ref[...]
-    for part in range(parts):
-        scaled = (dot(but, first[part].astype(BF16)) * inverse).astype(BF16)
-        second[part] = dot(bu, scaled)
+    joined = parts if parts * half <= full else 1
+    for low in range(0, parts, joined):
+        both = jnp.concatenate([first[low + k].astype(BF16) for k in range(joined)], axis=1)
+        scaled = (dot(but, both) * inv_ref[:, : joined * half]).astype(BF16)
+        back = dot(bu, scaled)
+        for k in range(joined):
+            second[low + k] = back[:, k * half : (k + 1) * half]
     for a in range(pairs):
         for odd in range(2):
             at = (2 * a + odd) * HALF
@@ -345,14 +350,14 @@
     constants = [refs.pop(0) for _ in range(5)]
     *scratch, held = refs[-4:]
     kept_ref, *sent = refs[:-4]
-    fill(held, units, choices, here_ref)
     base = held.shape[0] - piece
 
     def write(row, lane, value):
         rows, lanes = value.shape
         held[base + row : base + row + rows, lane : lane + lanes] = value
 
-    turn(inputs, raw_choice, here_ref, constants, scratch, write)
+    beside = functools.partial(fill, held, units, choices, here_ref)
+    turn(inputs, raw_choice, here_ref, constants, scratch, write, beside)
     products(held, x_refs, kept_ref)
     z, x = here_ref[0], here_ref[1]
     layers = len(sent) + 1

time: 59.5 us -> 59.1 us (level)
  transfers between devices with their start and end apart: 13 -> 13, of which waited for: 7 -> 7; matrix products, arithmetic and copies ran while one was open for 0% -> 0% of each run, Pallas kernels for 25% -> 24%
where the time goes in v5:
time: 59.1 us; the launch traced here: 58.8 us
  starting transfers between devices  22.1 us (37%)
  waiting for transfers between devices  20.2 us (34%)
  Pallas kernels  15 us (25%)
  local copies, waits for them, and re-layouts  1.36 us (2%)
    pallas_call x9, Pallas kernels, call(): pl.pallas_call(kernel, out_shape=out_shape, in_specs=in_specs, out_specs=...  14.4 us
    ppermute x1, waiting for transfers between devices, steps(): raw[1, 0] = lax.ppermute(own, 'blk', plan[1, 0])  10.6 us
    ppermute x3, starting transfers between devices, steps(): lax.ppermute(pair, 'blk', [(a, (a + d) % blocks) for a in range(blocks)])  7.36 us
    ppermute x1, starting transfers between devices, steps(): raw[1, 0] = lax.ppermute(own, 'blk', plan[1, 0])  5.91 us
    ppermute x4, starting transfers between devices, hop(): return lax.ppermute(value, 'blk', plan[step, parity])  3.94 us
    ppermute x4, waiting for transfers between devices, hop(): return lax.ppermute(value, 'blk', plan[step, parity])  3.39 us
    ppermute x2, starting transfers between devices, shifted(): lax.ppermute(s, 'layer', [(o, (o + d) % layers) for o in range(layers)])  2.88 us
    ppermute x3, waiting for transfers between devices, steps(): lax.ppermute(pair, 'blk', [(a, (a + d) % blocks) for a in range(blocks)])  2.86 us
  transfers between devices with their start and end apart: 13, of which 7 were waited for; matrix products, arithmetic and copies ran while one was open for 0% of the time, Pallas kernels for 24%

profile of v5, /device:TPU:0, one launch (start us, length us, event | category | flops | bytes accessed | tf_op | source)
XLA Modules:
  0.0 58.8 jit_solution(17429925473908194881)
XLA Ops:
  0.0 0.7 %collective-permute-start.5 = (bf16[64,4096]{1,0:T(8,128)(2,1)}, bf16[64,4096]{1,0:T(8,128)(2,1)S(1)}, u32[]{:S(2)}, u32[]{:S(2)}) collective-permute-start(bf16[64,4096]{1,0:T(8,128)(2,1)} %bitcast.5), channel_id=1, source_target_pairs={{4,8},{8,4},{5,9},{9,5},{6,10},{10,6},{7,11},{11,7},{20,24},{24,20... | collective-permute-start | bytes 1572872 | tf_op jit(solution)/shard_map/ppermute | solution.py:442
  0.7 5.9 %collective-permute-start.4 = (bf16[64,4096]{1,0:T(8,128)(2,1)}, bf16[64,4096]{1,0:T(8,128)(2,1)S(1)}, u32[]{:S(2)}, u32[]{:S(2)}) collective-permute-start(bf16[64,4096]{1,0:T(8,128)(2,1)} %bitcast.6), channel_id=1, source_target_pairs={{0,4},{4,0},{8,12},{12,8},{1,5},{5,1},{9,13},{13,9},{2,6},{6,2},{1... | collective-permute-start | bytes 1572872 | tf_op jit(solution)/shard_map/ppermute | solution.py:443
  6.6 0.0 collective-permute-done.5.refs_0_
  6.6 1.3 %collective-permute-start.6 = (bf16[64,4096]{1,0:T(8,128)(2,1)S(1)}, bf16[64,4096]{1,0:T(8,128)(2,1)S(1)}, u32[]{:S(2)}, u32[]{:S(2)}) collective-permute-start(bf16[64,4096]{1,0:T(8,128)(2,1)S(1)} %collective-permute-done.5.refs_0_), channel_id=1, source_target_pairs={{4,0},{8,12},{5,1},{9,13},{6,2},{10,14},{7,3},{11,15},{20,16},{24,... | collective-permute-start | bytes 1572872 | tf_op jit(solution)/shard_map/ppermute | solution.py:463
  7.9 10.6 %collective-permute-done.4.refs_0_.rows_ref = bf16[64,4096]{1,0:T(8,128)(2,1)S(1)} collective-permute-done((bf16[64,4096]{1,0:T(8,128)(2,1)}, bf16[64,4096]{1,0:T(8,128)(2,1)S(1)}, u32[]{:S(2)}, u32[]{:S(2)}) %collective-permute-start.4) | collective-permute-done | bytes 524320 | tf_op jit(solution)/shard_map/ppermute | solution.py:443
  18.5 0.7 %collective-permute-start.7 = (bf16[32,4096]{1,0:T(8,128)(2,1)S(1)}, bf16[32,4096]{1,0:T(8,128)(2,1)S(1)}, u32[]{:S(2)}, u32[]{:S(2)}) collective-permute-start(bf16[32,4096]{1,0:T(8,128)(2,1)S(1)} %shard_map.51), channel_id=1, source_target_pairs={{4,8},{8,4},{5,9},{9,5},{6,10},{10,6},{7,11},{11,7},{20,24},{24,20... | collective-permute-start | bytes 786440 | tf_op jit(solution)/shard_map/ppermute | solution.py:475
  19.2 0.0 copy-start.1
  19.2 0.7 %copy-done.1 = bf16[1,8,128]{2,1,0:T(8,128)(2,1)S(1)} copy-done((bf16[1,8,128]{2,1,0:T(8,128)(2,1)S(1)}, bf16[1,8,128]{2,1,0:T(8,128)(2,1)}, u32[]{:S(2)}) %copy-start.1) | copy-done | bytes 2072
  19.8 0.0 copy-start.2
  19.9 0.7 %copy-done.2 = f32[1,512]{1,0:T(1,128)S(1)} copy-done((f32[1,512]{1,0:T(1,128)S(1)}, f32[1,512]{1,0:T(1,128)}, u32[]{:S(2)}) %copy-start.2) | copy-done | bytes 2072
  20.5 0.0 collective-permute-start
  20.5 1.2 %collective-permute-done = f32[12,128]{1,0:T(8,128)S(1)} collective-permute-done((f32[12,128]{1,0:T(8,128)S(1)}, f32[12,128]{1,0:T(8,128)S(1)}, u32[]{:S(2)}, u32[]{:S(2)}) %collective-permute-start) | collective-permute-done | bytes 6176 | tf_op jit(solution)/shard_map/ppermute | solution.py:458
  21.7 4.5 %collective-permute-start.1 = (f32[24,128]{1,0:T(8,128)S(1)}, f32[24,128]{1,0:T(8,128)S(1)}, u32[]{:S(2)}, u32[]{:S(2)}) collective-permute-start(f32[24,128]{1,0:T(8,128)S(1)} %pad_maximum_fusion.refs_0_), channel_id=1, source_target_pairs={{0,4},{4,8},{8,12},{12,0},{1,5},{5,9},{9,13},{13,1},{2,6},{6,10},{... | collective-permute-start | bytes 36872 | tf_op jit(solution)/shard_map/ppermute | solution.py:462
  26.2 0.0 collective-permute-start.2
  26.2 2.9 %collective-permute-start.3 = (f32[24,128]{1,0:T(8,128)S(1)}, f32[24,128]{1,0:T(8,128)S(1)}, u32[]{:S(2)}, u32[]{:S(2)}) collective-permute-start(f32[24,128]{1,0:T(8,128)S(1)} %pad_maximum_fusion.refs_0_), channel_id=1, source_target_pairs={{0,12},{4,0},{8,4},{12,8},{1,13},{5,1},{9,5},{13,9},{2,14},{6,2},{... | collective-permute-start | bytes 36872 | tf_op jit(solution)/shard_map/ppermute | solution.py:462
  29.1 0.0 collective-permute-done.1.refs_1_
  29.1 1.9 %collective-permute-done.2.refs_2_ = f32[24,128]{1,0:T(8,128)S(1)} collective-permute-done((f32[24,128]{1,0:T(8,128)S(1)}, f32[24,128]{1,0:T(8,128)S(1)}, u32[]{:S(2)}, u32[]{:S(2)}) %collective-permute-start.2) | collective-permute-done | bytes 12320 | tf_op jit(solution)/shard_map/ppermute | solution.py:462
  31.0 1.0 %collective-permute-done.3.refs_3_ = f32[24,128]{1,0:T(8,128)S(1)} collective-permute-done((f32[24,128]{1,0:T(8,128)S(1)}, f32[24,128]{1,0:T(8,128)S(1)}, u32[]{:S(2)}, u32[]{:S(2)}) %collective-permute-start.3) | collective-permute-done | bytes 12320 | tf_op jit(solution)/shard_map/ppermute | solution.py:462
  31.9 1.6 %shard_map.47 = (bf16[512,512]{1,0:T(8,128)(2,1)S(1)}, bf16[512,512]{1,0:T(8,128)(2,1)S(1)}, bf16[512,512]{1,0:T(8,128)(2,1)S(1)}, bf16[512,512]{1,0:T(8,128)(2,...) custom-call(f32[24,128]{1,0:T(8,128)S(1)} %pad_maximum_fusion.refs_0_, ...), custom_call_target="tpu_custom_call" | custom-call | flops 67108864 | bytes 13156352 | tf_op jit(solution)/shard_map/pallas_call | solution.py:33
  33.6 0.0 copy-start
  33.6 2.6 %shard_map.49 = (bf16[64,4096]{1,0:T(8,128)(2,1)S(1)}, bf16[32,4096]{1,0:T(8,128)(2,1)S(1)}, bf16[256,4096]{1,0:T(8,128)(2,1)S(1)}) custom-call(bf16[64,4096]{1,0:T(8,128)(2,1)S(1)} %collective-permute-done.4.refs_0_.rows_ref, bf16[512,512]{1,0:T(8,128)(2,1)S(1)} %get-tuple-element.23.refs_1_.refs_2_.refs_9_, ...), custom_call_target="tpu_custom_call" | custom-call | flops 536870912 | bytes 14417920 | tf_op jit(solution)/shard_map/pallas_call | solution.py:33
  36.2 0.7 %collective-permute-start.10 = (bf16[32,4096]{1,0:T(8,128)(2,1)S(1)}, bf16[32,4096]{1,0:T(8,128)(2,1)S(1)}, u32[]{:S(2)}, u32[]{:S(2)}) collective-permute-start(bf16[32,4096]{1,0:T(8,128)(2,1)S(1)} %get-tuple-element.37), channel_id=1, source_target_pairs={{4,8},{8,4},{5,9},{9,5},{6,10},{10,6},{7,11},{11,7},{20,24},{24,20... | collective-permute-start | bytes 786440 | tf_op jit(solution)/shard_map/ppermute | solution.py:475
  36.9 0.0 collective-permute-done.7.refs_7_
  36.9 1.3 %collective-permute-start.8 = (bf16[32,4096]{1,0:T(8,128)(2,1)S(1)}, bf16[32,4096]{1,0:T(8,128)(2,1)S(1)}, u32[]{:S(2)}, u32[]{:S(2)}) collective-permute-start(bf16[32,4096]{1,0:T(8,128)(2,1)S(1)} %collective-permute-done.7.refs_7_), channel_id=1, source_target_pairs={{4,0},{8,12},{5,1},{9,13},{6,2},{10,14},{7,3},{11,15},{20,16},{24,... | collective-permute-start | bytes 786440 | tf_op jit(solution)/shard_map/ppermute | solution.py:475
  38.2 0.0 copy-done
  38.2 1.7 %shard_map.48 = (bf16[64,4096]{1,0:T(8,128)(2,1)S(1)}, bf16[256,4096]{1,0:T(8,128)(2,1)S(1)}) custom-call(bf16[64,4096]{1,0:T(8,128)(2,1)S(1)} %bitcast.7, bf16[512,512]{1,0:T(8,128)(2,1)S(1)} %get-tuple-element.23.refs_1_.refs_2_.refs_9_, bf16[512,512]{1,0:T(8,128)(2,1)S(1)} %get-tuple-element.24.refs_2_.refs_3_.refs_10_, ...), custom_call_target="tpu_custom_call" | custom-call | flops 536870912 | bytes 14155776 | tf_op jit(solution)/shard_map/pallas_call | solution.py:33
  39.9 0.0 collective-permute-done.6.refs_1_
  39.9 1.7 %shard_map.50 = (bf16[64,4096]{1,0:T(8,128)(2,1)S(1)}, bf16[256,4096]{1,0:T(8,128)(2,1)S(1)}) custom-call(bf16[64,4096]{1,0:T(8,128)(2,1)S(1)} %collective-permute-done.5.refs_0_, bf16[64,4096]{1,0:T(8,128)(2,1)S(1)} %collective-permute-done.6.refs_1_, bf16[512,512]{1,0:T(8,128)(2,1)S(1)} %get-tuple-element.23.refs_1_.refs_2_.refs_9_, ...), custom_call_target="tpu_custom_call" | custom-call | flops 536870912 | bytes 14680064 | tf_op jit(solution)/shard_map/pallas_call | solution.py:33
  41.6 0.0 collective-permute-done.10.refs_0_
  41.6 1.3 %collective-permute-start.11 = (bf16[32,4096]{1,0:T(8,128)(2,1)S(1)}, bf16[32,4096]{1,0:T(8,128)(2,1)S(1)}, u32[]{:S(2)}, u32[]{:S(2)}) collective-permute-start(bf16[32,4096]{1,0:T(8,128)(2,1)S(1)} %collective-permute-done.10.refs_0_), channel_id=1, source_target_pairs={{4,0},{8,12},{5,1},{9,13},{6,2},{10,14},{7,3},{11,15},{20,16},{24,... | collective-permute-start | bytes 786440 | tf_op jit(solution)/shard_map/ppermute | solution.py:475
  43.0 3.4 %collective-permute-done.8.refs_8_ = bf16[32,4096]{1,0:T(8,128)(2,1)S(1)} collective-permute-done((bf16[32,4096]{1,0:T(8,128)(2,1)S(1)}, bf16[32,4096]{1,0:T(8,128)(2,1)S(1)}, u32[]{:S(2)}, u32[]{:S(2)}) %collective-permute-start.8) | collective-permute-done | bytes 262176 | tf_op jit(solution)/shard_map/ppermute | solution.py:475
  46.3 3.5 %shard_map.52 = (f32[224,1024]{1,0:T(8,128)S(1)}, bf16[96,1024]{1,0:T(8,128)(2,1)S(1)}) custom-call(bf16[64,4096]{1,0:T(8,128)(2,1)S(1)} %get-tuple-element.28.refs_0_, bf16[64,4096]{1,0:T(8,128)(2,1)S(1)} %get-tuple-element.29.refs_1_, bf16[64,4096]{1,0:T(8,128)(2,1)S(1)} %get-tuple-element.30.refs_2_, ...), custom_call_target="tpu_custom_call" | custom-call | flops 1879048192 | bytes 14221312 | tf_op jit(solution)/shard_map/pallas_call | solution.py:33
  49.8 1.6 %collective-permute-start.9 = (bf16[96,1024]{1,0:T(8,128)(2,1)S(1)}, bf16[96,1024]{1,0:T(8,128)(2,1)S(1)}, u32[]{:S(2)}, u32[]{:S(2)}) collective-permute-start(bf16[96,1024]{1,0:T(8,128)(2,1)S(1)} %get-tuple-element.36), channel_id=1, source_target_pairs={{0,2},{2,0},{1,3},{3,1},{4,6},{6,4},{5,7},{7,5},{8,10},{10,8},{9,1... | collective-permute-start | bytes 589832 | tf_op jit(solution)/shard_map/ppermute | solution.py:549
  51.4 0.0 collective-permute-done.11.refs_1_
  51.4 2.4 %shard_map.54 = (f32[32,1024]{1,0:T(8,128)S(1)}, bf16[32,1024]{1,0:T(8,128)(2,1)S(1)}) custom-call(bf16[32,4096]{1,0:T(8,128)(2,1)S(1)} %collective-permute-done.10.refs_0_, bf16[32,4096]{1,0:T(8,128)(2,1)S(1)} %collective-permute-done.11.refs_1_, bf16[256,4096]{1,0:T(8,128)(2,1)S(1)} %get-tuple-element.31.refs_3_.refs_2_, ...), custom_call_target="tpu_custom_call" | custom-call | flops 268435456 | bytes 10027008 | tf_op jit(solution)/shard_map/pallas_call | solution.py:33
  53.8 1.3 %collective-permute-start.12 = (bf16[32,1024]{1,0:T(8,128)(2,1)S(1)}, bf16[32,1024]{1,0:T(8,128)(2,1)S(1)}, u32[]{:S(2)}, u32[]{:S(2)}) collective-permute-start(bf16[32,1024]{1,0:T(8,128)(2,1)S(1)} %get-tuple-element.40), channel_id=1, source_target_pairs={{0,2},{2,0},{1,3},{3,1},{4,6},{6,4},{5,7},{7,5},{8,10},{10,8},{9,1... | collective-permute-start | bytes 196616 | tf_op jit(solution)/shard_map/ppermute | solution.py:549
  55.1 1.2 %collective-permute-done.9.refs_0_ = bf16[96,1024]{1,0:T(8,128)(2,1)S(1)} collective-permute-done((bf16[96,1024]{1,0:T(8,128)(2,1)S(1)}, bf16[96,1024]{1,0:T(8,128)(2,1)S(1)}, u32[]{:S(2)}, u32[]{:S(2)}) %collective-permute-start.9) | collective-permute-done | bytes 196640 | tf_op jit(solution)/shard_map/ppermute | solution.py:549
  56.2 0.8 %shard_map.53._ = f32[128,1024]{1,0:T(8,128)} custom-call(f32[224,1024]{1,0:T(8,128)S(1)} %get-tuple-element.35.early_ref.refs_6_, bf16[96,1024]{1,0:T(8,128)(2,1)S(1)} %collective-permute-done.9.refs_0_), custom_call_target="tpu_custom_call" | custom-call | flops 131072 | bytes 1638400 | tf_op jit(solution)/shard_map/pallas_call | solution.py:33
  57.1 1.0 %collective-permute-done.12.refs_0_ = bf16[32,1024]{1,0:T(8,128)(2,1)S(1)} collective-permute-done((bf16[32,1024]{1,0:T(8,128)(2,1)S(1)}, bf16[32,1024]{1,0:T(8,128)(2,1)S(1)}, u32[]{:S(2)}, u32[]{:S(2)}) %collective-permute-start.12) | collective-permute-done | bytes 65568 | tf_op jit(solution)/shard_map/ppermute | solution.py:549
  58.1 0.7 %shard_map.55 = f32[128,1024]{1,0:T(8,128)} custom-call(f32[128,1024]{1,0:T(8,128)} %shard_map.53._, f32[224,1024]{1,0:T(8,128)S(1)} %get-tuple-element.35.early_ref.refs_6_, f32[32,1024]{1,0:T(8,128)S(1)} %get-tuple-element.39.late_ref, bf16[32,1024]{1,0:T(8,128)(2,1)S(1)} %collective-permute-done.12.refs_0_), custom_call_target="tpu_custom_call", output_to_operand_aliasing={{}: (0, {})} | custom-call | tf_op jit(solution)/shard_map/pallas_call | solution.py:595
  (3 shorter events, 0.0 us)
Async XLA Ops:
  0.0 6.6 %collective-permute-start.5 = (bf16[64,4096]{1,0:T(8,128)(2,1)}, bf16[64,4096]{1,0:T(8,128)(2,1)S(1)}, u32[]{:S(2)}, u32[]{:S(2)}) collective-permute-start(bf16[64,4096]{1,0:T(8,128)(2,1)} %bitcast.5), channel_id=1, source_target_pairs={{4,8},{8,4},{5,9},{9,5},{6,10},{10,6},{7,11},{11,7},{20,24},{24,20... | collective-permute-start | bytes 1572872 | tf_op jit(solution)/shard_map/ppermute | solution.py:442
  0.7 17.8 %collective-permute-start.4 = (bf16[64,4096]{1,0:T(8,128)(2,1)}, bf16[64,4096]{1,0:T(8,128)(2,1)S(1)}, u32[]{:S(2)}, u32[]{:S(2)}) collective-permute-start(bf16[64,4096]{1,0:T(8,128)(2,1)} %bitcast.6), channel_id=1, source_target_pairs={{0,4},{4,0},{8,12},{12,8},{1,5},{5,1},{9,13},{13,9},{2,6},{6,2},{1... | collective-permute-start | bytes 1572872 | tf_op jit(solution)/shard_map/ppermute | solution.py:443
  6.6 33.3 %collective-permute-start.6 = (bf16[64,4096]{1,0:T(8,128)(2,1)S(1)}, bf16[64,4096]{1,0:T(8,128)(2,1)S(1)}, u32[]{:S(2)}, u32[]{:S(2)}) collective-permute-start(bf16[64,4096]{1,0:T(8,128)(2,1)S(1)} %collective-permute-done.5.refs_0_), channel_id=1, source_target_pairs={{4,0},{8,12},{5,1},{9,13},{6,2},{10,14},{7,3},{11,15},{20,16},{24,... | collective-permute-start | bytes 1572872 | tf_op jit(solution)/shard_map/ppermute | solution.py:463
  18.5 18.4 %collective-permute-start.7 = (bf16[32,4096]{1,0:T(8,128)(2,1)S(1)}, bf16[32,4096]{1,0:T(8,128)(2,1)S(1)}, u32[]{:S(2)}, u32[]{:S(2)}) collective-permute-start(bf16[32,4096]{1,0:T(8,128)(2,1)S(1)} %shard_map.51), channel_id=1, source_target_pairs={{4,8},{8,4},{5,9},{9,5},{6,10},{10,6},{7,11},{11,7},{20,24},{24,20... | collective-permute-start | bytes 786440 | tf_op jit(solution)/shard_map/ppermute | solution.py:475
  19.2 0.7 %copy-start.1 = (bf16[1,8,128]{2,1,0:T(8,128)(2,1)S(1)}, bf16[1,8,128]{2,1,0:T(8,128)(2,1)}, u32[]{:S(2)}) copy-start(bf16[1,8,128]{2,1,0:T(8,128)(2,1)} %param.6) | copy-start | bytes 6148
  19.8 0.7 %copy-start.2 = (f32[1,512]{1,0:T(1,128)S(1)}, f32[1,512]{1,0:T(1,128)}, u32[]{:S(2)}) copy-start(f32[1,512]{1,0:T(1,128)} %param.7) | copy-start | bytes 6148
  20.5 1.2 %collective-permute-start = (f32[12,128]{1,0:T(8,128)S(1)}, f32[12,128]{1,0:T(8,128)S(1)}, u32[]{:S(2)}, u32[]{:S(2)}) collective-permute-start(f32[12,128]{1,0:T(8,128)S(1)} %shard_map.46), channel_id=1, source_target_pairs={{0,1},{1,0},{2,3},{3,2},{4,5},{5,4},{6,7},{7,6},{8,9},{9,8},{10,11... | collective-permute-start | bytes 18440 | tf_op jit(solution)/shard_map/ppermute | solution.py:458
  21.7 7.4 %collective-permute-start.1 = (f32[24,128]{1,0:T(8,128)S(1)}, f32[24,128]{1,0:T(8,128)S(1)}, u32[]{:S(2)}, u32[]{:S(2)}) collective-permute-start(f32[24,128]{1,0:T(8,128)S(1)} %pad_maximum_fusion.refs_0_), channel_id=1, source_target_pairs={{0,4},{4,8},{8,12},{12,0},{1,5},{5,9},{9,13},{13,1},{2,6},{6,10},{... | collective-permute-start | bytes 36872 | tf_op jit(solution)/shard_map/ppermute | solution.py:462
  26.2 4.8 %collective-permute-start.2 = (f32[24,128]{1,0:T(8,128)S(1)}, f32[24,128]{1,0:T(8,128)S(1)}, u32[]{:S(2)}, u32[]{:S(2)}) collective-permute-start(f32[24,128]{1,0:T(8,128)S(1)} %pad_maximum_fusion.refs_0_), channel_id=1, source_target_pairs={{0,8},{4,12},{8,0},{12,4},{1,9},{5,13},{9,1},{13,5},{2,10},{6,14},... | collective-permute-start | bytes 36872 | tf_op jit(solution)/shard_map/ppermute | solution.py:462
  26.2 5.7 %collective-permute-start.3 = (f32[24,128]{1,0:T(8,128)S(1)}, f32[24,128]{1,0:T(8,128)S(1)}, u32[]{:S(2)}, u32[]{:S(2)}) collective-permute-start(f32[24,128]{1,0:T(8,128)S(1)} %pad_maximum_fusion.refs_0_), channel_id=1, source_target_pairs={{0,12},{4,0},{8,4},{12,8},{1,13},{5,1},{9,5},{13,9},{2,14},{6,2},{... | collective-permute-start | bytes 36872 | tf_op jit(solution)/shard_map/ppermute | solution.py:462
  33.6 4.6 %copy-start = (bf16[1,1,64,4096]{3,2,1,0:T(8,128)(2,1)S(1)}, bf16[1,1,64,4096]{3,2,1,0:T(8,128)(2,1)}, u32[]{:S(2)}) copy-start(bf16[1,1,64,4096]{3,2,1,0:T(8,128)(2,1)} %param.5) | copy-start | bytes 1572868
  36.2 5.5 %collective-permute-start.10 = (bf16[32,4096]{1,0:T(8,128)(2,1)S(1)}, bf16[32,4096]{1,0:T(8,128)(2,1)S(1)}, u32[]{:S(2)}, u32[]{:S(2)}) collective-permute-start(bf16[32,4096]{1,0:T(8,128)(2,1)S(1)} %get-tuple-element.37), channel_id=1, source_target_pairs={{4,8},{8,4},{5,9},{9,5},{6,10},{10,6},{7,11},{11,7},{20,24},{24,20... | collective-permute-start | bytes 786440 | tf_op jit(solution)/shard_map/ppermute | solution.py:475
  36.9 9.4 %collective-permute-start.8 = (bf16[32,4096]{1,0:T(8,128)(2,1)S(1)}, bf16[32,4096]{1,0:T(8,128)(2,1)S(1)}, u32[]{:S(2)}, u32[]{:S(2)}) collective-permute-start(bf16[32,4096]{1,0:T(8,128)(2,1)S(1)} %collective-permute-done.7.refs_7_), channel_id=1, source_target_pairs={{4,0},{8,12},{5,1},{9,13},{6,2},{10,14},{7,3},{11,15},{20,16},{24,... | collective-permute-start | bytes 786440 | tf_op jit(solution)/shard_map/ppermute | solution.py:475
  41.6 9.7 %collective-permute-start.11 = (bf16[32,4096]{1,0:T(8,128)(2,1)S(1)}, bf16[32,4096]{1,0:T(8,128)(2,1)S(1)}, u32[]{:S(2)}, u32[]{:S(2)}) collective-permute-start(bf16[32,4096]{1,0:T(8,128)(2,1)S(1)} %collective-permute-done.10.refs_0_), channel_id=1, source_target_pairs={{4,0},{8,12},{5,1},{9,13},{6,2},{10,14},{7,3},{11,15},{20,16},{24,... | collective-permute-start | bytes 786440 | tf_op jit(solution)/shard_map/ppermute | solution.py:475
  49.8 6.4 %collective-permute-start.9 = (bf16[96,1024]{1,0:T(8,128)(2,1)S(1)}, bf16[96,1024]{1,0:T(8,128)(2,1)S(1)}, u32[]{:S(2)}, u32[]{:S(2)}) collective-permute-start(bf16[96,1024]{1,0:T(8,128)(2,1)S(1)} %get-tuple-element.36), channel_id=1, source_target_pairs={{0,2},{2,0},{1,3},{3,1},{4,6},{6,4},{5,7},{7,5},{8,10},{10,8},{9,1... | collective-permute-start | bytes 589832 | tf_op jit(solution)/shard_map/ppermute | solution.py:549
  53.8 4.3 %collective-permute-start.12 = (bf16[32,1024]{1,0:T(8,128)(2,1)S(1)}, bf16[32,1024]{1,0:T(8,128)(2,1)S(1)}, u32[]{:S(2)}, u32[]{:S(2)}) collective-permute-start(bf16[32,1024]{1,0:T(8,128)(2,1)S(1)} %get-tuple-element.40), channel_id=1, source_target_pairs={{0,2},{2,0},{1,3},{3,1},{4,6},{6,4},{5,7},{7,5},{8,10},{10,8},{9,1... | collective-permute-start | bytes 196616 | tf_op jit(solution)/shard_map/ppermute | solution.py:549
